TPU v7x, 32 devices: a whole 2x2x4 slice. The times are simulated.
32 devices in a mesh: ulysses: 4 (over x, core), blk: 8 (over z, y).
Axes of the slice: x: 2, y: 2, z: 4, core: 2. Of those that a mesh axis runs over, the one named last changes fastest.
Arguments:
- inputs: bfloat16 [8, 512, 1024], P('blk', 'ulysses'), may hold values from -6 to 6
- cotangent: bfloat16 [8, 512, 1024], P('blk', 'ulysses'), may hold values from -6 to 6
- segment_ids: int32 [8, 512], replicated, may hold values from 0 to 30, as said below
- bucket_table: int32 [257], replicated, may hold values from 0 to 31, as said below
- gain_attention: float32 [1024], replicated, may hold values from 0.5 to 1.5
- query_weight: bfloat16 [1024, 1024], P(('ulysses', 'blk')), may hold values from -0.046875 to 0.046875
- key_weight: bfloat16 [1024, 1024], P(('ulysses', 'blk')), may hold values from -0.1875 to 0.1875
- value_weight: bfloat16 [1024, 1024], P(('ulysses', 'blk')), may hold values from -0.1875 to 0.1875
- output_weight: bfloat16 [1024, 1024], P(('ulysses', 'blk')), may hold values from -0.75 to 0.75
- bucket_bias: float32 [32, 16], replicated, may hold values from -3 to 3
- gain_feedforward: float32 [1024], replicated, may hold values from 0.5 to 1.5
- gate_weight: bfloat16 [2816, 1024], P(('ulysses', 'blk')), may hold values from -0.1875 to 0.1875
- up_weight: bfloat16 [2816, 1024], P(('ulysses', 'blk')), may hold values from -0.1875 to 0.1875
- down_weight: bfloat16 [2816, 1024], P(('ulysses', 'blk')), may hold values from -0.109375 to 0.109375
Outputs:
- layer_out: bfloat16 [8, 512, 1024], P('blk', 'ulysses')
- grad_inputs: bfloat16 [8, 512, 1024], P('blk', 'ulysses')
- grad_gain_attention: float32 [1024], replicated
- grad_query_weight: float32 [1024, 1024], P(('ulysses', 'blk'))
- grad_key_weight: float32 [1024, 1024], P(('ulysses', 'blk'))
- grad_value_weight: float32 [1024, 1024], P(('ulysses', 'blk'))
- grad_output_weight: float32 [1024, 1024], P(('ulysses', 'blk'))
- grad_bucket_bias: float32 [32, 16], replicated
- grad_gain_feedforward: float32 [1024], replicated
- grad_gate_weight: float32 [2816, 1024], P(('ulysses', 'blk'))
- grad_up_weight: float32 [2816, 1024], P(('ulysses', 'blk'))
- grad_down_weight: float32 [2816, 1024], P(('ulysses', 'blk'))
Inputs may be any that keep to these rules, and one draw needn't show every extreme that they name: bucket_table[128 + o] is the bucket of a key o positions after its query, for o from -128 to 128 (farther keys take the end entries): 0 at o = 0, 1 to 15 for keys before the query, 16 to 31 for keys after it, never falling as |o| grows, 15 and 31 at the two ends. `segment_ids`: never falling along the sequence. Positions 256 * w to 256 * w + 255 form window w; window 0 is block 0, every later window w holds exactly the two non-empty blocks 2 w - 1 and 2 w.
All inputs are finite; a program needn't handle non-finite values.
Results may differ from a plain program's by a relative error of at most 0.025.
Values may be sent and summed in bfloat16 or wider, within the bound.
No kernel may reach another device: no remote copies, remote signals or barrier semaphores. Data moves between devices by JAX's collectives and lax.ppermute only.
A program may use at most 192 MiB of HBM per device.

v0:
```python
import functools

import jax
import jax.numpy as jnp
from jax import lax
from jax.experimental import pallas as pl
from jax.experimental.pallas import tpu as pltpu
from jax.sharding import Mesh
from jax.sharding import PartitionSpec as P

EPSILON = 1e-06
NEGATIVE = -1e30
HIGHEST = lax.Precision.HIGHEST
F32 = jnp.float32
BF16 = jnp.bfloat16
VMEM_LIMIT = 60 * 1024 * 1024
SQUARE = ("x", "y")
UNITS_GROUP = ("z", "c", "r")
EVERY = ("x", "c", "z", "y", "r")


def norm_scale(values):
    return lax.rsqrt(jnp.mean(values * values, axis=-1, keepdims=True) + EPSILON)


def norm_back(values, scaling, gain_vec, upstream):
    inner_sum = jnp.mean(values * gain_vec * upstream, axis=-1, keepdims=True)
    return scaling * gain_vec * upstream - values * scaling * scaling * scaling * inner_sum


def nt(left, right):
    return lax.dot_general(left, right, (((1,), (1,)), ((), ())), preferred_element_type=F32)


def nn(left, right):
    return lax.dot_general(left, right, (((1,), (0,)), ((), ())), preferred_element_type=F32)


def tn(left, right):
    return lax.dot_general(left, right, (((0,), (0,)), ((), ())), preferred_element_type=F32)


def swap(value, axis, mask):
    size = lax.axis_size(axis)
    return lax.ppermute(value, axis, [(at, at ^ mask) for at in range(size)])


def from_group(value, axis):
    return [value] + [swap(value, axis, mask) for mask in (1, 2, 3)]


def to_group(values, axis):
    return [values[0]] + [swap(values[mask], axis, mask) for mask in (1, 2, 3)]


def sum_everywhere(value, axis):
    first, second, third, fourth = from_group(value, axis)
    return (first + second) + (third + fourth)


def sum_over_z(rows, values):
    width = rows.shape[-1]
    lines = -(-values.size // width)
    padded = jnp.pad(values, (0, lines * width - values.size)).reshape(lines, width)
    high = lax.reduce_precision(padded, 8, 7)
    extra = jnp.concatenate([high, padded - high]).astype(BF16)
    extra = jnp.pad(extra, ((0, -2 * lines % 8), (0, 0)))
    arrived = to_group([jnp.concatenate([rows[at], extra]) for at in range(4)], "z")
    arrived = [part.astype(F32) for part in arrived]
    count = rows.shape[1]
    tails = [part[count : count + lines] + part[count + lines : count + 2 * lines] for part in arrived]
    total = (tails[0] + tails[1]) + (tails[2] + tails[3])
    return sum(part[:count] for part in arrived), total.ravel()[: values.size]


def kernel_call(body, out_shapes, inputs, scratch=(), scalars=1, micros=4):
    in_specs = [pl.BlockSpec(memory_space=pltpu.SMEM)] * scalars
    in_specs += [pl.BlockSpec(memory_space=pltpu.VMEM)] * (len(inputs) - scalars)
    return pl.pallas_call(
        body,
        out_shape=out_shapes,
        in_specs=in_specs,
        out_specs=jax.tree.map(lambda _: pl.BlockSpec(memory_space=pltpu.VMEM), out_shapes),
        scratch_shapes=list(scratch),
        compiler_params=pltpu.CompilerParams(vmem_limit_bytes=VMEM_LIMIT),
        cost_estimate=pl.CostEstimate(
            flops=int(micros * 1.15e9), bytes_accessed=1 << 20, transcendentals=0
        ),
    )(*inputs)


def shape(dims, dtype):
    return jax.ShapeDtypeStruct(dims, dtype)


def qkv_body(hd, coords, *refs):
    blocks, parts, other_rows, pieces = refs[:4], refs[4:8], refs[8], refs[9:13]
    rows_all, weights = refs[13:15]
    c_at, y_at = coords[1], coords[3]
    tokens, width = blocks[0].shape
    half = hd // 2
    for at in range(4):
        rows_all[at * tokens : (at + 1) * tokens, :] = blocks[at][...]
    for core in range(2):
        for dest in range(4):
            column = y_at ^ c_at ^ core
            place = (dest >> 1) * 2 + column
            shift = pl.multiple_of((y_at ^ (dest & 1)) * half, half)
            source = other_rows.at[dest * half : (dest + 1) * half] if core else parts[dest]
            for kind, first, step in ((0, 8 * hd, hd), (1, 0, 2 * hd), (2, hd, 2 * hd)):
                start = pl.multiple_of(first + place * step + shift, half)
                weights[pl.ds(start, half), :] = source[:, kind * width : (kind + 1) * width]
    normed = rows_all[...]
    pairs = nt(normed, weights[0 : 8 * hd, :]).astype(BF16)
    queries = nt(weights[8 * hd : 12 * hd, :], normed).astype(BF16)
    for dest in range(4):
        pieces[dest][0 : 4 * tokens, :] = pairs[:, dest * 2 * hd : (dest + 1) * 2 * hd]
        for at in range(4):
            pieces[dest][4 * tokens + at * hd : 4 * tokens + (at + 1) * hd, :] = queries[
                dest * hd : (dest + 1) * hd, at * tokens : (at + 1) * tokens
            ]


def bias_tiles(hvec, tokens):
    tiles = {}
    for at, diff in enumerate((-1, 0, 1)):
        spread = jnp.broadcast_to(hvec[at : at + 1, :], (tokens, 2 * tokens))
        tiles[diff] = pltpu.roll(spread, 0, 1, stride=1, stride_axis=0)[:, :tokens]
    return tiles


def fill_bias(hvec_ref, bias, cuts, repeat, c_at, r_at, tokens):
    tiles = bias_tiles(hvec_ref[...], tokens)
    zero = jnp.zeros((tokens, tokens), F32)
    bias[0] = jnp.zeros(bias.shape[1:], F32)
    for rows in range(8):
        for half in range(2):
            diff = rows - 4 - 2 * half
            even, odd = tiles.get(diff, zero), tiles.get(diff - 1, zero)
            row = (rows % 4) * tokens
            bias[1 + rows // 4, row : row + tokens, half * tokens : (half + 1) * tokens] = (
                jnp.where(c_at == 0, even, odd)
            )

    def mask(back, carry):
        place = bias.shape[0] - 3 - back
        allowed = allowed_mask(cuts, place * repeat + r_at, c_at, tokens)
        bias[2 + place] = jnp.where(allowed, bias[2], NEGATIVE)
        return carry

    lax.fori_loop(0, bias.shape[0] - 2, mask, 0)


def bias_slab(bias, place, run, at):
    return bias[jnp.where(at == run, 2 + place, jnp.where(at == run - 1, 1, 0))]


def allowed_mask(cuts, run, c_at, tokens):
    rows, cols = 4 * tokens, 2 * tokens
    key_at = lax.broadcasted_iota(jnp.int32, (rows, cols), 0)
    query_at = lax.broadcasted_iota(jnp.int32, (rows, cols), 1)
    key_window = key_at >= 2 * tokens
    query_window = query_at >= tokens
    key_in = jnp.where(key_window, key_at - 2 * tokens, key_at)
    query_in = jnp.where(query_window, query_at - tokens, query_at) + c_at * tokens
    cut = jnp.where(query_window, cuts[2 * run + 1], cuts[2 * run])
    inside = (key_in < cut) | (query_in >= cut)
    before = jnp.logical_and(jnp.logical_not(key_window), query_window)
    same = key_window == query_window
    return before | (same & inside)


def each_slot(run_low, run_high, repeat, step):
    def one(slot, carry):
        high = (slot > run_low).astype(jnp.int32)
        at = jnp.where(slot > run_low, slot - run_low - 1, slot)
        step(slot, high, at)
        return carry

    count = run_low + run_high + 2
    if repeat == 1:
        for slot in range(9):
            one(jnp.int32(slot), 0)
    else:
        lax.fori_loop(0, count, one, 0)


def chunk(at, block):
    return pl.ds(pl.multiple_of(at * block, block), block)


def fold_rows(values, how):
    rows, cols = values.shape
    return how(values.reshape(rows // 8, 8, cols), axis=0)


def attend_body(tokens, hd, repeat, coords, cuts, hvec, *refs):
    pieces, own, other = refs[:4], refs[4:8], refs[8:12]
    if repeat == 1:
        pieces = refs[:4]
        own, other, refs = refs[:4], refs[4:8], refs[8:]
    else:
        refs = refs[12:]
    out, lse, attended, keys, keys_t, queries, scores, bias, padded, peaks, totals, mixes = refs
    x_at, c_at, z_at, y_at, r_at = (coords[at] for at in range(5))
    block = 4 * tokens
    for dest in range(4):
        x_from, y_from = x_at ^ (dest >> 1), y_at ^ (dest & 1)
        for at in range(4):
            place = (z_at ^ at) * 2 + y_from
            for rep in range(repeat):
                run = place * repeat + rep
                base = run * block + x_from * 2 * tokens
                source = slice(rep * block + at * tokens, rep * block + (at + 1) * tokens)
                keys[pl.ds(pl.multiple_of(base + c_at * tokens, tokens), tokens), :] = own[dest][
                    source, :
                ]
                keys[pl.ds(pl.multiple_of(base + (1 - c_at) * tokens, tokens), tokens), :] = other[
                    dest
                ][source, :]
            start = block + at * hd
            queries[place, :, pl.ds(pl.multiple_of(x_from * tokens, tokens), tokens)] = pieces[
                dest
            ][start : start + hd, :]
    fill_bias(hvec, bias, cuts, repeat, c_at, r_at, tokens)

    def turn(at, carry):
        keys_t[at] = keys[chunk(at, block), :].T
        return carry

    lax.fori_loop(0, keys.shape[0] // block, turn, 0)
    places = queries.shape[0]
    padded[:, 0:hd, :] = queries[...]
    padded[:, hd:, :] = jnp.zeros_like(padded[:, hd:, :])

    def pair(low, carry):
        place_of = (low, places - 1 - low)
        run_of = tuple(place * repeat + r_at for place in place_of)
        peaks[...] = jnp.full_like(peaks, NEGATIVE)
        totals[...] = jnp.zeros_like(totals)
        mixes[...] = jnp.zeros_like(mixes)

        def score(slot, high, at):
            place = jnp.where(high == 1, place_of[1], place_of[0])
            run = place * repeat + r_at
            values = nn(keys[chunk(at, block), :], padded[place])
            values = values + bias_slab(bias, place, run, at)
            scores[slot] = values
            peaks[high] = jnp.maximum(peaks[high], fold_rows(values, jnp.max))

        each_slot(*run_of, repeat, score)
        for high in range(2):
            top = jnp.max(peaks[high], axis=0, keepdims=True)
            peaks[high] = jnp.broadcast_to(top, peaks.shape[1:])

        def mix(slot, high, at):
            weights = jnp.exp(scores[slot] - peaks[high][0:1, :])
            totals[high] += fold_rows(weights, jnp.sum)
            mixes[high] += nn(keys_t[at, hd:, :], weights.astype(BF16))

        each_slot(*run_of, repeat, mix)
        for high, place in enumerate(place_of):
            total = jnp.sum(totals[high], axis=0, keepdims=True)
            mixed = mixes[high] / total
            attended[place] = mixed
            lse[place] = peaks[high] + jnp.log(jnp.broadcast_to(total, peaks.shape[1:]))
            part = mixed.astype(BF16)
            for half in range(2):
                out[half * 8 + (place & 1) * 4 + (place >> 1)] = part[
                    :, half * tokens : (half + 1) * tokens
                ]
        return carry

    lax.fori_loop(0, places // 2, pair, 0)


def attend_back_body(tokens, hd, repeat, coords, cuts, hvec, *refs):
    arrived, queries, keys, keys_t, attended, lse = refs[:6]
    grad_own, grad_other, grad_q, table_out, far_out = refs[6:11]
    bias, grad_keys, table_acc, left, right, shifts, grad_queries = refs[11:]
    x_at, c_at, z_at, y_at, r_at = (coords[at] for at in range(5))
    block = 4 * tokens
    places = queries.shape[0]
    fill_bias(hvec, bias, cuts, repeat, c_at, r_at, tokens)
    grad_keys[...] = jnp.zeros_like(grad_keys)
    table_acc[...] = jnp.zeros_like(table_acc)

    def prepare(place, carry):
        query_t = queries[place]
        upstream_t = jnp.concatenate(
            [arrived[half * 8 + (place & 1) * 4 + (place >> 1)] for half in range(2)], axis=1
        )
        zero = jnp.zeros_like(query_t)
        query_pad = jnp.concatenate([query_t, zero], axis=0)
        upstream_pad = jnp.concatenate([zero, upstream_t], axis=0)
        left[place, :, 0 : 2 * tokens] = query_pad
        left[place, :, 2 * tokens :] = upstream_pad
        right[place, 0 : 2 * tokens, :] = query_pad.T
        right[place, 2 * tokens :, :] = upstream_pad.T
        shifts[place, 0:8, :] = lse[place]
        delta = jnp.sum(upstream_t.astype(F32) * attended[place], axis=0, keepdims=True)
        shifts[place, 8:16, :] = jnp.broadcast_to(delta, (8, 2 * tokens))
        return carry

    lax.fori_loop(0, places, prepare, 0)

    def pair(low, carry):
        place_of = (low, places - 1 - low)
        run_of = tuple(place * repeat + r_at for place in place_of)
        grad_queries[...] = jnp.zeros_like(grad_queries)

        def step(slot, high, at):
            place = jnp.where(high == 1, place_of[1], place_of[0])
            run = place * repeat + r_at
            rows = chunk(at, block)
            both = nn(keys[rows, :], left[place])
            values = both[:, 0 : 2 * tokens] + bias_slab(bias, place, run, at)
            probs = jnp.exp(values - shifts[place, 0:1, :])
            grad_scores = probs * (both[:, 2 * tokens :] - shifts[place, 8:9, :])
            grad_low = grad_scores.astype(BF16)
            grad_keys[rows, :] += nn(
                jnp.concatenate([grad_low, probs.astype(BF16)], axis=1), right[place]
            )
            grad_queries[high] += nn(keys_t[at, :hd, :], grad_low)
            kind = jnp.where(at == run, 2, jnp.where(at == run - 1, 1, 0))
            table_acc[kind] += grad_low.astype(F32)

        each_slot(*run_of, repeat, step)
        for high, place in enumerate(place_of):
            low_part = grad_queries[high].astype(BF16)
            for half in range(2):
                part = low_part[:, half * tokens : (half + 1) * tokens]
                dest = (x_at ^ half) * 2 + ((place & 1) ^ y_at)
                grad_q[dest * 4 + ((place >> 1) ^ z_at)] = part
        return carry

    lax.fori_loop(0, places // 2, pair, 0)

    for dest in range(4):
        x_from, y_from = x_at ^ (dest >> 1), y_at ^ (dest & 1)
        for at in range(4):
            place = (z_at ^ at) * 2 + y_from
            for rep in range(repeat):
                base = (place * repeat + rep) * block + x_from * 2 * tokens
                start = (dest * repeat + rep) * block + at * tokens
                target = slice(start, start + tokens)
                grad_own[target, :] = grad_keys[
                    pl.ds(pl.multiple_of(base + c_at * tokens, tokens), tokens), :
                ]
                grad_other[target, :] = grad_keys[
                    pl.ds(pl.multiple_of(base + (1 - c_at) * tokens, tokens), tokens), :
                ].astype(BF16)

    def tile_at(rows, half):
        row = (rows % 4) * tokens
        return table_acc[
            1 + rows // 4, row : row + tokens, half * tokens : (half + 1) * tokens
        ]

    spots = [(rows, half) for rows in range(8) for half in range(2)]
    flip = (
        lax.broadcasted_iota(jnp.int32, (tokens, tokens), 0)
        + lax.broadcasted_iota(jnp.int32, (tokens, tokens), 1)
        == tokens - 1
    ).astype(F32)
    far_even = jnp.zeros((tokens, tokens), F32)
    far_odd = jnp.zeros((tokens, tokens), F32)
    for rows, half in spots:
        diff = rows - 4 - 2 * half
        if diff <= -2:
            far_even += tile_at(rows, half)
        if diff - 1 <= -2:
            far_odd += tile_at(rows, half)
    extra = fold_rows(jnp.where(c_at == 0, far_even, far_odd), jnp.sum)
    far_out[...] = fold_rows(table_acc[0], jnp.sum)
    far_out[:, :tokens] += extra
    table_out[...] = jnp.zeros_like(table_out)
    for index, diff in enumerate((-1, 0, 1)):
        even = sum(tile_at(rows, half) for rows, half in spots if rows - 4 - 2 * half == diff)
        odd = sum(tile_at(rows, half) for rows, half in spots if rows - 5 - 2 * half == diff)
        tile = jnp.where(c_at == 0, even, odd)
        turned = jnp.dot(flip, tile, precision=HIGHEST, preferred_element_type=F32)
        wide = jnp.concatenate([turned, jnp.zeros_like(turned)], axis=1)
        wide = pltpu.roll(wide, tokens + 1, 1, stride=1, stride_axis=0)
        table_out[index : index + 1, :] = jnp.sum(wide, axis=0, keepdims=True)


def project_back_body(hd, coords, *refs):
    pieces, (rows_all, weights, gain), out = refs[:4], refs[4:7], refs[7]
    gain_out, pairs_t, queries_t, pairs, queries = refs[8:]
    tokens, width = out.shape[1:]
    z_at = coords[2]
    for dest in range(4):
        lanes = slice(dest * 2 * hd, (dest + 1) * 2 * hd)
        part = pieces[dest][0 : 4 * tokens, :]
        pairs[:, lanes] = part
        pairs_t[lanes, :] = part.T
        for at in range(4):
            queries_t[dest * hd : (dest + 1) * hd, at * tokens : (at + 1) * tokens] = pieces[dest][
                4 * tokens + at * hd : 4 * tokens + (at + 1) * hd, :
            ]
    queries[...] = queries_t[...].T
    grad = nn(pairs[...], weights[0 : 8 * hd, :]) + nn(queries[...], weights[8 * hd :, :])
    unit = rows_all[...].astype(F32) / gain[...]
    gain_out[...] = fold_rows(grad * unit, jnp.sum)
    for at in range(4):
        out[z_at ^ at] = grad[at * tokens : (at + 1) * tokens, :].astype(BF16)


def head_grads_body(hd, coords, pairs_t, queries_t, rows_all, keep, send):
    c_at, y_at = coords[1], coords[3]
    width = rows_all.shape[1]
    half = hd // 2
    normed = rows_all[...]
    pair_rows = nn(pairs_t[...], normed).astype(BF16)
    query_rows = nn(queries_t[...], normed).astype(BF16)
    for dest in range(4):
        other = (y_at ^ (dest & 1)) ^ c_at

        def put(target, dest=dest):
            for part in range(2):
                place = (dest >> 1) * 2 + (y_at ^ part)
                for kind, rows, first in (
                    (0, query_rows, dest * hd),
                    (1, pair_rows, dest * 2 * hd),
                    (2, pair_rows, dest * 2 * hd + hd),
                ):
                    first += part * half
                    target[place, :, kind * width : (kind + 1) * width] = rows[
                        first : first + half, :
                    ]

        pl.when(other == 0)(functools.partial(put, keep))
        pl.when(other == 1)(functools.partial(put, send))


def output_body(hd, coords, *refs):
    arrived, own_in, gain, parts, middle_out, normed_out, weights, features = refs
    x_at, c_at, z_at, y_at = coords[0], coords[1], coords[2], coords[3]
    half, tokens = hd // 2, arrived.shape[1]
    for z_of in range(4):
        for c_of in range(2):
            for dest in range(4):
                head = ((x_at ^ (dest >> 1)) * 2 + c_of) * 4 + z_of
                start = pl.multiple_of(head * hd + (y_at ^ (dest & 1)) * half, half)
                weights[pl.ds(start, half), :] = parts[
                    z_of * 2 + c_of, dest * half : (dest + 1) * half, :
                ]
    for dest in range(4):
        for core in range(2):
            for near in range(4):
                head = ((x_at ^ (dest >> 1)) * 2 + (c_at ^ core)) * 4 + (z_at ^ near)
                start = pl.multiple_of(head * hd + (y_at ^ (dest & 1)) * half, half)
                lanes = slice((core * 4 + near) * tokens, (core * 4 + near + 1) * tokens)
                features[dest, :, lanes] = arrived[pl.ds(start, half), :]
    middle = own_in[...].astype(F32) + nn(arrived[...].T, weights[...])
    middle_out[...] = middle
    normed_out[...] = (middle * norm_scale(middle) * gain[...]).astype(BF16)


def finish_body(*refs):
    parts, own_in, grad_middle, gain, out = refs
    values = own_in[...].astype(F32)
    grad = sum(parts[at].astype(F32) for at in range(4))
    out[...] = (
        grad_middle[...] + norm_back(values, norm_scale(values), gain[...], grad)
    ).astype(BF16)


def gated(gate_act, up_act):
    return jax.nn.gelu(gate_act, approximate=True) * up_act


def body(
    inputs,
    cotangent,
    segment_ids,
    bucket_table,
    gain_attention,
    query_weight,
    key_weight,
    value_weight,
    output_weight,
    bucket_bias,
    gain_feedforward,
    gate_weight,
    up_weight,
    down_weight,
):
    tokens, width = inputs.shape[1:]
    repeat = lax.axis_size("r")
    x_at, c_at, z_at, y_at, r_at = (lax.axis_index(name) for name in EVERY)
    coords = jnp.stack([x_at, c_at, z_at, y_at, r_at]).astype(jnp.int32)
    bucket_count, head_count = bucket_bias.shape
    hd = width // head_count
    block = 4 * tokens
    length = segment_ids.size
    reach = (bucket_table.shape[0] - 1) // 2
    assert reach == tokens and lax.axis_size("x") == lax.axis_size("c") == 2

    hidden_in = inputs[0].astype(F32)
    cot_own = cotangent[0]
    scale_first = norm_scale(hidden_in)
    normed = (hidden_in * scale_first * gain_attention).astype(BF16)
    normed_parts = from_group(normed, "z")

    joined = jnp.concatenate([query_weight, key_weight, value_weight, output_weight], axis=1)
    if repeat > 1:
        joined = lax.all_gather(joined, "r", axis=0, tiled=True)
    head_rows = from_group(joined, SQUARE)
    other_rows = swap(jnp.concatenate([part[:, : 3 * width] for part in head_rows]), "c", 1)
    out_rows = jnp.concatenate([part[:, 3 * width :] for part in head_rows])
    units = jnp.concatenate([gate_weight, up_weight, down_weight], axis=1)
    unit_rows = lax.all_gather(units, UNITS_GROUP, axis=0, tiled=True)
    gate_piece, up_piece, down_piece = (
        unit_rows[:, at * width : (at + 1) * width] for at in range(3)
    )

    windows = segment_ids.reshape(-1, 2 * tokens)
    cuts = jnp.sum((windows < windows[:, -1:]).astype(jnp.int32), axis=1)
    turned = bucket_table[::-1]
    low_half, high_half = turned[reach : 2 * reach], turned[:reach]
    spots = jnp.concatenate(
        [
            jnp.broadcast_to(bucket_table[:1], (reach,)),
            low_half,
            low_half,
            high_half,
            high_half,
            jnp.broadcast_to(bucket_table[2 * reach :], (reach,)),
        ]
    )
    buckets = jnp.arange(bucket_count, dtype=jnp.int32)
    onehot = (spots[:, None] == buckets[None, :]).astype(F32)
    far_onehot = (bucket_table[0] == buckets).astype(F32)
    head_at = (x_at * 2 + y_at) * 4 + z_at
    bias_col = lax.dynamic_slice_in_dim(bucket_bias, head_at, 1, 1)[:, 0]
    diag = jnp.dot(onehot, bias_col, precision=HIGHEST) - jnp.sum(far_onehot * bias_col)
    hvec = jnp.pad(diag.reshape(3, 2 * reach), ((0, 5), (0, 0)))

    normed_parts, hvec, cuts, coords, out_rows = lax.optimization_barrier(
        (normed_parts, hvec, cuts, coords, out_rows)
    )
    made = kernel_call(
        functools.partial(qkv_body, hd),
        [shape((block + 4 * hd, 2 * hd), BF16)] * 4
        + [shape((block, width), BF16), shape((12 * hd, width), BF16)],
        [coords, *normed_parts, *head_rows, other_rows],
    )
    pieces, (normed_all, group_weights) = made[:4], made[4:]
    pieces = to_group(pieces, SQUARE)

    out_all = lax.all_gather(out_rows, ("z", "c"), axis=0, tiled=False)
    own = [piece[:block] for piece in pieces]
    other = swap(jnp.concatenate(own, axis=0), "c", 1)
    other = [other[at * block : (at + 1) * block] for at in range(4)]
    if repeat == 1:
        arrays = [*pieces, *other]
    else:
        own = [lax.all_gather(part, "r", axis=0, tiled=True) for part in own]
        other = [lax.all_gather(part, "r", axis=0, tiled=True) for part in other]
        arrays = [*pieces, *own, *other]
    places = 8
    out_t, lse, attended, keys, keys_t, queries = kernel_call(
        functools.partial(attend_body, tokens, hd, repeat),
        [
            shape((16, hd, tokens), BF16),
            shape((places, 8, 2 * tokens), F32),
            shape((places, hd, 2 * tokens), F32),
            shape((length, 2 * hd), BF16),
            shape((length // block, 2 * hd, block), BF16),
            shape((places, hd, 2 * tokens), BF16),
        ],
        [coords, cuts, hvec, *arrays],
        [
            pltpu.VMEM((9 * repeat, block, 2 * tokens), F32),
            pltpu.VMEM((places + 2, block, 2 * tokens), F32),
            pltpu.VMEM((places, 2 * hd, 2 * tokens), BF16),
            pltpu.VMEM((2, 8, 2 * tokens), F32),
            pltpu.VMEM((2, 8, 2 * tokens), F32),
            pltpu.VMEM((2, hd, 2 * tokens), F32),
        ],
        scalars=2,
        micros=20,
    )
    cot_sent, _ = lax.optimization_barrier((cot_own, other))
    cot_parts, out_t = lax.optimization_barrier((from_group(cot_sent, SQUARE), out_t))
    cot_all = jnp.concatenate(cot_parts, axis=0)
    arrived = lax.all_to_all(out_t, ("x", "y", "z"), split_axis=0, concat_axis=0, tiled=True)

    middle, normed_mid, out_full, features = kernel_call(
        functools.partial(output_body, hd),
        [
            shape((tokens, width), F32),
            shape((tokens, width), BF16),
            shape((width, width), BF16),
            shape((4, hd // 2, 8 * tokens), BF16),
        ],
        [
            coords,
            arrived.reshape(width, tokens),
            inputs[0],
            gain_feedforward.reshape(1, width),
            out_all,
        ],
    )
    scale_second = norm_scale(middle)
    mid_all = jnp.concatenate(from_group(normed_mid, SQUARE), axis=0)

    gate_act = nt(mid_all, gate_piece)
    up_act = nt(mid_all, up_piece)
    hidden_val, pullback = jax.vjp(gated, gate_act, up_act)
    hidden = hidden_val.astype(BF16)
    grad_gate, grad_up = pullback(nt(cot_all, down_piece))
    gate_low, up_low = grad_gate.astype(BF16), grad_up.astype(BF16)
    grad_norm = (nn(gate_low, gate_piece) + nn(up_low, up_piece)).astype(BF16)
    grad_parts = to_group(
        [grad_norm[at * tokens : (at + 1) * tokens] for at in range(4)], SQUARE
    )
    unit_grads = jnp.concatenate(
        [tn(gate_low, mid_all), tn(up_low, mid_all), tn(hidden, cot_all)], axis=1
    ).astype(BF16)
    feed = nn(hidden, down_piece).astype(BF16)
    grad_parts, unit_grads, feed = lax.optimization_barrier((grad_parts, unit_grads, feed))
    grad_norm_mid = sum(part.astype(F32) for part in grad_parts)

    grad_middle = cot_own.astype(F32) + norm_back(
        middle, scale_second, gain_feedforward, grad_norm_mid
    )
    gain_second_term = jnp.sum(grad_norm_mid * middle * scale_second, axis=0)
    grad_mid_low = grad_middle.astype(BF16)
    grad_attended = nt(out_full, grad_mid_low).astype(BF16)
    grad_arrived = lax.all_to_all(
        grad_attended.reshape(16, hd, tokens),
        ("x", "y", "z"),
        split_axis=0,
        concat_axis=0,
        tiled=True,
    )
    grad_arrived, grad_mid_low, unit_grads = lax.optimization_barrier(
        (grad_arrived, grad_mid_low, unit_grads)
    )
    grad_units = lax.psum_scatter(unit_grads, UNITS_GROUP, scatter_dimension=0, tiled=True)
    mixed = to_group(
        [
            jnp.concatenate(
                [
                    feed[at * tokens : (at + 1) * tokens],
                    grad_mid_low,
                    features[at],
                ]
            )
            for at in range(4)
        ],
        SQUARE,
    )

    grad_own, grad_other, grad_q, table_out, far_out = kernel_call(
        functools.partial(attend_back_body, tokens, hd, repeat),
        [
            shape((4 * repeat * block, 2 * hd), F32),
            shape((4 * repeat * block, 2 * hd), BF16),
            shape((16, hd, tokens), BF16),
            shape((8, 2 * tokens), F32),
            shape((8, 2 * tokens), F32),
        ],
        [coords, cuts, hvec, grad_arrived, queries, keys, keys_t, attended, lse],
        [
            pltpu.VMEM((places + 2, block, 2 * tokens), F32),
            pltpu.VMEM((length, 2 * hd), F32),
            pltpu.VMEM((3, block, 2 * tokens), F32),
            pltpu.VMEM((places, 2 * hd, 4 * tokens), BF16),
            pltpu.VMEM((places, 4 * tokens, 2 * hd), BF16),
            pltpu.VMEM((places, 16, 2 * tokens), F32),
            pltpu.VMEM((2, hd, 2 * tokens), F32),
        ],
        scalars=2,
        micros=20,
    )
    mixed, grad_own = lax.optimization_barrier((mixed, grad_own))
    grad_pairs = (grad_own + swap(grad_other, "c", 1).astype(F32)).astype(BF16)
    grad_pairs = [
        grad_pairs[at * repeat * block : (at + 1) * repeat * block] for at in range(4)
    ]
    if repeat > 1:
        grad_pairs = [
            lax.psum_scatter(part, "r", scatter_dimension=0, tiled=True) for part in grad_pairs
        ]
    grad_pieces = [
        jnp.concatenate([grad_pairs[at], grad_q[4 * at : 4 * at + 4].reshape(4 * hd, tokens)])
        for at in range(4)
    ]
    mixed, grad_pieces = lax.optimization_barrier((mixed, grad_pieces))
    grad_pieces = to_group(grad_pieces, SQUARE)

    made = kernel_call(
        functools.partial(project_back_body, hd),
        [
            shape((4, tokens, width), BF16),
            shape((8, width), F32),
            shape((8 * hd, block), BF16),
            shape((4 * hd, block), BF16),
        ],
        [coords, *grad_pieces, normed_all, group_weights, gain_attention.reshape(1, width)],
        [pltpu.VMEM((block, 8 * hd), BF16), pltpu.VMEM((block, 4 * hd), BF16)],
    )
    normed_grads, gain_first_rows, pairs_t, queries_t = made
    normed_grads = lax.all_to_all(normed_grads, "z", split_axis=0, concat_axis=0, tiled=True)
    keep, send = kernel_call(
        functools.partial(head_grads_body, hd),
        [shape((4, hd // 2, 3 * width), BF16)] * 2,
        [coords, pairs_t, queries_t, normed_all],
    )
    layer_out = (middle + sum(part[:tokens].astype(F32) for part in mixed)).astype(BF16)
    grad_mid_all = jnp.concatenate([part[tokens : 2 * tokens] for part in mixed], axis=0)
    near = jnp.stack([part[2 * tokens :] for part in mixed]).reshape(4, hd // 2, 8, tokens)
    near = near.transpose(2, 1, 0, 3).reshape(4 * hd, block)
    out_grads = nn(near, grad_mid_all).astype(BF16)

    table_out, far_out, keep, send, grad_units, out_grads = lax.optimization_barrier(
        (table_out, far_out, keep, send, grad_units, out_grads)
    )
    out_grads = out_grads.reshape(2, 4, hd // 2, width)
    out_grads = (out_grads[0].astype(F32) + swap(out_grads[1], "c", 1).astype(F32)).astype(BF16)
    head_grads = (keep.astype(F32) + swap(send, "c", 1).astype(F32)).astype(BF16)
    bucket_grad = jnp.dot(table_out[:3].reshape(1, -1), onehot, precision=HIGHEST)[0]
    bucket_grad = bucket_grad + far_onehot * jnp.sum(far_out)
    head_mark = (jnp.arange(head_count) == head_at).astype(F32)
    bias_term = bucket_grad[:, None] * head_mark[None, :]
    sums = jnp.concatenate([jnp.sum(gain_first_rows, axis=0), gain_second_term, bias_term.ravel()])
    sums = sums + swap(sums, "c", 1)
    sums = sum_everywhere(sums, SQUARE)
    head_grads = to_group([head_grads[at] for at in range(4)], SQUARE)
    normed_grads, head_grads, sums, out_grads = lax.optimization_barrier(
        (normed_grads, head_grads, sums, out_grads)
    )
    out_grads, sums = sum_over_z(out_grads, sums)
    head_grads = sum(part.astype(F32) for part in head_grads)
    if repeat > 1:
        sums = lax.psum(sums, "r")
        out_grads = lax.psum_scatter(
            out_grads.astype(BF16), "r", scatter_dimension=0, tiled=True
        ).astype(F32)
        head_grads = lax.psum_scatter(
            head_grads.astype(BF16), "r", scatter_dimension=0, tiled=True
        ).astype(F32)
    gain_first_grad, gain_second_grad = sums[:width], sums[width : 2 * width]
    bias_grad = sums[2 * width :].reshape(bucket_count, head_count)

    grad_inputs = kernel_call(
        finish_body,
        shape((tokens, width), BF16),
        [normed_grads, inputs[0], grad_middle, gain_attention.reshape(1, width)],
        scalars=0,
        micros=100,
    )
    unit_grads = grad_units.astype(F32)
    return (
        layer_out[None],
        grad_inputs[None],
        gain_first_grad,
        head_grads[:, :width],
        head_grads[:, width : 2 * width],
        head_grads[:, 2 * width :],
        out_grads,
        bias_grad,
        gain_second_grad,
        unit_grads[:, :width],
        unit_grads[:, width : 2 * width],
        unit_grads[:, 2 * width :],
    )


def solution(mesh):
    owners, runs = mesh.shape["ulysses"], mesh.shape["blk"]
    fine = Mesh(mesh.devices.reshape(2, owners // 2, 4, 2, runs // 8), EVERY)
    tokens = P(("z", "y", "r"), ("x", "c"), None)
    rows = P(EVERY, None)
    return jax.shard_map(
        body,
        mesh=fine,
        in_specs=(tokens, tokens) + (P(),) * 3 + (rows,) * 4 + (P(),) * 2 + (rows,) * 3,
        out_specs=(tokens, tokens, P()) + (rows,) * 4 + (P(),) * 2 + (rows,) * 3,
        check_vma=False,
    )
```

profile of v0, /device:TPU:0, one launch (start us, length us, event | category | flops | bytes accessed | tf_op | source)
XLA Modules:
  0.0 257.4 jit_solution(2250219389354995577)
XLA Ops:
  9.6 3.1 %collective-permute-start = (bf16[128,1024]{1,0:T(8,128)(2,1)S(1)}, bf16[128,1024]{1,0:T(8,128)(2,1)S(1)}, u32[]{:S(2)}, u32[]{:S(2)}) collective-permute-start(bf16[128,1024]{1,0:T(8,128)(2,1)S(1)} %fusion.31.refs_0_), channel_id=1, source_target_pairs={{0,2},{2,0},{4,6},{6,4},{1,3},{3,1},{5,7},{7,5},{8,10},{10,8},{12,... | collective-permute-start | bytes 786440 | tf_op jit(solution)/shard_map/ppermute | solution.py:45
  12.7 2.6 %collective-permute-start.1 = (bf16[128,1024]{1,0:T(8,128)(2,1)S(1)}, bf16[128,1024]{1,0:T(8,128)(2,1)S(1)}, u32[]{:S(2)}, u32[]{:S(2)}) collective-permute-start(bf16[128,1024]{1,0:T(8,128)(2,1)S(1)} %fusion.31.refs_0_), channel_id=1, source_target_pairs={{0,4},{2,6},{4,0},{6,2},{1,5},{3,7},{5,1},{7,3},{8,12},{10,14},{12... | collective-permute-start | bytes 786440 | tf_op jit(solution)/shard_map/ppermute | solution.py:45
  18.7 2.7 %collective-permute-start.5 = (bf16[32,4096]{1,0:T(8,128)(2,1)S(1)}, bf16[32,4096]{1,0:T(8,128)(2,1)S(1)}, u32[]{:S(2)}, u32[]{:S(2)}) collective-permute-start(bf16[32,4096]{1,0:T(8,128)(2,1)S(1)} %constant_dynamic-update-slice_fusion.1.refs_4_), channel_id=1, source_target_pairs={{0,17},{1,16},{16,1},{17,0},{2,19},{3,18},{18,3},{19,2},{4,21},{5,... | collective-permute-start | bytes 786440 | tf_op jit(solution)/shard_map/ppermute | solution.py:45
  37.6 2.3 collective-permute-done.6.refs_8_
  40.7 4.1 %shard_map.229 = (bf16[768,128]{1,0:T(8,128)(2,1)}, bf16[768,128]{1,0:T(8,128)(2,1)}, bf16[768,128]{1,0:T(8,128)(2,1)}, bf16[768,128]{1,0:T(8,128)(2,1)}, bf16[5...) custom-call(s32[5]{0:T(128)} %stack.35.coords, bf16[128,1024]{1,0:T(8,128)(2,1)} %copy-done.6, ...), custom_call_target="tpu_custom_call" | custom-call | flops 4600000000 | bytes 1048576 | tf_op jit(solution)/shard_map/pallas_call | solution.py:79
  44.8 2.5 collective-permute-start.9
  49.3 4.5 %collective-permute-done.9.refs_3_ = bf16[768,128]{1,0:T(8,128)(2,1)S(1)} collective-permute-done((bf16[768,128]{1,0:T(8,128)(2,1)}, bf16[768,128]{1,0:T(8,128)(2,1)S(1)}, u32[]{:S(2)}, u32[]{:S(2)}) %collective-permute-start.9) | collective-permute-done | bytes 196640 | tf_op jit(solution)/shard_map/ppermute | solution.py:45
  53.8 3.5 %collective-permute-done.8.refs_2_ = bf16[768,128]{1,0:T(8,128)(2,1)S(1)} collective-permute-done((bf16[768,128]{1,0:T(8,128)(2,1)}, bf16[768,128]{1,0:T(8,128)(2,1)S(1)}, u32[]{:S(2)}, u32[]{:S(2)}) %collective-permute-start.8) | collective-permute-done | bytes 196640 | tf_op jit(solution)/shard_map/ppermute | solution.py:45
  63.6 13.0 %shard_map.230 = (bf16[16,64,128]{2,1,0:T(8,128)(2,1)}, f32[8,8,256]{2,1,0:T(8,128)}, f32[8,64,256]{2,1,0:T(8,128)}, bf16[4096,128]{1,0:T(8,128)(2,1)}, bf16[8,1...) custom-call(s32[5]{0:T(128)} %stack.35.coords, s32[16]{0:T(128)} %convert_reduce_fusion.cuts, f32[8,256]{1,0:T(8,128)} %pad.12.hvec, ...), custom_call_target="tpu_custom_call" | custom-call | flops 23000000512 | bytes 1048576 | tf_op jit(solution)/shard_map/pallas_call | solution.py:79
  76.6 6.8 %all-to-all-start = ((bf16[16,64,128]{2,1,0:T(8,128)(2,1)}), bf16[16,64,128]{2,1,0:T(8,128)(2,1)S(1)}, u32[]{:S(2)}, u32[]{:S(2)}) async-start(bf16[16,64,128]{2,1,0:T(8,128)(2,1)} %get-tuple-element.101), calls=%async_computation | async-start | bytes 524288 | tf_op jit(solution)/shard_map/all_to_all | solution.py:589
  83.7 17.0 %all-to-all-done = bf16[16,64,128]{2,1,0:T(8,128)(2,1)S(1)} async-done(((bf16[16,64,128]{2,1,0:T(8,128)(2,1)}), bf16[16,64,128]{2,1,0:T(8,128)(2,1)S(1)}, u32[]{:S(2)}, u32[]{:S(2)}) %all-to-all-start) | async-done | bytes 262176 | tf_op jit(solution)/shard_map/all_to_all | solution.py:589
  101.5 4.1 %shard_map.231 = (f32[128,1024]{1,0:T(8,128)}, bf16[128,1024]{1,0:T(8,128)(2,1)}, bf16[1024,1024]{1,0:T(8,128)(2,1)}, bf16[4,32,1024]{2,1,0:T(8,128)(2,1)}) custom-call(s32[5]{0:T(128)} %stack.35.coords, bf16[1024,128]{1,0:T(8,128)(2,1)} %bitcast.115, bf16[128,1024]{1,0:T(8,128)(2,1)} %bitcast.107, f32[1,1024]{1,0:T(1,128)} %bitcast.121, ...), custom_call_target="tpu_custom_call" | custom-call | flops 4600000000 | bytes 1048576 | tf_op jit(solution)/shard_map/pallas_call | solution.py:79
  106.6 2.4 collective-permute-start.16
  111.2 2.9 %collective-permute-done.14 = bf16[128,1024]{1,0:T(8,128)(2,1)S(1)} collective-permute-done((bf16[128,1024]{1,0:T(8,128)(2,1)}, bf16[128,1024]{1,0:T(8,128)(2,1)S(1)}, u32[]{:S(2)}, u32[]{:S(2)}) %collective-permute-start.14) | collective-permute-done | bytes 262176 | tf_op jit(solution)/shard_map/ppermute | solution.py:45
  115.0 5.6 %collective-permute-done.16 = bf16[128,1024]{1,0:T(8,128)(2,1)S(1)} collective-permute-done((bf16[128,1024]{1,0:T(8,128)(2,1)}, bf16[128,1024]{1,0:T(8,128)(2,1)S(1)}, u32[]{:S(2)}, u32[]{:S(2)}) %collective-permute-start.16) | collective-permute-done | bytes 262176 | tf_op jit(solution)/shard_map/ppermute | solution.py:45
  121.9 2.5 fusion.9
  136.5 2.2 pad_maximum_fusion
  138.7 2.6 %convolution_convert_fusion.3 = bf16[512,1024]{1,0:T(8,128)(2,1)S(1)} fusion(bf16[512,704]{0,1:T(8,128)(2,1)} %copy-done.38, bf16[704,3072]{1,0:T(8,128)(2,1)} %all-gather.4.cloned.1.call-done), kind=kOutput, calls=%fused_computation.8 | convolution fusion | flops 738721792 | bytes 3211264 | tf_op jit(solution)/shard_map/dot_general | solution.py:36
  142.7 4.6 %collective-permute-done.19 = bf16[128,1024]{1,0:T(8,128)(2,1)S(1)} collective-permute-done((bf16[128,1024]{1,0:T(8,128)(2,1)S(1)}, bf16[128,1024]{1,0:T(8,128)(2,1)S(1)}, u32[]{:S(2)}, u32[]{:S(2)}) %collective-permute-start.19) | collective-permute-done | bytes 262176 | tf_op jit(solution)/shard_map/ppermute | solution.py:45
  150.1 14.1 %all_to_all.15.refs_0_ = bf16[16,64,128]{2,1,0:T(8,128)(2,1)} all-to-all(bf16[16,64,128]{2,1,0:T(8,128)(2,1)S(1)} %bitcast.106), channel_id=1, replica_groups=mesh['x'=2,'c'=2,'z'=4,'y'=2,'r'=1] {'x','y','z'}, dimensions={0} | all-to-all | bytes 524288 | tf_op jit(solution)/shard_map/all_to_all | solution.py:633
  167.6 2.4 collective-permute-start.22
  170.0 17.6 %shard_map.232 = (f32[2048,128]{1,0:T(8,128)}, bf16[2048,128]{1,0:T(8,128)(2,1)}, bf16[16,64,128]{2,1,0:T(8,128)(2,1)}, f32[8,256]{1,0:T(8,128)}, f32[8,256]{1,0:T(8,128)}) custom-call(s32[5]{0:T(128)} %stack.35.coords, s32[16]{0:T(128)} %convert_reduce_fusion.cuts, f32[8,256]{1,0:T(8,128)} %pad.12.hvec, bf16[16,64,128]{2,1,0:T(8,128)(2,1)} %all_to_all.15.refs_0_, ...), custom_call_target="tpu_custom_call" | custom-call | flops 23000000512 | bytes 1048576 | tf_op jit(solution)/shard_map/pallas_call | solution.py:79
  188.6 4.1 %collective-permute-done.22 = bf16[288,1024]{1,0:T(8,128)(2,1)S(1)} collective-permute-done((bf16[288,1024]{1,0:T(8,128)(2,1)S(1)}, bf16[288,1024]{1,0:T(8,128)(2,1)S(1)}, u32[]{:S(2)}, u32[]{:S(2)}) %collective-permute-start.22) | collective-permute-done | bytes 589856 | tf_op jit(solution)/shard_map/ppermute | solution.py:45
  196.3 2.1 collective-permute-start.26
  202.1 2.1 collective-permute-done.26.refs_3_
  204.9 4.3 %shard_map.233 = (bf16[4,128,1024]{2,1,0:T(8,128)(2,1)}, f32[8,1024]{1,0:T(8,128)}, bf16[512,512]{1,0:T(8,128)(2,1)}, bf16[256,512]{1,0:T(8,128)(2,1)}) custom-call(s32[5]{0:T(128)} %stack.35.coords, bf16[768,128]{1,0:T(8,128)(2,1)} %get-tuple-element.136.refs_0_, bf16[768,128]{1,0:T(8,128)(2,1)} %copy-done.35, bf16[768,128]{1,0:T(8,128)(2,1)} %copy-done.36, ...), custom_call_target="tpu_custom_call" | custom-call | flops 4600000000 | bytes 1048576 | tf_op jit(solution)/shard_map/pallas_call | solution.py:79
  209.2 4.2 %all-to-all-start.2 = ((bf16[4,128,1024]{2,1,0:T(8,128)(2,1)}), bf16[4,128,1024]{2,1,0:T(8,128)(2,1)S(1)}, u32[]{:S(2)}, u32[]{:S(2)}) async-start(bf16[4,128,1024]{2,1,0:T(8,128)(2,1)} %get-tuple-element.142), calls=%async_computation.2 | async-start | bytes 2097152 | tf_op jit(solution)/shard_map/all_to_all | solution.py:708
  213.5 3.8 %shard_map.234 = (bf16[4,32,3072]{2,1,0:T(8,128)(2,1)}, bf16[4,32,3072]{2,1,0:T(8,128)(2,1)}) custom-call(s32[5]{0:T(128)} %stack.35.coords, bf16[512,512]{1,0:T(8,128)(2,1)} %get-tuple-element.145.pairs_t, bf16[256,512]{1,0:T(8,128)(2,1)} %get-tuple-element.146.queries_t, bf16[512,1024]{1,0:T(8,128)(2,1)} %get-tuple-element.140.refs_4_.rows_all), custom_call_target="tpu_custom_call" | custom-call | flops 4600000000 | bytes 1048576 | tf_op jit(solution)/shard_map/pallas_call | solution.py:79
  231.8 4.2 %all-to-all-done.2.refs_0_ = bf16[4,128,1024]{2,1,0:T(8,128)(2,1)S(1)} async-done(((bf16[4,128,1024]{2,1,0:T(8,128)(2,1)}), bf16[4,128,1024]{2,1,0:T(8,128)(2,1)S(1)}, u32[]{:S(2)}, u32[]{:S(2)}) %all-to-all-start.2) | async-done | bytes 1048608 | tf_op jit(solution)/shard_map/all_to_all | solution.py:708
  236.2 2.9 %collective-permute-done.30 = bf16[32,3072]{1,0:T(8,128)(2,1)S(1)} collective-permute-done((bf16[32,3072]{1,0:T(8,128)(2,1)S(1)}, bf16[32,3072]{1,0:T(8,128)(2,1)S(1)}, u32[]{:S(2)}, u32[]{:S(2)}) %collective-permute-start.30) | collective-permute-done | bytes 196640 | tf_op jit(solution)/shard_map/ppermute | solution.py:45
  239.2 3.9 %collective-permute-start.38 = (bf16[40,1024]{1,0:T(8,128)(2,1)S(1)}, bf16[40,1024]{1,0:T(8,128)(2,1)S(1)}, u32[]{:S(2)}, u32[]{:S(2)}) collective-permute-start(bf16[40,1024]{1,0:T(8,128)(2,1)S(1)} %get-tuple-element.232), channel_id=1, source_target_pairs={{0,6},{2,4},{4,2},{6,0},{1,7},{3,5},{5,3},{7,1},{8,14},{10,12},{12... | collective-permute-start | bytes 245768 | tf_op jit(solution)/shard_map/ppermute | solution.py:45
  243.8 2.5 shard_map.235
  (273 shorter events, 85.7 us)
Async XLA Ops:
  7.2 93.5 %all-gather.6.cloned.1.call-start = ((), (), s32[]{:S(2)}) async-start(), calls=%async_computation.6 | async-start | bytes 2359296 | tf_op jit(solution)/shard_map/all_gather | solution.py:553
  9.6 26.6 %collective-permute-start = (bf16[128,1024]{1,0:T(8,128)(2,1)S(1)}, bf16[128,1024]{1,0:T(8,128)(2,1)S(1)}, u32[]{:S(2)}, u32[]{:S(2)}) collective-permute-start(bf16[128,1024]{1,0:T(8,128)(2,1)S(1)} %fusion.31.refs_0_), channel_id=1, source_target_pairs={{0,2},{2,0},{4,6},{6,4},{1,3},{3,1},{5,7},{7,5},{8,10},{10,8},{12,... | collective-permute-start | bytes 786440 | tf_op jit(solution)/shard_map/ppermute | solution.py:45
  12.7 23.5 %collective-permute-start.1 = (bf16[128,1024]{1,0:T(8,128)(2,1)S(1)}, bf16[128,1024]{1,0:T(8,128)(2,1)S(1)}, u32[]{:S(2)}, u32[]{:S(2)}) collective-permute-start(bf16[128,1024]{1,0:T(8,128)(2,1)S(1)} %fusion.31.refs_0_), channel_id=1, source_target_pairs={{0,4},{2,6},{4,0},{6,2},{1,5},{3,7},{5,1},{7,3},{8,12},{10,14},{12... | collective-permute-start | bytes 786440 | tf_op jit(solution)/shard_map/ppermute | solution.py:45
  15.3 20.9 %collective-permute-start.2 = (bf16[128,1024]{1,0:T(8,128)(2,1)S(1)}, bf16[128,1024]{1,0:T(8,128)(2,1)S(1)}, u32[]{:S(2)}, u32[]{:S(2)}) collective-permute-start(bf16[128,1024]{1,0:T(8,128)(2,1)S(1)} %fusion.31.refs_0_), channel_id=1, source_target_pairs={{0,6},{2,4},{4,2},{6,0},{1,7},{3,5},{5,3},{7,1},{8,14},{10,12},{12... | collective-permute-start | bytes 786440 | tf_op jit(solution)/shard_map/ppermute | solution.py:45
  18.7 10.1 %collective-permute-start.5 = (bf16[32,4096]{1,0:T(8,128)(2,1)S(1)}, bf16[32,4096]{1,0:T(8,128)(2,1)S(1)}, u32[]{:S(2)}, u32[]{:S(2)}) collective-permute-start(bf16[32,4096]{1,0:T(8,128)(2,1)S(1)} %constant_dynamic-update-slice_fusion.1.refs_4_), channel_id=1, source_target_pairs={{0,17},{1,16},{16,1},{17,0},{2,19},{3,18},{18,3},{19,2},{4,21},{5,... | collective-permute-start | bytes 786440 | tf_op jit(solution)/shard_map/ppermute | solution.py:45
  21.4 12.1 %collective-permute-start.4 = (bf16[32,4096]{1,0:T(8,128)(2,1)S(1)}, bf16[32,4096]{1,0:T(8,128)(2,1)S(1)}, u32[]{:S(2)}, u32[]{:S(2)}) collective-permute-start(bf16[32,4096]{1,0:T(8,128)(2,1)S(1)} %constant_dynamic-update-slice_fusion.1.refs_4_), channel_id=1, source_target_pairs={{0,16},{1,17},{16,0},{17,1},{2,18},{3,19},{18,2},{19,3},{4,20},{5,... | collective-permute-start | bytes 786440 | tf_op jit(solution)/shard_map/ppermute | solution.py:45
  36.3 85.5 %all-gather.4.cloned.1.call-start = ((), (), s32[]{:S(2)}) async-start(), calls=%async_computation.4 | async-start | bytes 4866048 | tf_op jit(solution)/shard_map/all_gather | solution.py:514
  44.8 8.9 %collective-permute-start.9 = (bf16[768,128]{1,0:T(8,128)(2,1)}, bf16[768,128]{1,0:T(8,128)(2,1)S(1)}, u32[]{:S(2)}, u32[]{:S(2)}) collective-permute-start(bf16[768,128]{1,0:T(8,128)(2,1)} %get-tuple-element.96), channel_id=1, source_target_pairs={{0,17},{1,16},{16,1},{17,0},{2,19},{3,18},{18,3},{19,2},{4,21},{5,... | collective-permute-start | bytes 589832 | tf_op jit(solution)/shard_map/ppermute | solution.py:45
  47.3 9.9 %collective-permute-start.8 = (bf16[768,128]{1,0:T(8,128)(2,1)}, bf16[768,128]{1,0:T(8,128)(2,1)S(1)}, u32[]{:S(2)}, u32[]{:S(2)}) collective-permute-start(bf16[768,128]{1,0:T(8,128)(2,1)} %get-tuple-element.95), channel_id=1, source_target_pairs={{0,16},{1,17},{16,0},{17,1},{2,18},{3,19},{18,2},{19,3},{4,20},{5,... | collective-permute-start | bytes 589832 | tf_op jit(solution)/shard_map/ppermute | solution.py:45
  47.8 9.4 %collective-permute-start.7 = (bf16[768,128]{1,0:T(8,128)(2,1)}, bf16[768,128]{1,0:T(8,128)(2,1)S(1)}, u32[]{:S(2)}, u32[]{:S(2)}) collective-permute-start(bf16[768,128]{1,0:T(8,128)(2,1)} %get-tuple-element.94), channel_id=1, source_target_pairs={{0,1},{1,0},{16,17},{17,16},{2,3},{3,2},{18,19},{19,18},{4,5},{5,4... | collective-permute-start | bytes 589832 | tf_op jit(solution)/shard_map/ppermute | solution.py:45
  60.1 16.5 %collective-permute-start.11 = (bf16[128,1024]{1,0:T(8,128)(2,1)S(1)}, bf16[128,1024]{1,0:T(8,128)(2,1)S(1)}, u32[]{:S(2)}, u32[]{:S(2)}) collective-permute-start(bf16[128,1024]{1,0:T(8,128)(2,1)S(1)} %bitcast.102), channel_id=1, source_target_pairs={{0,1},{1,0},{16,17},{17,16},{2,3},{3,2},{18,19},{19,18},{4,5},{5,4... | collective-permute-start | bytes 786440 | tf_op jit(solution)/shard_map/ppermute | solution.py:45
  61.5 15.1 %collective-permute-start.12 = (bf16[128,1024]{1,0:T(8,128)(2,1)S(1)}, bf16[128,1024]{1,0:T(8,128)(2,1)S(1)}, u32[]{:S(2)}, u32[]{:S(2)}) collective-permute-start(bf16[128,1024]{1,0:T(8,128)(2,1)S(1)} %bitcast.103), channel_id=1, source_target_pairs={{0,16},{1,17},{16,0},{17,1},{2,18},{3,19},{18,2},{19,3},{4,20},{5,... | collective-permute-start | bytes 786440 | tf_op jit(solution)/shard_map/ppermute | solution.py:45
  63.0 13.6 %collective-permute-start.13 = (bf16[128,1024]{1,0:T(8,128)(2,1)S(1)}, bf16[128,1024]{1,0:T(8,128)(2,1)S(1)}, u32[]{:S(2)}, u32[]{:S(2)}) collective-permute-start(bf16[128,1024]{1,0:T(8,128)(2,1)S(1)} %bitcast.104), channel_id=1, source_target_pairs={{0,17},{1,16},{16,1},{17,0},{2,19},{3,18},{18,3},{19,2},{4,21},{5,... | collective-permute-start | bytes 786440 | tf_op jit(solution)/shard_map/ppermute | solution.py:45
  76.6 24.1 %all-to-all-start = ((bf16[16,64,128]{2,1,0:T(8,128)(2,1)}), bf16[16,64,128]{2,1,0:T(8,128)(2,1)S(1)}, u32[]{:S(2)}, u32[]{:S(2)}) async-start(bf16[16,64,128]{2,1,0:T(8,128)(2,1)} %get-tuple-element.101), calls=%async_computation | async-start | bytes 524288 | tf_op jit(solution)/shard_map/all_to_all | solution.py:589
  83.4 133.9 %reduce-scatter.2.cloned.1.call-start = ((), (), s32[]{:S(2)}) async-start(), calls=%async_computation.5 | async-start | bytes 4866048 | tf_op jit(solution)/shard_map/reduce_scatter | solution.py:643
  105.5 8.5 %collective-permute-start.14 = (bf16[128,1024]{1,0:T(8,128)(2,1)}, bf16[128,1024]{1,0:T(8,128)(2,1)S(1)}, u32[]{:S(2)}, u32[]{:S(2)}) collective-permute-start(bf16[128,1024]{1,0:T(8,128)(2,1)} %get-tuple-element.108), channel_id=1, source_target_pairs={{0,1},{1,0},{16,17},{17,16},{2,3},{3,2},{18,19},{19,18},{4,5},{5,4... | collective-permute-start | bytes 786440 | tf_op jit(solution)/shard_map/ppermute | solution.py:45
  105.5 9.4 %collective-permute-start.15 = (bf16[128,1024]{1,0:T(8,128)(2,1)}, bf16[128,1024]{1,0:T(8,128)(2,1)S(1)}, u32[]{:S(2)}, u32[]{:S(2)}) collective-permute-start(bf16[128,1024]{1,0:T(8,128)(2,1)} %get-tuple-element.108), channel_id=1, source_target_pairs={{0,16},{1,17},{16,0},{17,1},{2,18},{3,19},{18,2},{19,3},{4,20},{5,... | collective-permute-start | bytes 786440 | tf_op jit(solution)/shard_map/ppermute | solution.py:45
  106.6 13.9 %collective-permute-start.16 = (bf16[128,1024]{1,0:T(8,128)(2,1)}, bf16[128,1024]{1,0:T(8,128)(2,1)S(1)}, u32[]{:S(2)}, u32[]{:S(2)}) collective-permute-start(bf16[128,1024]{1,0:T(8,128)(2,1)} %get-tuple-element.108), channel_id=1, source_target_pairs={{0,17},{1,16},{16,1},{17,0},{2,19},{3,18},{18,3},{19,2},{4,21},{5,... | collective-permute-start | bytes 786440 | tf_op jit(solution)/shard_map/ppermute | solution.py:45
  132.1 9.3 %collective-permute-start.17 = (bf16[128,1024]{1,0:T(8,128)(2,1)}, bf16[128,1024]{1,0:T(8,128)(2,1)S(1)}, u32[]{:S(2)}, u32[]{:S(2)}) collective-permute-start(bf16[128,1024]{1,0:T(8,128)(2,1)} %get-tuple-element.189), channel_id=1, source_target_pairs={{0,1},{1,0},{16,17},{17,16},{2,3},{3,2},{18,19},{19,18},{4,5},{5,4... | collective-permute-start | bytes 786440 | tf_op jit(solution)/shard_map/ppermute | solution.py:45
  133.6 9.2 %collective-permute-start.18 = (bf16[128,1024]{1,0:T(8,128)(2,1)S(1)}, bf16[128,1024]{1,0:T(8,128)(2,1)S(1)}, u32[]{:S(2)}, u32[]{:S(2)}) collective-permute-start(bf16[128,1024]{1,0:T(8,128)(2,1)S(1)} %get-tuple-element.188), channel_id=1, source_target_pairs={{0,16},{1,17},{16,0},{17,1},{2,18},{3,19},{18,2},{19,3},{4,20},{5,... | collective-permute-start | bytes 786440 | tf_op jit(solution)/shard_map/ppermute | solution.py:45
  135.0 12.3 %collective-permute-start.19 = (bf16[128,1024]{1,0:T(8,128)(2,1)S(1)}, bf16[128,1024]{1,0:T(8,128)(2,1)S(1)}, u32[]{:S(2)}, u32[]{:S(2)}) collective-permute-start(bf16[128,1024]{1,0:T(8,128)(2,1)S(1)} %get-tuple-element.187), channel_id=1, source_target_pairs={{0,17},{1,16},{16,1},{17,0},{2,19},{3,18},{18,3},{19,2},{4,21},{5,... | collective-permute-start | bytes 786440 | tf_op jit(solution)/shard_map/ppermute | solution.py:45
  166.5 22.1 %collective-permute-start.20 = (bf16[288,1024]{1,0:T(8,128)(2,1)}, bf16[288,1024]{1,0:T(8,128)(2,1)S(1)}, u32[]{:S(2)}, u32[]{:S(2)}) collective-permute-start(bf16[288,1024]{1,0:T(8,128)(2,1)} %get-tuple-element.220), channel_id=1, source_target_pairs={{0,1},{1,0},{16,17},{17,16},{2,3},{3,2},{18,19},{19,18},{4,5},{5,4... | collective-permute-start | bytes 1769480 | tf_op jit(solution)/shard_map/ppermute | solution.py:45
  166.5 22.1 %collective-permute-start.21 = (bf16[288,1024]{1,0:T(8,128)(2,1)}, bf16[288,1024]{1,0:T(8,128)(2,1)S(1)}, u32[]{:S(2)}, u32[]{:S(2)}) collective-permute-start(bf16[288,1024]{1,0:T(8,128)(2,1)} %get-tuple-element.221), channel_id=1, source_target_pairs={{0,16},{1,17},{16,0},{17,1},{2,18},{3,19},{18,2},{19,3},{4,20},{5,... | collective-permute-start | bytes 1769480 | tf_op jit(solution)/shard_map/ppermute | solution.py:45
  167.6 25.1 %collective-permute-start.22 = (bf16[288,1024]{1,0:T(8,128)(2,1)S(1)}, bf16[288,1024]{1,0:T(8,128)(2,1)S(1)}, u32[]{:S(2)}, u32[]{:S(2)}) collective-permute-start(bf16[288,1024]{1,0:T(8,128)(2,1)S(1)} %get-tuple-element.219), channel_id=1, source_target_pairs={{0,17},{1,16},{16,1},{17,0},{2,19},{3,18},{18,3},{19,2},{4,21},{5,... | collective-permute-start | bytes 1769480 | tf_op jit(solution)/shard_map/ppermute | solution.py:45
  196.3 7.9 %collective-permute-start.26 = (bf16[768,128]{1,0:T(8,128)(2,1)S(1)}, bf16[768,128]{1,0:T(8,128)(2,1)S(1)}, u32[]{:S(2)}, u32[]{:S(2)}) collective-permute-start(bf16[768,128]{1,0:T(8,128)(2,1)S(1)} %get-tuple-element.139), channel_id=1, source_target_pairs={{0,17},{1,16},{16,1},{17,0},{2,19},{3,18},{18,3},{19,2},{4,21},{5,... | collective-permute-start | bytes 589832 | tf_op jit(solution)/shard_map/ppermute | solution.py:45
  209.2 26.8 %all-to-all-start.2 = ((bf16[4,128,1024]{2,1,0:T(8,128)(2,1)}), bf16[4,128,1024]{2,1,0:T(8,128)(2,1)S(1)}, u32[]{:S(2)}, u32[]{:S(2)}) async-start(bf16[4,128,1024]{2,1,0:T(8,128)(2,1)} %get-tuple-element.142), calls=%async_computation.2 | async-start | bytes 2097152 | tf_op jit(solution)/shard_map/all_to_all | solution.py:708
  217.3 10.7 %collective-permute-start.27 = (bf16[4,32,3072]{2,1,0:T(8,128)(2,1)}, bf16[4,32,3072]{2,1,0:T(8,128)(2,1)S(1)}, u32[]{:S(2)}, u32[]{:S(2)}) collective-permute-start(bf16[4,32,3072]{2,1,0:T(8,128)(2,1)} %get-tuple-element.151), channel_id=1, source_target_pairs={{0,8},{8,0},{1,9},{9,1},{2,10},{10,2},{3,11},{11,3},{4,12},{12,4},... | collective-permute-start | bytes 2359304 | tf_op jit(solution)/shard_map/ppermute | solution.py:45
  220.3 11.5 %collective-permute-start.35 = (bf16[4,32,1024]{2,1,0:T(8,128)(2,1)S(1)}, bf16[4,32,1024]{2,1,0:T(8,128)(2,1)S(1)}, u32[]{:S(2)}, u32[]{:S(2)}) collective-permute-start(bf16[4,32,1024]{2,1,0:T(8,128)(2,1)S(1)} %bitcast.116), channel_id=1, source_target_pairs={{0,8},{8,0},{1,9},{9,1},{2,10},{10,2},{3,11},{11,3},{4,12},{12,4},... | collective-permute-start | bytes 786440 | tf_op jit(solution)/shard_map/ppermute | solution.py:45
  228.2 7.8 %collective-permute-start.28 = (bf16[32,3072]{1,0:T(8,128)(2,1)S(1)}, bf16[32,3072]{1,0:T(8,128)(2,1)S(1)}, u32[]{:S(2)}, u32[]{:S(2)}) collective-permute-start(bf16[32,3072]{1,0:T(8,128)(2,1)S(1)} %get-tuple-element.193), channel_id=1, source_target_pairs={{0,1},{1,0},{16,17},{17,16},{2,3},{3,2},{18,19},{19,18},{4,5},{5,4... | collective-permute-start | bytes 589832 | tf_op jit(solution)/shard_map/ppermute | solution.py:45
  228.7 7.4 %collective-permute-start.29 = (bf16[32,3072]{1,0:T(8,128)(2,1)S(1)}, bf16[32,3072]{1,0:T(8,128)(2,1)S(1)}, u32[]{:S(2)}, u32[]{:S(2)}) collective-permute-start(bf16[32,3072]{1,0:T(8,128)(2,1)S(1)} %get-tuple-element.192), channel_id=1, source_target_pairs={{0,16},{1,17},{16,0},{17,1},{2,18},{3,19},{18,2},{19,3},{4,20},{5,... | collective-permute-start | bytes 589832 | tf_op jit(solution)/shard_map/ppermute | solution.py:45
  230.3 8.8 %collective-permute-start.30 = (bf16[32,3072]{1,0:T(8,128)(2,1)S(1)}, bf16[32,3072]{1,0:T(8,128)(2,1)S(1)}, u32[]{:S(2)}, u32[]{:S(2)}) collective-permute-start(bf16[32,3072]{1,0:T(8,128)(2,1)S(1)} %get-tuple-element.191), channel_id=1, source_target_pairs={{0,17},{1,16},{16,1},{17,0},{2,19},{3,18},{18,3},{19,2},{4,21},{5,... | collective-permute-start | bytes 589832 | tf_op jit(solution)/shard_map/ppermute | solution.py:45
  239.2 7.9 %collective-permute-start.38 = (bf16[40,1024]{1,0:T(8,128)(2,1)S(1)}, bf16[40,1024]{1,0:T(8,128)(2,1)S(1)}, u32[]{:S(2)}, u32[]{:S(2)}) collective-permute-start(bf16[40,1024]{1,0:T(8,128)(2,1)S(1)} %get-tuple-element.232), channel_id=1, source_target_pairs={{0,6},{2,4},{4,2},{6,0},{1,7},{3,5},{5,3},{7,1},{8,14},{10,12},{12... | collective-permute-start | bytes 245768 | tf_op jit(solution)/shard_map/ppermute | solution.py:45
  (51 other events, 410.2 us)
Sparse Core Ops, SparseCore 0:
  36.4 30.3 all-gather.5
  68.4 53.3 all-gather.3
  164.4 48.4 reduce-scatter.1
where the time goes:
time: 259 us; the launch traced here: 257 us
  waiting for transfers between devices  67.2 us (26%)
  starting transfers between devices  55.3 us (21%)
  Pallas kernels  49.4 us (19%)
  local copies, waits for them, and re-layouts  21.3 us (8%)
  other arithmetic  18.8 us (7%)
  matrix products  16.5 us (6%)
  between operations  14.8 us (6%)
  blocking collectives  14.1 us (5%)
    pallas_call x7, Pallas kernels, kernel_call(): pl.pallas_call(body, out_shape=out_shapes, in_specs=in_specs, out_specs=j...  49.4 us
    ppermute x39, waiting for transfers between devices, swap(): return lax.ppermute(value, axis, [(at, at ^ mask) for at in range(size)])  44.6 us
    ppermute x39, starting transfers between devices, swap(): return lax.ppermute(value, axis, [(at, at ^ mask) for at in range(size)])  44 us
    all_to_all x1, waiting for transfers between devices, body(): lax.all_to_all(out_t, ('x', 'y', 'z'), split_axis=0, concat_axis=0, tiled...  17 us
    all_to_all x1, blocking collectives, body(): lax.all_to_all(grad_attended.reshape(16, hd, tokens), ('x', 'y', 'z'), sp...  14.1 us
    unnamed x104, local copies, waits for them, and re-layouts  9.26 us
    all_to_all x1, starting transfers between devices, body(): lax.all_to_all(out_t, ('x', 'y', 'z'), split_axis=0, concat_axis=0, tiled...  6.76 us
    dot_general x4, matrix products, nt(): lax.dot_general(left, right, (((1,), (1,)), ((), ())), preferred_element_...  6.05 us
  transfers between devices with their start and end apart: 44, of which 23 were waited for; matrix products, arithmetic and copies ran while one was open for 14% of the time, Pallas kernels for 19%

commit v1 on v0

--- a/solution.py
+++ b/solution.py
@@ -13,7 +13,7 @@
 HIGHEST = lax.Precision.HIGHEST
 F32 = jnp.float32
 BF16 = jnp.bfloat16
-VMEM_LIMIT = 60 * 1024 * 1024
+MEBI = 1024 * 1024
 SQUARE = ("x", "y")
 UNITS_GROUP = ("z", "c", "r")
 EVERY = ("x", "c", "z", "y", "r")
@@ -73,7 +73,7 @@
     return sum(part[:count] for part in arrived), total.ravel()[: values.size]
 
 
-def kernel_call(body, out_shapes, inputs, scratch=(), scalars=1, micros=4):
+def kernel_call(body, out_shapes, inputs, scratch=(), scalars=1, micros=4, mebi=60):
     in_specs = [pl.BlockSpec(memory_space=pltpu.SMEM)] * scalars
     in_specs += [pl.BlockSpec(memory_space=pltpu.VMEM)] * (len(inputs) - scalars)
     return pl.pallas_call(
@@ -82,7 +82,7 @@
         in_specs=in_specs,
         out_specs=jax.tree.map(lambda _: pl.BlockSpec(memory_space=pltpu.VMEM), out_shapes),
         scratch_shapes=list(scratch),
-        compiler_params=pltpu.CompilerParams(vmem_limit_bytes=VMEM_LIMIT),
+        compiler_params=pltpu.CompilerParams(vmem_limit_bytes=mebi * MEBI),
         cost_estimate=pl.CostEstimate(
             flops=int(micros * 1.15e9), bytes_accessed=1 << 20, transcendentals=0
         ),
@@ -93,14 +93,46 @@
     return jax.ShapeDtypeStruct(dims, dtype)
 
 
+def pack_body(*refs):
+    own_in, gain, out_rows = refs[:3]
+    heads, units = refs[3:6], refs[6:9]
+    message, joined, joined_units = refs[9:]
+    tokens, width = own_in.shape
+    values = own_in[...].astype(F32)
+    message[0:tokens, :] = (values * norm_scale(values) * gain[...]).astype(BF16)
+    message[tokens:, :] = out_rows[...]
+    for at in range(3):
+        joined[:, at * width : (at + 1) * width] = heads[at][...]
+        joined_units[:, at * width : (at + 1) * width] = units[at][...]
+
+
+def anchor_body(*refs):
+    refs[-1][...] = jnp.zeros_like(refs[-1])
+
+
+def anchor(values, micros):
+    return pl.pallas_call(
+        anchor_body,
+        out_shape=shape((8, 128), F32),
+        in_specs=[pl.BlockSpec(memory_space=pl.ANY)] * len(values),
+        out_specs=pl.BlockSpec(memory_space=pltpu.VMEM),
+        cost_estimate=pl.CostEstimate(
+            flops=int(micros * 1.15e9), bytes_accessed=1 << 20, transcendentals=0
+        ),
+    )(*values)
+
+
 def qkv_body(hd, coords, *refs):
-    blocks, parts, other_rows, pieces = refs[:4], refs[4:8], refs[8], refs[9:13]
-    rows_all, weights = refs[13:15]
+    blocks, parts, other_rows, cot_own, pieces = refs[:4], refs[4:8], refs[8], refs[9], refs[11:15]
+    rows_all, weights, onward = refs[15:18]
     c_at, y_at = coords[1], coords[3]
-    tokens, width = blocks[0].shape
-    half = hd // 2
+    width, half = rows_all.shape[1], hd // 2
+    tokens = rows_all.shape[0] // 4
     for at in range(4):
-        rows_all[at * tokens : (at + 1) * tokens, :] = blocks[at][...]
+        rows_all[at * tokens : (at + 1) * tokens, :] = blocks[at][0:tokens, :]
+        start = tokens + at * half
+        onward[start : start + half, :] = blocks[at][tokens:, :]
+    onward[0:tokens, :] = cot_own[...]
     for core in range(2):
         for dest in range(4):
             column = y_at ^ c_at ^ core
@@ -195,12 +227,8 @@
 
 
 def attend_body(tokens, hd, repeat, coords, cuts, hvec, *refs):
-    pieces, own, other = refs[:4], refs[4:8], refs[8:12]
-    if repeat == 1:
-        pieces = refs[:4]
-        own, other, refs = refs[:4], refs[4:8], refs[8:]
-    else:
-        refs = refs[12:]
+    pieces = refs[:4]
+    own, other, refs = (pieces, *refs[4:5], refs[5:]) if repeat == 1 else (refs[4:8], refs[8], refs[9:])
     out, lse, attended, keys, keys_t, queries, scores, bias, padded, peaks, totals, mixes = refs
     x_at, c_at, z_at, y_at, r_at = (coords[at] for at in range(5))
     block = 4 * tokens
@@ -215,9 +243,10 @@
                 keys[pl.ds(pl.multiple_of(base + c_at * tokens, tokens), tokens), :] = own[dest][
                     source, :
                 ]
+                start = (dest * repeat + rep) * block + at * tokens
                 keys[pl.ds(pl.multiple_of(base + (1 - c_at) * tokens, tokens), tokens), :] = other[
-                    dest
-                ][source, :]
+                    start : start + tokens, :
+                ]
             start = block + at * hd
             queries[place, :, pl.ds(pl.multiple_of(x_from * tokens, tokens), tokens)] = pieces[
                 dest
@@ -435,17 +464,16 @@
 
 
 def output_body(hd, coords, *refs):
-    arrived, own_in, gain, parts, middle_out, normed_out, weights, features = refs
+    arrived, own_in, gain, here, other, middle_out, normed_out, weights, features = refs
     x_at, c_at, z_at, y_at = coords[0], coords[1], coords[2], coords[3]
     half, tokens = hd // 2, arrived.shape[1]
-    for z_of in range(4):
-        for c_of in range(2):
-            for dest in range(4):
-                head = ((x_at ^ (dest >> 1)) * 2 + c_of) * 4 + z_of
+    for core, source in enumerate((here, other)):
+        for dest in range(4):
+            for near in range(4):
+                head = ((x_at ^ (dest >> 1)) * 2 + (c_at ^ core)) * 4 + (z_at ^ near)
                 start = pl.multiple_of(head * hd + (y_at ^ (dest & 1)) * half, half)
-                weights[pl.ds(start, half), :] = parts[
-                    z_of * 2 + c_of, dest * half : (dest + 1) * half, :
-                ]
+                first = (dest * 4 + near) * half
+                weights[pl.ds(start, half), :] = source[first : first + half, :]
     for dest in range(4):
         for core in range(2):
             for near in range(4):
@@ -498,23 +526,36 @@
     reach = (bucket_table.shape[0] - 1) // 2
     assert reach == tokens and lax.axis_size("x") == lax.axis_size("c") == 2
 
-    hidden_in = inputs[0].astype(F32)
     cot_own = cotangent[0]
-    scale_first = norm_scale(hidden_in)
-    normed = (hidden_in * scale_first * gain_attention).astype(BF16)
-    normed_parts = from_group(normed, "z")
-
-    joined = jnp.concatenate([query_weight, key_weight, value_weight, output_weight], axis=1)
+    out_rows = output_weight
+    if repeat > 1:
+        out_rows = lax.all_gather(out_rows, "r", axis=0, tiled=True)
+    message, joined, units = kernel_call(
+        pack_body,
+        [
+            shape((tokens + hd // 2, width), BF16),
+            shape((query_weight.shape[0], 3 * width), BF16),
+            shape((gate_weight.shape[0], 3 * width), BF16),
+        ],
+        [
+            inputs[0],
+            gain_attention.reshape(1, width),
+            out_rows,
+            query_weight,
+            key_weight,
+            value_weight,
+            gate_weight,
+            up_weight,
+            down_weight,
+        ],
+        scalars=0,
+        micros=2,
+    )
+    messages = from_group(message, "z")
     if repeat > 1:
         joined = lax.all_gather(joined, "r", axis=0, tiled=True)
     head_rows = from_group(joined, SQUARE)
-    other_rows = swap(jnp.concatenate([part[:, : 3 * width] for part in head_rows]), "c", 1)
-    out_rows = jnp.concatenate([part[:, 3 * width :] for part in head_rows])
-    units = jnp.concatenate([gate_weight, up_weight, down_weight], axis=1)
-    unit_rows = lax.all_gather(units, UNITS_GROUP, axis=0, tiled=True)
-    gate_piece, up_piece, down_piece = (
-        unit_rows[:, at * width : (at + 1) * width] for at in range(3)
-    )
+    other_rows = swap(jnp.concatenate(head_rows, axis=0), "c", 1)
 
     windows = segment_ids.reshape(-1, 2 * tokens)
     cuts = jnp.sum((windows < windows[:, -1:]).astype(jnp.int32), axis=1)
@@ -538,28 +579,36 @@
     diag = jnp.dot(onehot, bias_col, precision=HIGHEST) - jnp.sum(far_onehot * bias_col)
     hvec = jnp.pad(diag.reshape(3, 2 * reach), ((0, 5), (0, 0)))
 
-    normed_parts, hvec, cuts, coords, out_rows = lax.optimization_barrier(
-        (normed_parts, hvec, cuts, coords, out_rows)
-    )
+    messages, hvec, cuts, coords, units = lax.optimization_barrier(
+        (messages, hvec, cuts, coords, units)
+    )
+    unit_rows = lax.all_gather(units, UNITS_GROUP, axis=0, tiled=True)
+    gate_piece, up_piece, down_piece = (
+        unit_rows[:, at * width : (at + 1) * width] for at in range(3)
+    )
+
     made = kernel_call(
         functools.partial(qkv_body, hd),
         [shape((block + 4 * hd, 2 * hd), BF16)] * 4
-        + [shape((block, width), BF16), shape((12 * hd, width), BF16)],
-        [coords, *normed_parts, *head_rows, other_rows],
-    )
-    pieces, (normed_all, group_weights) = made[:4], made[4:]
+        + [
+            shape((block, width), BF16),
+            shape((12 * hd, width), BF16),
+            shape((tokens + 2 * hd, width), BF16),
+        ],
+        [coords, *messages, *head_rows, other_rows, cot_own, anchor(messages, 30)],
+    )
+    pieces, (normed_all, group_weights, sent) = made[:4], made[4:]
     pieces = to_group(pieces, SQUARE)
 
-    out_all = lax.all_gather(out_rows, ("z", "c"), axis=0, tiled=False)
     own = [piece[:block] for piece in pieces]
     other = swap(jnp.concatenate(own, axis=0), "c", 1)
-    other = [other[at * block : (at + 1) * block] for at in range(4)]
     if repeat == 1:
-        arrays = [*pieces, *other]
+        arrays = [*pieces, other]
     else:
         own = [lax.all_gather(part, "r", axis=0, tiled=True) for part in own]
-        other = [lax.all_gather(part, "r", axis=0, tiled=True) for part in other]
-        arrays = [*pieces, *own, *other]
+        other = other.reshape(4, block, 2 * hd)
+        other = [lax.all_gather(other[at], "r", axis=0, tiled=True) for at in range(4)]
+        arrays = [*pieces, *own, jnp.concatenate(other, axis=0)]
     places = 8
     out_t, lse, attended, keys, keys_t, queries = kernel_call(
         functools.partial(attend_body, tokens, hd, repeat),
@@ -583,10 +632,13 @@
         scalars=2,
         micros=20,
     )
-    cot_sent, _ = lax.optimization_barrier((cot_own, other))
-    cot_parts, out_t = lax.optimization_barrier((from_group(cot_sent, SQUARE), out_t))
-    cot_all = jnp.concatenate(cot_parts, axis=0)
+    sent, _ = lax.optimization_barrier((sent, pieces))
+    parts = from_group(sent, SQUARE)
     arrived = lax.all_to_all(out_t, ("x", "y", "z"), split_axis=0, concat_axis=0, tiled=True)
+    parts, arrived = lax.optimization_barrier((parts, arrived))
+    cot_all = jnp.concatenate([part[:tokens] for part in parts], axis=0)
+    out_here = jnp.concatenate([part[tokens:] for part in parts], axis=0)
+    out_other = swap(out_here, "c", 1)
 
     middle, normed_mid, out_full, features = kernel_call(
         functools.partial(output_body, hd),
@@ -601,7 +653,8 @@
             arrived.reshape(width, tokens),
             inputs[0],
             gain_feedforward.reshape(1, width),
-            out_all,
+            out_here,
+            out_other,
         ],
     )
     scale_second = norm_scale(middle)
@@ -703,6 +756,7 @@
         ],
         [coords, *grad_pieces, normed_all, group_weights, gain_attention.reshape(1, width)],
         [pltpu.VMEM((block, 8 * hd), BF16), pltpu.VMEM((block, 4 * hd), BF16)],
+        mebi=16,
     )
     normed_grads, gain_first_rows, pairs_t, queries_t = made
     normed_grads = lax.all_to_all(normed_grads, "z", split_axis=0, concat_axis=0, tiled=True)
@@ -753,6 +807,7 @@
         [normed_grads, inputs[0], grad_middle, gain_attention.reshape(1, width)],
         scalars=0,
         micros=100,
+        mebi=16,
     )
     unit_grads = grad_units.astype(F32)
     return (

time: 259 us -> 253 us (0.977)
  waiting for transfers between devices: 67.2 us -> 61 us
  starting transfers between devices: 55.3 us -> 59.9 us
  other arithmetic: 18.8 us -> 15.6 us
    all_to_all x1, starting transfers between devices: 6.76 us -> 13.5 us  [body(): lax.all_to_all(out_t, ('x', 'y', 'z'), split_axis=0, concat_axis=0, tiled...]
    all_to_all x1, waiting for transfers between devices: 17 us -> 13.2 us  [body(): lax.all_to_all(out_t, ('x', 'y', 'z'), split_axis=0, concat_axis=0, tiled...]
    unnamed x104 -> x90, local copies, waits for them, and re-layouts: 9.26 us -> 11.9 us
    ppermute x39 -> x40, waiting for transfers between devices: 44.6 us -> 42.3 us  [swap(): return lax.ppermute(value, axis, [(at, at ^ mask) for at in range(size)])]
    ppermute x39 -> x40, starting transfers between devices: 44 us -> 42.6 us  [swap(): return lax.ppermute(value, axis, [(at, at ^ mask) for at in range(size)])]
    pallas_call x7 -> x8, Pallas kernels: 49.4 us -> 48.8 us  [kernel_call(): pl.pallas_call(body, out_shape=out_shapes, in_specs=in_specs, out_specs=j...]
  transfers between devices with their start and end apart: 44 -> 44, of which waited for: 23 -> 21; matrix products, arithmetic and copies ran while one was open for 14% -> 13% of each run, Pallas kernels for 19% -> 19%
where the time goes in v1:
time: 253 us; the launch traced here: 251 us
  waiting for transfers between devices  61 us (24%)
  starting transfers between devices  59.9 us (24%)
  Pallas kernels  49.4 us (20%)
  local copies, waits for them, and re-layouts  21.8 us (9%)
  matrix products  16.6 us (7%)
  other arithmetic  15.6 us (6%)
  between operations  15 us (6%)
  blocking collectives  12.1 us (5%)
    pallas_call x8, Pallas kernels, kernel_call(): pl.pallas_call(body, out_shape=out_shapes, in_specs=in_specs, out_specs=j...  48.8 us
    ppermute x40, starting transfers between devices, swap(): return lax.ppermute(value, axis, [(at, at ^ mask) for at in range(size)])  42.6 us
    ppermute x40, waiting for transfers between devices, swap(): return lax.ppermute(value, axis, [(at, at ^ mask) for at in range(size)])  42.3 us
    all_to_all x1, starting transfers between devices, body(): lax.all_to_all(out_t, ('x', 'y', 'z'), split_axis=0, concat_axis=0, tiled...  13.5 us
    all_to_all x1, waiting for transfers between devices, body(): lax.all_to_all(out_t, ('x', 'y', 'z'), split_axis=0, concat_axis=0, tiled...  13.2 us
    all_to_all x1, blocking collectives, body(): lax.all_to_all(grad_attended.reshape(16, hd, tokens), ('x', 'y', 'z'), sp...  12.1 us
    unnamed x90, local copies, waits for them, and re-layouts  11.9 us
    dot_general x4, matrix products, nt(): lax.dot_general(left, right, (((1,), (1,)), ((), ())), preferred_element_...  6.06 us
  transfers between devices with their start and end apart: 44, of which 21 were waited for; matrix products, arithmetic and copies ran while one was open for 13% of the time, Pallas kernels for 19%

profile of v1, /device:TPU:0, one launch (start us, length us, event | category | flops | bytes accessed | tf_op | source)
XLA Modules:
  0.0 251.5 jit_solution(11213621083220651418)
XLA Ops:
  7.2 2.3 shard_map.229
  9.6 3.0 %collective-permute-start = (bf16[160,1024]{1,0:T(8,128)(2,1)}, bf16[160,1024]{1,0:T(8,128)(2,1)S(1)}, u32[]{:S(2)}, u32[]{:S(2)}) collective-permute-start(bf16[160,1024]{1,0:T(8,128)(2,1)} %get-tuple-element.95.refs_0_), channel_id=1, source_target_pairs={{0,2},{2,0},{4,6},{6,4},{1,3},{3,1},{5,7},{7,5},{8,10},{10,8},{12,... | collective-permute-start | bytes 983048 | tf_op jit(solution)/shard_map/ppermute | solution.py:45
  12.6 2.6 %collective-permute-start.1 = (bf16[160,1024]{1,0:T(8,128)(2,1)}, bf16[160,1024]{1,0:T(8,128)(2,1)S(1)}, u32[]{:S(2)}, u32[]{:S(2)}) collective-permute-start(bf16[160,1024]{1,0:T(8,128)(2,1)} %get-tuple-element.95.refs_0_), channel_id=1, source_target_pairs={{0,4},{2,6},{4,0},{6,2},{1,5},{3,7},{5,1},{7,3},{8,12},{10,14},{12... | collective-permute-start | bytes 983048 | tf_op jit(solution)/shard_map/ppermute | solution.py:45
  28.1 9.0 %collective-permute-done.1.refs_2_ = bf16[160,1024]{1,0:T(8,128)(2,1)S(1)} collective-permute-done((bf16[160,1024]{1,0:T(8,128)(2,1)}, bf16[160,1024]{1,0:T(8,128)(2,1)S(1)}, u32[]{:S(2)}, u32[]{:S(2)}) %collective-permute-start.1) | collective-permute-done | bytes 327712 | tf_op jit(solution)/shard_map/ppermute | solution.py:45
  39.4 4.4 %shard_map.231 = (bf16[768,128]{1,0:T(8,128)(2,1)}, bf16[768,128]{1,0:T(8,128)(2,1)}, bf16[768,128]{1,0:T(8,128)(2,1)}, bf16[768,128]{1,0:T(8,128)(2,1)}, bf16[5...) custom-call(s32[5]{0:T(128)} %stack.35.coords, ...), custom_call_target="tpu_custom_call" | custom-call | flops 4600000000 | bytes 1048576 | tf_op jit(solution)/shard_map/pallas_call | solution.py:79
  43.8 2.5 %collective-permute-start.9 = (bf16[768,128]{1,0:T(8,128)(2,1)}, bf16[768,128]{1,0:T(8,128)(2,1)S(1)}, u32[]{:S(2)}, u32[]{:S(2)}) collective-permute-start(bf16[768,128]{1,0:T(8,128)(2,1)} %get-tuple-element.104), channel_id=1, source_target_pairs={{0,17},{1,16},{16,1},{17,0},{2,19},{3,18},{18,3},{19,2},{4,21},{5,... | collective-permute-start | bytes 589832 | tf_op jit(solution)/shard_map/ppermute | solution.py:45
  48.2 2.8 %collective-permute-done.9.refs_3_ = bf16[768,128]{1,0:T(8,128)(2,1)S(1)} collective-permute-done((bf16[768,128]{1,0:T(8,128)(2,1)}, bf16[768,128]{1,0:T(8,128)(2,1)S(1)}, u32[]{:S(2)}, u32[]{:S(2)}) %collective-permute-start.9) | collective-permute-done | bytes 196640 | tf_op jit(solution)/shard_map/ppermute | solution.py:45
  51.1 2.1 collective-permute-done.8.refs_2_
  57.8 13.0 %shard_map.232 = (bf16[16,64,128]{2,1,0:T(8,128)(2,1)}, f32[8,8,256]{2,1,0:T(8,128)}, f32[8,64,256]{2,1,0:T(8,128)}, bf16[4096,128]{1,0:T(8,128)(2,1)}, bf16[8,1...) custom-call(s32[5]{0:T(128)} %stack.35.coords, s32[16]{0:T(128)} %convert_reduce_fusion.cuts, f32[8,256]{1,0:T(8,128)} %pad.12.hvec, ...), custom_call_target="tpu_custom_call" | custom-call | flops 23000000512 | bytes 1048576 | tf_op jit(solution)/shard_map/pallas_call | solution.py:79
  70.8 13.5 %all-to-all-start = ((bf16[16,64,128]{2,1,0:T(8,128)(2,1)}), bf16[16,64,128]{2,1,0:T(8,128)(2,1)S(1)}, u32[]{:S(2)}, u32[]{:S(2)}) async-start(bf16[16,64,128]{2,1,0:T(8,128)(2,1)} %get-tuple-element.108), calls=%async_computation | async-start | bytes 524288 | tf_op jit(solution)/shard_map/all_to_all | solution.py:637
  84.6 13.2 %all-to-all-done = bf16[16,64,128]{2,1,0:T(8,128)(2,1)S(1)} async-done(((bf16[16,64,128]{2,1,0:T(8,128)(2,1)}), bf16[16,64,128]{2,1,0:T(8,128)(2,1)S(1)}, u32[]{:S(2)}, u32[]{:S(2)}) %all-to-all-start) | async-done | bytes 262176 | tf_op jit(solution)/shard_map/all_to_all | solution.py:637
  98.6 2.6 %collective-permute-done.14.refs_4_ = bf16[512,1024]{1,0:T(8,128)(2,1)S(1)} collective-permute-done((bf16[512,1024]{1,0:T(8,128)(2,1)S(1)}, bf16[512,1024]{1,0:T(8,128)(2,1)S(1)}, u32[]{:S(2)}, u32[]{:S(2)}) %collective-permute-start.14) | collective-permute-done | bytes 1048608 | tf_op jit(solution)/shard_map/ppermute | solution.py:45
  102.2 3.9 %shard_map.233 = (f32[128,1024]{1,0:T(8,128)}, bf16[128,1024]{1,0:T(8,128)(2,1)}, bf16[1024,1024]{1,0:T(8,128)(2,1)}, bf16[4,32,1024]{2,1,0:T(8,128)(2,1)}) custom-call(s32[5]{0:T(128)} %stack.35.coords, bf16[1024,128]{1,0:T(8,128)(2,1)} %bitcast.111, bf16[128,1024]{1,0:T(8,128)(2,1)} %bitcast.98, f32[1,1024]{1,0:T(1,128)} %bitcast.117, ...), custom_call_target="tpu_custom_call" | custom-call | flops 4600000000 | bytes 1048576 | tf_op jit(solution)/shard_map/pallas_call | solution.py:79
  107.3 2.4 collective-permute-start.17
  111.8 2.9 %collective-permute-done.15 = bf16[128,1024]{1,0:T(8,128)(2,1)S(1)} collective-permute-done((bf16[128,1024]{1,0:T(8,128)(2,1)}, bf16[128,1024]{1,0:T(8,128)(2,1)S(1)}, u32[]{:S(2)}, u32[]{:S(2)}) %collective-permute-start.15) | collective-permute-done | bytes 262176 | tf_op jit(solution)/shard_map/ppermute | solution.py:45
  115.6 6.0 %collective-permute-done.17 = bf16[128,1024]{1,0:T(8,128)(2,1)S(1)} collective-permute-done((bf16[128,1024]{1,0:T(8,128)(2,1)}, bf16[128,1024]{1,0:T(8,128)(2,1)S(1)}, u32[]{:S(2)}, u32[]{:S(2)}) %collective-permute-start.17) | collective-permute-done | bytes 262176 | tf_op jit(solution)/shard_map/ppermute | solution.py:45
  121.6 2.5 fusion.9
  132.9 2.4 collective-permute-start.20
  136.2 2.2 pad_maximum_fusion
  138.5 2.6 %convolution_convert_fusion.3 = bf16[512,1024]{1,0:T(8,128)(2,1)S(1)} fusion(bf16[512,704]{0,1:T(8,128)(2,1)} %copy-done.34, bf16[704,3072]{1,0:T(8,128)(2,1)} %all-gather.2.cloned.1.call-done), kind=kOutput, calls=%fused_computation.8 | convolution fusion | flops 738721792 | bytes 3211264 | tf_op jit(solution)/shard_map/dot_general | solution.py:36
  141.3 4.5 %collective-permute-done.20 = bf16[128,1024]{1,0:T(8,128)(2,1)S(1)} collective-permute-done((bf16[128,1024]{1,0:T(8,128)(2,1)S(1)}, bf16[128,1024]{1,0:T(8,128)(2,1)S(1)}, u32[]{:S(2)}, u32[]{:S(2)}) %collective-permute-start.20) | collective-permute-done | bytes 262176 | tf_op jit(solution)/shard_map/ppermute | solution.py:45
  148.4 12.1 %all_to_all.15.refs_0_ = bf16[16,64,128]{2,1,0:T(8,128)(2,1)} all-to-all(bf16[16,64,128]{2,1,0:T(8,128)(2,1)S(1)} %bitcast.103), channel_id=1, replica_groups=mesh['x'=2,'c'=2,'z'=4,'y'=2,'r'=1] {'x','y','z'}, dimensions={0} | all-to-all | bytes 524288 | tf_op jit(solution)/shard_map/all_to_all | solution.py:686
  164.3 2.2 collective-permute-start.23
  166.5 17.6 %shard_map.234 = (f32[2048,128]{1,0:T(8,128)}, bf16[2048,128]{1,0:T(8,128)(2,1)}, bf16[16,64,128]{2,1,0:T(8,128)(2,1)}, f32[8,256]{1,0:T(8,128)}, f32[8,256]{1,0:T(8,128)}) custom-call(s32[5]{0:T(128)} %stack.35.coords, s32[16]{0:T(128)} %convert_reduce_fusion.cuts, f32[8,256]{1,0:T(8,128)} %pad.12.hvec, bf16[16,64,128]{2,1,0:T(8,128)(2,1)} %all_to_all.15.refs_0_, ...), custom_call_target="tpu_custom_call" | custom-call | flops 23000000512 | bytes 1048576 | tf_op jit(solution)/shard_map/pallas_call | solution.py:79
  185.1 3.9 %collective-permute-done.23 = bf16[288,1024]{1,0:T(8,128)(2,1)} collective-permute-done((bf16[288,1024]{1,0:T(8,128)(2,1)}, bf16[288,1024]{1,0:T(8,128)(2,1)}, u32[]{:S(2)}, u32[]{:S(2)}) %collective-permute-start.23) | collective-permute-done | bytes 589856 | tf_op jit(solution)/shard_map/ppermute | solution.py:45
  191.9 2.2 collective-permute-start.27
  200.7 2.6 %shard_map.235 = (bf16[4,128,1024]{2,1,0:T(8,128)(2,1)}, f32[8,1024]{1,0:T(8,128)S(1)}, bf16[512,512]{1,0:T(8,128)(2,1)S(1)}, bf16[256,512]{1,0:T(8,128)(2,1)S(1)}) custom-call(s32[5]{0:T(128)S(1)} %copy-done, bf16[768,128]{1,0:T(8,128)(2,1)S(1)} %pad_maximum_fusion.10.refs_0_, bf16[768,128]{1,0:T(8,128)(2,1)S(1)} %collective-permute-done.25.refs_1_, ...), custom_call_target="tpu_custom_call" | custom-call | flops 4600000000 | bytes 1048576 | tf_op jit(solution)/shard_map/pallas_call | solution.py:79
  204.9 3.5 %all-to-all-start.2 = ((bf16[4,128,1024]{2,1,0:T(8,128)(2,1)}), bf16[4,128,1024]{2,1,0:T(8,128)(2,1)S(1)}, u32[]{:S(2)}, u32[]{:S(2)}) async-start(bf16[4,128,1024]{2,1,0:T(8,128)(2,1)} %get-tuple-element.150), calls=%async_computation.2 | async-start | bytes 2097152 | tf_op jit(solution)/shard_map/all_to_all | solution.py:762
  208.4 3.8 %shard_map.236 = (bf16[4,32,3072]{2,1,0:T(8,128)(2,1)}, bf16[4,32,3072]{2,1,0:T(8,128)(2,1)}) custom-call(s32[5]{0:T(128)} %stack.35.coords, bf16[512,512]{1,0:T(8,128)(2,1)} %copy-done.5, bf16[256,512]{1,0:T(8,128)(2,1)} %copy-done.6, bf16[512,1024]{1,0:T(8,128)(2,1)} %get-tuple-element.148.refs_4_.rows_all), custom_call_target="tpu_custom_call" | custom-call | flops 4600000000 | bytes 1048576 | tf_op jit(solution)/shard_map/pallas_call | solution.py:79
  225.6 5.5 %all-to-all-done.2.refs_0_ = bf16[4,128,1024]{2,1,0:T(8,128)(2,1)S(1)} async-done(((bf16[4,128,1024]{2,1,0:T(8,128)(2,1)}), bf16[4,128,1024]{2,1,0:T(8,128)(2,1)S(1)}, u32[]{:S(2)}, u32[]{:S(2)}) %all-to-all-start.2) | async-done | bytes 1048608 | tf_op jit(solution)/shard_map/all_to_all | solution.py:762
  233.2 3.8 %collective-permute-start.39 = (bf16[40,1024]{1,0:T(8,128)(2,1)S(1)}, bf16[40,1024]{1,0:T(8,128)(2,1)S(1)}, u32[]{:S(2)}, u32[]{:S(2)}) collective-permute-start(bf16[40,1024]{1,0:T(8,128)(2,1)S(1)} %get-tuple-element.244), channel_id=1, source_target_pairs={{0,6},{2,4},{4,2},{6,0},{1,7},{3,5},{5,3},{7,1},{8,14},{10,12},{12... | collective-permute-start | bytes 245768 | tf_op jit(solution)/shard_map/ppermute | solution.py:45
  240.2 2.3 collective-permute-done.38
  (251 shorter events, 76.5 us)
Async XLA Ops:
  7.2 114.4 %all-gather.2.cloned.1.call-start = ((), (), s32[]{:S(2)}) async-start(), calls=%async_computation.4 | async-start | bytes 4866048 | tf_op jit(solution)/shard_map/all_gather | solution.py:585
  9.6 18.5 %collective-permute-start = (bf16[160,1024]{1,0:T(8,128)(2,1)}, bf16[160,1024]{1,0:T(8,128)(2,1)S(1)}, u32[]{:S(2)}, u32[]{:S(2)}) collective-permute-start(bf16[160,1024]{1,0:T(8,128)(2,1)} %get-tuple-element.95.refs_0_), channel_id=1, source_target_pairs={{0,2},{2,0},{4,6},{6,4},{1,3},{3,1},{5,7},{7,5},{8,10},{10,8},{12,... | collective-permute-start | bytes 983048 | tf_op jit(solution)/shard_map/ppermute | solution.py:45
  12.6 24.5 %collective-permute-start.1 = (bf16[160,1024]{1,0:T(8,128)(2,1)}, bf16[160,1024]{1,0:T(8,128)(2,1)S(1)}, u32[]{:S(2)}, u32[]{:S(2)}) collective-permute-start(bf16[160,1024]{1,0:T(8,128)(2,1)} %get-tuple-element.95.refs_0_), channel_id=1, source_target_pairs={{0,4},{2,6},{4,0},{6,2},{1,5},{3,7},{5,1},{7,3},{8,12},{10,14},{12... | collective-permute-start | bytes 983048 | tf_op jit(solution)/shard_map/ppermute | solution.py:45
  15.2 11.6 %collective-permute-start.3 = (bf16[32,3072]{1,0:T(8,128)(2,1)}, bf16[32,3072]{1,0:T(8,128)(2,1)S(1)}, u32[]{:S(2)}, u32[]{:S(2)}) collective-permute-start(bf16[32,3072]{1,0:T(8,128)(2,1)} %get-tuple-element.99.refs_4_), channel_id=1, source_target_pairs={{0,1},{1,0},{16,17},{17,16},{2,3},{3,2},{18,19},{19,18},{4,5},{5,4... | collective-permute-start | bytes 589832 | tf_op jit(solution)/shard_map/ppermute | solution.py:45
  16.7 10.0 %collective-permute-start.4 = (bf16[32,3072]{1,0:T(8,128)(2,1)}, bf16[32,3072]{1,0:T(8,128)(2,1)S(1)}, u32[]{:S(2)}, u32[]{:S(2)}) collective-permute-start(bf16[32,3072]{1,0:T(8,128)(2,1)} %get-tuple-element.99.refs_4_), channel_id=1, source_target_pairs={{0,16},{1,17},{16,0},{17,1},{2,18},{3,19},{18,2},{19,3},{4,20},{5,... | collective-permute-start | bytes 589832 | tf_op jit(solution)/shard_map/ppermute | solution.py:45
  18.2 8.7 %collective-permute-start.5 = (bf16[32,3072]{1,0:T(8,128)(2,1)}, bf16[32,3072]{1,0:T(8,128)(2,1)S(1)}, u32[]{:S(2)}, u32[]{:S(2)}) collective-permute-start(bf16[32,3072]{1,0:T(8,128)(2,1)} %get-tuple-element.99.refs_4_), channel_id=1, source_target_pairs={{0,17},{1,16},{16,1},{17,0},{2,19},{3,18},{18,3},{19,2},{4,21},{5,... | collective-permute-start | bytes 589832 | tf_op jit(solution)/shard_map/ppermute | solution.py:45
  26.8 10.3 %collective-permute-start.2 = (bf16[160,1024]{1,0:T(8,128)(2,1)}, bf16[160,1024]{1,0:T(8,128)(2,1)S(1)}, u32[]{:S(2)}, u32[]{:S(2)}) collective-permute-start(bf16[160,1024]{1,0:T(8,128)(2,1)} %get-tuple-element.95.refs_0_), channel_id=1, source_target_pairs={{0,6},{2,4},{4,2},{6,0},{1,7},{3,5},{5,3},{7,1},{8,14},{10,12},{12... | collective-permute-start | bytes 983048 | tf_op jit(solution)/shard_map/ppermute | solution.py:45
  28.0 10.5 %collective-permute-start.6 = (bf16[128,3072]{1,0:T(8,128)(2,1)S(1)}, bf16[128,3072]{1,0:T(8,128)(2,1)S(1)}, u32[]{:S(2)}, u32[]{:S(2)}) collective-permute-start(bf16[128,3072]{1,0:T(8,128)(2,1)S(1)} %pad_maximum_fusion.7), channel_id=1, source_target_pairs={{0,8},{8,0},{1,9},{9,1},{2,10},{10,2},{3,11},{11,3},{4,12},{12,4},... | collective-permute-start | bytes 2359304 | tf_op jit(solution)/shard_map/ppermute | solution.py:45
  43.8 7.3 %collective-permute-start.9 = (bf16[768,128]{1,0:T(8,128)(2,1)}, bf16[768,128]{1,0:T(8,128)(2,1)S(1)}, u32[]{:S(2)}, u32[]{:S(2)}) collective-permute-start(bf16[768,128]{1,0:T(8,128)(2,1)} %get-tuple-element.104), channel_id=1, source_target_pairs={{0,17},{1,16},{16,1},{17,0},{2,19},{3,18},{18,3},{19,2},{4,21},{5,... | collective-permute-start | bytes 589832 | tf_op jit(solution)/shard_map/ppermute | solution.py:45
  53.4 31.2 %collective-permute-start.10 = (bf16[256,1024]{1,0:T(8,128)(2,1)S(1)}, bf16[256,1024]{1,0:T(8,128)(2,1)S(1)}, u32[]{:S(2)}, u32[]{:S(2)}) collective-permute-start(bf16[256,1024]{1,0:T(8,128)(2,1)S(1)} %copy-done.12), channel_id=1, source_target_pairs={{0,1},{1,0},{16,17},{17,16},{2,3},{3,2},{18,19},{19,18},{4,5},{5,4... | collective-permute-start | bytes 1572872 | tf_op jit(solution)/shard_map/ppermute | solution.py:45
  54.9 29.7 %collective-permute-start.11 = (bf16[256,1024]{1,0:T(8,128)(2,1)S(1)}, bf16[256,1024]{1,0:T(8,128)(2,1)S(1)}, u32[]{:S(2)}, u32[]{:S(2)}) collective-permute-start(bf16[256,1024]{1,0:T(8,128)(2,1)S(1)} %copy-done.12), channel_id=1, source_target_pairs={{0,16},{1,17},{16,0},{17,1},{2,18},{3,19},{18,2},{19,3},{4,20},{5,... | collective-permute-start | bytes 1572872 | tf_op jit(solution)/shard_map/ppermute | solution.py:45
  56.4 28.2 %collective-permute-start.12 = (bf16[256,1024]{1,0:T(8,128)(2,1)S(1)}, bf16[256,1024]{1,0:T(8,128)(2,1)S(1)}, u32[]{:S(2)}, u32[]{:S(2)}) collective-permute-start(bf16[256,1024]{1,0:T(8,128)(2,1)S(1)} %copy-done.12), channel_id=1, source_target_pairs={{0,17},{1,16},{16,1},{17,0},{2,19},{3,18},{18,3},{19,2},{4,21},{5,... | collective-permute-start | bytes 1572872 | tf_op jit(solution)/shard_map/ppermute | solution.py:45
  70.8 27.0 %all-to-all-start = ((bf16[16,64,128]{2,1,0:T(8,128)(2,1)}), bf16[16,64,128]{2,1,0:T(8,128)(2,1)S(1)}, u32[]{:S(2)}, u32[]{:S(2)}) async-start(bf16[16,64,128]{2,1,0:T(8,128)(2,1)} %get-tuple-element.108), calls=%async_computation | async-start | bytes 524288 | tf_op jit(solution)/shard_map/all_to_all | solution.py:637
  84.3 128.0 %reduce-scatter.2.cloned.1.call-start = ((), (), s32[]{:S(2)}) async-start(), calls=%async_computation.5 | async-start | bytes 4866048 | tf_op jit(solution)/shard_map/reduce_scatter | solution.py:696
  106.2 8.6 %collective-permute-start.15 = (bf16[128,1024]{1,0:T(8,128)(2,1)}, bf16[128,1024]{1,0:T(8,128)(2,1)S(1)}, u32[]{:S(2)}, u32[]{:S(2)}) collective-permute-start(bf16[128,1024]{1,0:T(8,128)(2,1)} %get-tuple-element.116), channel_id=1, source_target_pairs={{0,1},{1,0},{16,17},{17,16},{2,3},{3,2},{18,19},{19,18},{4,5},{5,4... | collective-permute-start | bytes 786440 | tf_op jit(solution)/shard_map/ppermute | solution.py:45
  106.2 9.4 %collective-permute-start.16 = (bf16[128,1024]{1,0:T(8,128)(2,1)}, bf16[128,1024]{1,0:T(8,128)(2,1)S(1)}, u32[]{:S(2)}, u32[]{:S(2)}) collective-permute-start(bf16[128,1024]{1,0:T(8,128)(2,1)} %get-tuple-element.116), channel_id=1, source_target_pairs={{0,16},{1,17},{16,0},{17,1},{2,18},{3,19},{18,2},{19,3},{4,20},{5,... | collective-permute-start | bytes 786440 | tf_op jit(solution)/shard_map/ppermute | solution.py:45
  107.3 14.2 %collective-permute-start.17 = (bf16[128,1024]{1,0:T(8,128)(2,1)}, bf16[128,1024]{1,0:T(8,128)(2,1)S(1)}, u32[]{:S(2)}, u32[]{:S(2)}) collective-permute-start(bf16[128,1024]{1,0:T(8,128)(2,1)} %get-tuple-element.116), channel_id=1, source_target_pairs={{0,17},{1,16},{16,1},{17,0},{2,19},{3,18},{18,3},{19,2},{4,21},{5,... | collective-permute-start | bytes 786440 | tf_op jit(solution)/shard_map/ppermute | solution.py:45
  131.8 9.3 %collective-permute-start.18 = (bf16[128,1024]{1,0:T(8,128)(2,1)}, bf16[128,1024]{1,0:T(8,128)(2,1)S(1)}, u32[]{:S(2)}, u32[]{:S(2)}) collective-permute-start(bf16[128,1024]{1,0:T(8,128)(2,1)} %get-tuple-element.197), channel_id=1, source_target_pairs={{0,1},{1,0},{16,17},{17,16},{2,3},{3,2},{18,19},{19,18},{4,5},{5,4... | collective-permute-start | bytes 786440 | tf_op jit(solution)/shard_map/ppermute | solution.py:45
  132.1 9.2 %collective-permute-start.19 = (bf16[128,1024]{1,0:T(8,128)(2,1)S(1)}, bf16[128,1024]{1,0:T(8,128)(2,1)S(1)}, u32[]{:S(2)}, u32[]{:S(2)}) collective-permute-start(bf16[128,1024]{1,0:T(8,128)(2,1)S(1)} %get-tuple-element.196), channel_id=1, source_target_pairs={{0,16},{1,17},{16,0},{17,1},{2,18},{3,19},{18,2},{19,3},{4,20},{5,... | collective-permute-start | bytes 786440 | tf_op jit(solution)/shard_map/ppermute | solution.py:45
  132.9 12.9 %collective-permute-start.20 = (bf16[128,1024]{1,0:T(8,128)(2,1)S(1)}, bf16[128,1024]{1,0:T(8,128)(2,1)S(1)}, u32[]{:S(2)}, u32[]{:S(2)}) collective-permute-start(bf16[128,1024]{1,0:T(8,128)(2,1)S(1)} %get-tuple-element.195), channel_id=1, source_target_pairs={{0,17},{1,16},{16,1},{17,0},{2,19},{3,18},{18,3},{19,2},{4,21},{5,... | collective-permute-start | bytes 786440 | tf_op jit(solution)/shard_map/ppermute | solution.py:45
  163.0 22.1 %collective-permute-start.21 = (bf16[288,1024]{1,0:T(8,128)(2,1)}, bf16[288,1024]{1,0:T(8,128)(2,1)S(1)}, u32[]{:S(2)}, u32[]{:S(2)}) collective-permute-start(bf16[288,1024]{1,0:T(8,128)(2,1)} %get-tuple-element.232), channel_id=1, source_target_pairs={{0,1},{1,0},{16,17},{17,16},{2,3},{3,2},{18,19},{19,18},{4,5},{5,4... | collective-permute-start | bytes 1769480 | tf_op jit(solution)/shard_map/ppermute | solution.py:45
  163.4 21.7 %collective-permute-start.22 = (bf16[288,1024]{1,0:T(8,128)(2,1)}, bf16[288,1024]{1,0:T(8,128)(2,1)S(1)}, u32[]{:S(2)}, u32[]{:S(2)}) collective-permute-start(bf16[288,1024]{1,0:T(8,128)(2,1)} %get-tuple-element.233), channel_id=1, source_target_pairs={{0,16},{1,17},{16,0},{17,1},{2,18},{3,19},{18,2},{19,3},{4,20},{5,... | collective-permute-start | bytes 1769480 | tf_op jit(solution)/shard_map/ppermute | solution.py:45
  164.3 24.7 %collective-permute-start.23 = (bf16[288,1024]{1,0:T(8,128)(2,1)}, bf16[288,1024]{1,0:T(8,128)(2,1)}, u32[]{:S(2)}, u32[]{:S(2)}) collective-permute-start(bf16[288,1024]{1,0:T(8,128)(2,1)} %get-tuple-element.231), channel_id=1, source_target_pairs={{0,17},{1,16},{16,1},{17,0},{2,19},{3,18},{18,3},{19,2},{4,21},{5,... | collective-permute-start | bytes 1769480 | tf_op jit(solution)/shard_map/ppermute | solution.py:45
  190.5 9.0 %collective-permute-start.25 = (bf16[768,128]{1,0:T(8,128)(2,1)S(1)}, bf16[768,128]{1,0:T(8,128)(2,1)S(1)}, u32[]{:S(2)}, u32[]{:S(2)}) collective-permute-start(bf16[768,128]{1,0:T(8,128)(2,1)S(1)} %pad_maximum_fusion.11), channel_id=1, source_target_pairs={{0,1},{1,0},{16,17},{17,16},{2,3},{3,2},{18,19},{19,18},{4,5},{5,4... | collective-permute-start | bytes 589832 | tf_op jit(solution)/shard_map/ppermute | solution.py:45
  190.9 8.5 %collective-permute-start.26 = (bf16[768,128]{1,0:T(8,128)(2,1)S(1)}, bf16[768,128]{1,0:T(8,128)(2,1)S(1)}, u32[]{:S(2)}, u32[]{:S(2)}) collective-permute-start(bf16[768,128]{1,0:T(8,128)(2,1)S(1)} %pad_maximum_fusion.12), channel_id=1, source_target_pairs={{0,16},{1,17},{16,0},{17,1},{2,18},{3,19},{18,2},{19,3},{4,20},{5,... | collective-permute-start | bytes 589832 | tf_op jit(solution)/shard_map/ppermute | solution.py:45
  191.9 8.3 %collective-permute-start.27 = (bf16[768,128]{1,0:T(8,128)(2,1)S(1)}, bf16[768,128]{1,0:T(8,128)(2,1)S(1)}, u32[]{:S(2)}, u32[]{:S(2)}) collective-permute-start(bf16[768,128]{1,0:T(8,128)(2,1)S(1)} %pad_maximum_fusion.13), channel_id=1, source_target_pairs={{0,17},{1,16},{16,1},{17,0},{2,19},{3,18},{18,3},{19,2},{4,21},{5,... | collective-permute-start | bytes 589832 | tf_op jit(solution)/shard_map/ppermute | solution.py:45
  204.9 26.2 %all-to-all-start.2 = ((bf16[4,128,1024]{2,1,0:T(8,128)(2,1)}), bf16[4,128,1024]{2,1,0:T(8,128)(2,1)S(1)}, u32[]{:S(2)}, u32[]{:S(2)}) async-start(bf16[4,128,1024]{2,1,0:T(8,128)(2,1)} %get-tuple-element.150), calls=%async_computation.2 | async-start | bytes 2097152 | tf_op jit(solution)/shard_map/all_to_all | solution.py:762
  212.3 9.4 %collective-permute-start.28 = (bf16[4,32,3072]{2,1,0:T(8,128)(2,1)}, bf16[4,32,3072]{2,1,0:T(8,128)(2,1)S(1)}, u32[]{:S(2)}, u32[]{:S(2)}) collective-permute-start(bf16[4,32,3072]{2,1,0:T(8,128)(2,1)} %get-tuple-element.159), channel_id=1, source_target_pairs={{0,8},{8,0},{1,9},{9,1},{2,10},{10,2},{3,11},{11,3},{4,12},{12,4},... | collective-permute-start | bytes 2359304 | tf_op jit(solution)/shard_map/ppermute | solution.py:45
  215.4 10.2 %collective-permute-start.36 = (bf16[4,32,1024]{2,1,0:T(8,128)(2,1)S(1)}, bf16[4,32,1024]{2,1,0:T(8,128)(2,1)S(1)}, u32[]{:S(2)}, u32[]{:S(2)}) collective-permute-start(bf16[4,32,1024]{2,1,0:T(8,128)(2,1)S(1)} %bitcast.112), channel_id=1, source_target_pairs={{0,8},{8,0},{1,9},{9,1},{2,10},{10,2},{3,11},{11,3},{4,12},{12,4},... | collective-permute-start | bytes 786440 | tf_op jit(solution)/shard_map/ppermute | solution.py:45
  222.0 9.1 %collective-permute-start.29 = (bf16[32,3072]{1,0:T(8,128)(2,1)S(1)}, bf16[32,3072]{1,0:T(8,128)(2,1)S(1)}, u32[]{:S(2)}, u32[]{:S(2)}) collective-permute-start(bf16[32,3072]{1,0:T(8,128)(2,1)S(1)} %get-tuple-element.201), channel_id=1, source_target_pairs={{0,1},{1,0},{16,17},{17,16},{2,3},{3,2},{18,19},{19,18},{4,5},{5,4... | collective-permute-start | bytes 589832 | tf_op jit(solution)/shard_map/ppermute | solution.py:45
  223.7 7.5 %collective-permute-start.30 = (bf16[32,3072]{1,0:T(8,128)(2,1)S(1)}, bf16[32,3072]{1,0:T(8,128)(2,1)S(1)}, u32[]{:S(2)}, u32[]{:S(2)}) collective-permute-start(bf16[32,3072]{1,0:T(8,128)(2,1)S(1)} %get-tuple-element.200), channel_id=1, source_target_pairs={{0,16},{1,17},{16,0},{17,1},{2,18},{3,19},{18,2},{19,3},{4,20},{5,... | collective-permute-start | bytes 589832 | tf_op jit(solution)/shard_map/ppermute | solution.py:45
  224.2 8.8 %collective-permute-start.31 = (bf16[32,3072]{1,0:T(8,128)(2,1)S(1)}, bf16[32,3072]{1,0:T(8,128)(2,1)S(1)}, u32[]{:S(2)}, u32[]{:S(2)}) collective-permute-start(bf16[32,3072]{1,0:T(8,128)(2,1)S(1)} %get-tuple-element.199), channel_id=1, source_target_pairs={{0,17},{1,16},{16,1},{17,0},{2,19},{3,18},{18,3},{19,2},{4,21},{5,... | collective-permute-start | bytes 589832 | tf_op jit(solution)/shard_map/ppermute | solution.py:45
  (47 other events, 238.5 us)
Sparse Core Ops, SparseCore 0:
  37.2 59.2 all-gather.1
  160.6 48.8 reduce-scatter.1

commit v2 on v1

--- a/solution.py
+++ b/solution.py
@@ -1,4 +1,5 @@
 import functools
+import math
 
 import jax
 import jax.numpy as jnp
@@ -14,6 +15,9 @@
 F32 = jnp.float32
 BF16 = jnp.bfloat16
 MEBI = 1024 * 1024
+FEED_MEBI = 24
+GELU_SCALE = math.sqrt(2.0 / math.pi)
+GELU_CUBE = 0.044715
 SQUARE = ("x", "y")
 UNITS_GROUP = ("z", "c", "r")
 EVERY = ("x", "c", "z", "y", "r")
@@ -495,8 +499,72 @@
     ).astype(BF16)
 
 
-def gated(gate_act, up_act):
-    return jax.nn.gelu(gate_act, approximate=True) * up_act
+def feed_body(count, *refs):
+    blocks, cot, rows = refs[:count], refs[count], refs[count + 1]
+    outs = refs[-5 - count : -5]
+    mid_out, gate_out, up_out, hidden_out, acc = refs[-5:]
+    tokens, width = blocks[0].shape
+    for at in range(count):
+        mid_out[at * tokens : (at + 1) * tokens, :] = blocks[at][...]
+    units = rows.shape[0]
+    for start in range(0, units, 256):
+        part = slice(start, min(start + 256, units))
+        gate_rows = rows[part, 0:width]
+        up_rows = rows[part, width : 2 * width]
+        gate_act = nt(mid_out[...], gate_rows)
+        up_act = nt(mid_out[...], up_rows)
+        upstream = nt(cot[...], rows[part, 2 * width :])
+        square = gate_act * gate_act
+        curve = jnp.tanh(GELU_SCALE * gate_act * (1.0 + GELU_CUBE * square))
+        half = 0.5 + 0.5 * curve
+        gelu = gate_act * half
+        slope = half + (0.5 * GELU_SCALE) * gate_act * (1.0 - curve * curve) * (
+            1.0 + 3.0 * GELU_CUBE * square
+        )
+        hidden_out[:, part] = (gelu * up_act).astype(BF16)
+        gate_low = (upstream * up_act * slope).astype(BF16)
+        up_low = (upstream * gelu).astype(BF16)
+        gate_out[:, part] = gate_low
+        up_out[:, part] = up_low
+        step = nn(gate_low, gate_rows) + nn(up_low, up_rows)
+        if start == 0:
+            acc[...] = step
+        else:
+            acc[...] += step
+    for at in range(count):
+        outs[at][...] = acc[at * tokens : (at + 1) * tokens, :].astype(BF16)
+
+
+def feed_call(blocks, place, cot_all, unit_rows, kept):
+    count, (tokens, width) = len(blocks), blocks[0].shape
+    total, units = cot_all.shape[0], unit_rows.shape[0]
+    size = count * tokens
+    once = pl.Buffered(1)
+
+    def whole(dims):
+        return pl.BlockSpec(dims, lambda i: (0, 0), pipeline_mode=once)
+
+    def mine(columns):
+        return pl.BlockSpec((size, columns), lambda i: (place, 0), pipeline_mode=once)
+
+    made = pl.pallas_call(
+        functools.partial(feed_body, count),
+        grid=(1,),
+        in_specs=[whole((tokens, width))] * count
+        + [mine(width), whole(unit_rows.shape)]
+        + [pl.BlockSpec(memory_space=pl.ANY)] * len(kept),
+        out_specs=[whole((tokens, width))] * count + [mine(width)] + [mine(units)] * 3,
+        out_shape=[shape((tokens, width), BF16)] * count
+        + [shape((total, width), BF16)]
+        + [shape((total, units), BF16)] * 3,
+        scratch_shapes=[pltpu.VMEM((size, width), F32)],
+        input_output_aliases={count + 2 + at: count + at for at in range(len(kept))},
+        compiler_params=pltpu.CompilerParams(vmem_limit_bytes=MEBI * FEED_MEBI),
+        cost_estimate=pl.CostEstimate(
+            flops=int(2.5e9 * count), bytes_accessed=1 << 20, transcendentals=0
+        ),
+    )(*blocks, cot_all, unit_rows, *kept)
+    return made[:count], made[count:]
 
 
 def body(
@@ -583,9 +651,7 @@
         (messages, hvec, cuts, coords, units)
     )
     unit_rows = lax.all_gather(units, UNITS_GROUP, axis=0, tiled=True)
-    gate_piece, up_piece, down_piece = (
-        unit_rows[:, at * width : (at + 1) * width] for at in range(3)
-    )
+    down_piece = unit_rows[:, 2 * width :]
 
     made = kernel_call(
         functools.partial(qkv_body, hd),
@@ -636,7 +702,7 @@
     parts = from_group(sent, SQUARE)
     arrived = lax.all_to_all(out_t, ("x", "y", "z"), split_axis=0, concat_axis=0, tiled=True)
     parts, arrived = lax.optimization_barrier((parts, arrived))
-    cot_all = jnp.concatenate([part[:tokens] for part in parts], axis=0)
+    cot_all = jnp.concatenate([parts[at][:tokens] for at in (1, 2, 0, 3)], axis=0)
     out_here = jnp.concatenate([part[tokens:] for part in parts], axis=0)
     out_other = swap(out_here, "c", 1)
 
@@ -658,24 +724,20 @@
         ],
     )
     scale_second = norm_scale(middle)
-    mid_all = jnp.concatenate(from_group(normed_mid, SQUARE), axis=0)
-
-    gate_act = nt(mid_all, gate_piece)
-    up_act = nt(mid_all, up_piece)
-    hidden_val, pullback = jax.vjp(gated, gate_act, up_act)
-    hidden = hidden_val.astype(BF16)
-    grad_gate, grad_up = pullback(nt(cot_all, down_piece))
-    gate_low, up_low = grad_gate.astype(BF16), grad_up.astype(BF16)
-    grad_norm = (nn(gate_low, gate_piece) + nn(up_low, up_piece)).astype(BF16)
-    grad_parts = to_group(
-        [grad_norm[at * tokens : (at + 1) * tokens] for at in range(4)], SQUARE
-    )
+    own, second, third, fourth = from_group(normed_mid, SQUARE)
+
+    (grad_own_part,), kept = feed_call([own], 2, cot_all, unit_rows, [])
+    grad_near, kept = feed_call([second, third], 0, cot_all, unit_rows, kept)
+    (grad_last,), kept = feed_call([fourth], 3, cot_all, unit_rows, kept)
+    mid_all, gate_low, up_low, hidden = kept
+    grad_parts = to_group([grad_own_part, *grad_near, grad_last], SQUARE)
     unit_grads = jnp.concatenate(
         [tn(gate_low, mid_all), tn(up_low, mid_all), tn(hidden, cot_all)], axis=1
     ).astype(BF16)
     feed = nn(hidden, down_piece).astype(BF16)
     grad_parts, unit_grads, feed = lax.optimization_barrier((grad_parts, unit_grads, feed))
     grad_norm_mid = sum(part.astype(F32) for part in grad_parts)
+    feed, grad_norm_mid = lax.optimization_barrier((feed, grad_norm_mid))
 
     grad_middle = cot_own.astype(F32) + norm_back(
         middle, scale_second, gain_feedforward, grad_norm_mid
@@ -698,12 +760,12 @@
         [
             jnp.concatenate(
                 [
-                    feed[at * tokens : (at + 1) * tokens],
+                    feed[order * tokens : (order + 1) * tokens],
                     grad_mid_low,
                     features[at],
                 ]
             )
-            for at in range(4)
+            for at, order in enumerate((2, 0, 1, 3))
         ],
         SQUARE,
     )

time: 253 us -> 244 us (0.964)
  waiting for transfers between devices: 61 us -> 45.5 us
  Pallas kernels: 49.4 us -> 57.5 us
  matrix products: 16.6 us -> 10.8 us
  local copies, waits for them, and re-layouts: 21.8 us -> 24.8 us
    ppermute x40, waiting for transfers between devices: 42.3 us -> 27.6 us  [swap(): return lax.ppermute(value, axis, [(at, at ^ mask) for at in range(size)])]
    pallas_call x0 -> x3, Pallas kernels: none -> 7.91 us  [feed_call(): pl.pallas_call(functools.partial(feed_body, count), grid=(1,), in_specs=[...]
    dot_general x4 -> x1, matrix products: 6.06 us -> 0.71 us  [nt(): lax.dot_general(left, right, (((1,), (1,)), ((), ())), preferred_element_...]
    unnamed x90 -> x103, local copies, waits for them, and re-layouts: 11.9 us -> 13.6 us
    dot_general x4 -> x2, matrix products: 5.08 us -> 4.64 us  [nn(): lax.dot_general(left, right, (((1,), (0,)), ((), ())), preferred_element_...]
  transfers between devices with their start and end apart: 44 -> 44, of which waited for: 21 -> 13; matrix products, arithmetic and copies ran while one was open for 13% -> 15% of each run, Pallas kernels for 19% -> 23%
where the time goes in v2:
time: 244 us; the launch traced here: 243 us
  starting transfers between devices  59.7 us (24%)
  Pallas kernels  57.5 us (24%)
  waiting for transfers between devices  45.5 us (19%)
  local copies, waits for them, and re-layouts  24.8 us (10%)
  other arithmetic  16.7 us (7%)
  between operations  15 us (6%)
  blocking collectives  13 us (5%)
  matrix products  10.8 us (4%)
    pallas_call x8, Pallas kernels, kernel_call(): pl.pallas_call(body, out_shape=out_shapes, in_specs=in_specs, out_specs=j...  49 us
    ppermute x40, starting transfers between devices, swap(): return lax.ppermute(value, axis, [(at, at ^ mask) for at in range(size)])  42.5 us
    ppermute x40, waiting for transfers between devices, swap(): return lax.ppermute(value, axis, [(at, at ^ mask) for at in range(size)])  27.6 us
    unnamed x103, local copies, waits for them, and re-layouts  13.6 us
    all_to_all x1, starting transfers between devices, body(): lax.all_to_all(out_t, ('x', 'y', 'z'), split_axis=0, concat_axis=0, tiled...  13.4 us
    all_to_all x1, waiting for transfers between devices, body(): lax.all_to_all(out_t, ('x', 'y', 'z'), split_axis=0, concat_axis=0, tiled...  13.1 us
    all_to_all x1, blocking collectives, body(): lax.all_to_all(grad_attended.reshape(16, hd, tokens), ('x', 'y', 'z'), sp...  13 us
    pallas_call x3, Pallas kernels, feed_call(): pl.pallas_call(functools.partial(feed_body, count), grid=(1,), in_specs=[...  7.91 us
  transfers between devices with their start and end apart: 44, of which 13 were waited for; matrix products, arithmetic and copies ran while one was open for 15% of the time, Pallas kernels for 23%

profile of v2, /device:TPU:0, one launch (start us, length us, event | category | flops | bytes accessed | tf_op | source)
XLA Modules:
  0.0 243.0 jit_solution(5813687727752193856)
XLA Ops:
  7.2 2.3 shard_map.229
  9.6 3.0 %collective-permute-start = (bf16[160,1024]{1,0:T(8,128)(2,1)}, bf16[160,1024]{1,0:T(8,128)(2,1)S(1)}, u32[]{:S(2)}, u32[]{:S(2)}) collective-permute-start(bf16[160,1024]{1,0:T(8,128)(2,1)} %get-tuple-element.113.refs_0_), channel_id=1, source_target_pairs={{0,2},{2,0},{4,6},{6,4},{1,3},{3,1},{5,7},{7,5},{8,10},{10,8},{12,... | collective-permute-start | bytes 983048 | tf_op jit(solution)/shard_map/ppermute | solution.py:49
  12.6 2.6 %collective-permute-start.1 = (bf16[160,1024]{1,0:T(8,128)(2,1)}, bf16[160,1024]{1,0:T(8,128)(2,1)S(1)}, u32[]{:S(2)}, u32[]{:S(2)}) collective-permute-start(bf16[160,1024]{1,0:T(8,128)(2,1)} %get-tuple-element.113.refs_0_), channel_id=1, source_target_pairs={{0,4},{2,6},{4,0},{6,2},{1,5},{3,7},{5,1},{7,3},{8,12},{10,14},{12... | collective-permute-start | bytes 983048 | tf_op jit(solution)/shard_map/ppermute | solution.py:49
  28.0 9.0 %collective-permute-done.1.refs_2_ = bf16[160,1024]{1,0:T(8,128)(2,1)S(1)} collective-permute-done((bf16[160,1024]{1,0:T(8,128)(2,1)}, bf16[160,1024]{1,0:T(8,128)(2,1)S(1)}, u32[]{:S(2)}, u32[]{:S(2)}) %collective-permute-start.1) | collective-permute-done | bytes 327712 | tf_op jit(solution)/shard_map/ppermute | solution.py:49
  39.4 4.4 %shard_map.231 = (bf16[768,128]{1,0:T(8,128)(2,1)}, bf16[768,128]{1,0:T(8,128)(2,1)}, bf16[768,128]{1,0:T(8,128)(2,1)}, bf16[768,128]{1,0:T(8,128)(2,1)}, bf16[5...) custom-call(s32[5]{0:T(128)} %stack.35.coords, ...), custom_call_target="tpu_custom_call" | custom-call | flops 4600000000 | bytes 1048576 | tf_op jit(solution)/shard_map/pallas_call | solution.py:83
  43.8 2.5 %collective-permute-start.9 = (bf16[768,128]{1,0:T(8,128)(2,1)}, bf16[768,128]{1,0:T(8,128)(2,1)S(1)}, u32[]{:S(2)}, u32[]{:S(2)}) collective-permute-start(bf16[768,128]{1,0:T(8,128)(2,1)} %get-tuple-element.122), channel_id=1, source_target_pairs={{0,17},{1,16},{16,1},{17,0},{2,19},{3,18},{18,3},{19,2},{4,21},{5,... | collective-permute-start | bytes 589832 | tf_op jit(solution)/shard_map/ppermute | solution.py:49
  48.3 2.9 %collective-permute-done.9.refs_3_ = bf16[768,128]{1,0:T(8,128)(2,1)S(1)} collective-permute-done((bf16[768,128]{1,0:T(8,128)(2,1)}, bf16[768,128]{1,0:T(8,128)(2,1)S(1)}, u32[]{:S(2)}, u32[]{:S(2)}) %collective-permute-start.9) | collective-permute-done | bytes 196640 | tf_op jit(solution)/shard_map/ppermute | solution.py:49
  51.2 2.1 collective-permute-done.8.refs_2_
  57.9 13.0 %shard_map.232 = (bf16[16,64,128]{2,1,0:T(8,128)(2,1)}, f32[8,8,256]{2,1,0:T(8,128)}, f32[8,64,256]{2,1,0:T(8,128)}, bf16[4096,128]{1,0:T(8,128)(2,1)}, bf16[8,1...) custom-call(s32[5]{0:T(128)} %stack.35.coords, s32[16]{0:T(128)} %convert_reduce_fusion.cuts, f32[8,256]{1,0:T(8,128)} %pad.12.hvec, ...), custom_call_target="tpu_custom_call" | custom-call | flops 23000000512 | bytes 1048576 | tf_op jit(solution)/shard_map/pallas_call | solution.py:83
  70.9 13.4 %all-to-all-start = ((bf16[16,64,128]{2,1,0:T(8,128)(2,1)}), bf16[16,64,128]{2,1,0:T(8,128)(2,1)S(1)}, u32[]{:S(2)}, u32[]{:S(2)}) async-start(bf16[16,64,128]{2,1,0:T(8,128)(2,1)} %get-tuple-element.126), calls=%async_computation | async-start | bytes 524288 | tf_op jit(solution)/shard_map/all_to_all | solution.py:703
  84.6 13.1 %all-to-all-done = bf16[16,64,128]{2,1,0:T(8,128)(2,1)S(1)} async-done(((bf16[16,64,128]{2,1,0:T(8,128)(2,1)}), bf16[16,64,128]{2,1,0:T(8,128)(2,1)S(1)}, u32[]{:S(2)}, u32[]{:S(2)}) %all-to-all-start) | async-done | bytes 262176 | tf_op jit(solution)/shard_map/all_to_all | solution.py:703
  99.3 2.0 collective-permute-done.14.refs_4_
  102.2 3.9 %shard_map.233 = (f32[128,1024]{1,0:T(8,128)}, bf16[128,1024]{1,0:T(8,128)(2,1)}, bf16[1024,1024]{1,0:T(8,128)(2,1)}, bf16[4,32,1024]{2,1,0:T(8,128)(2,1)}) custom-call(s32[5]{0:T(128)} %stack.35.coords, bf16[1024,128]{1,0:T(8,128)(2,1)} %bitcast.106, bf16[128,1024]{1,0:T(8,128)(2,1)} %bitcast.94, f32[1,1024]{1,0:T(1,128)} %bitcast.113, ...), custom_call_target="tpu_custom_call" | custom-call | flops 4600000000 | bytes 1048576 | tf_op jit(solution)/shard_map/pallas_call | solution.py:83
  107.3 2.4 collective-permute-start.19
  110.9 2.2 copy-done.1
  114.0 2.5 %shard_map.234 = (bf16[128,1024]{1,0:T(8,128)(2,1)S(1)}, bf16[512,1024]{1,0:T(8,128)(2,1)S(1)}, bf16[512,704]{1,0:T(8,128)(2,1)S(1)}, bf16[512,704]{1,0:T(8,128)(2,1)S(1)}, bf16[512,704]{1,0:T(8,128)(2,1)S(1)}) custom-call(bf16[128,1024]{1,0:T(8,128)(2,1)S(1)} %copy-done.3, bf16[512,1024]{1,0:T(8,128)(2,1)S(1)} %pad_maximum_fusion.2.refs_1_.refs_2_, ...), custom_call_target="tpu_custom_call" | custom-call | flops 2500000000 | bytes 1048576 | tf_op jit(solution)/shard_map/pallas_call | solution.py:550
  116.5 3.0 %shard_map.235 = (bf16[128,1024]{1,0:T(8,128)(2,1)S(1)}, bf16[128,1024]{1,0:T(8,128)(2,1)S(1)}, bf16[512,1024]{1,0:T(8,128)(2,1)S(1)}, bf16[512,704]{1,0:T(8,128...) custom-call(bf16[128,1024]{1,0:T(8,128)(2,1)S(1)} %collective-permut, ...), custom_call_target="tpu_custom_call", output_to_operand_aliasing={{2}: (4, {}), {3}: (5, {}), {4}: (6, {}), {5}: (7, {})} | custom-call | flops 5000000000 | bytes 1048576 | tf_op jit(solution)/shard_map/pallas_call | solution.py:550
  121.5 2.5 %shard_map.236 = (bf16[128,1024]{1,0:T(8,128)(2,1)S(1)}, bf16[512,1024]{1,0:T(8,128)(2,1)S(1)}, bf16[512,704]{1,0:T(8,128)(2,1)S(1)}, bf16[512,704]{1,0:T(8,128)(2,1)S(1)}, bf16[512,704]{1,0:T(8,128)(2,1)S(1)}) custom-call(bf16[128,1024]{1,0:T(8,128)(2,1)S(1)} %collective-permute-done.19.refs, ...), custom_call_target="tpu_custom_call", output_to_operand_aliasing={{1}: (3, {}), {2}: (4, {}), {3}: (5, {}), {4}: (6, {})} | custom-call | flops 2500000000 | bytes 1048576 | tf_op jit(solution)/shard_map/pallas_call | solution.py:550
  128.5 2.2 pad_maximum_fusion
  130.7 3.4 %convolution_convert_fusion.3 = bf16[512,1024]{1,0:T(8,128)(2,1)} fusion(bf16[512,704]{1,0:T(8,128)(2,1)S(1)} %get-tuple-element.150, bf16[704,3072]{1,0:T(8,128)(2,1)} %all-gather.2.cloned.1.call-done.refs_2_.refs_3_), kind=kOutput, calls=%fused_computation.5 | convolution fusion | flops 738721792 | bytes 3211264 | tf_op jit(solution)/shard_map/dot_general | solution.py:40
  136.6 13.0 %all_to_all.15.refs_0_ = bf16[16,64,128]{2,1,0:T(8,128)(2,1)} all-to-all(bf16[16,64,128]{2,1,0:T(8,128)(2,1)S(1)} %bitcast.99), channel_id=1, replica_groups=mesh['x'=2,'c'=2,'z'=4,'y'=2,'r'=1] {'x','y','z'}, dimensions={0} | all-to-all | bytes 524288 | tf_op jit(solution)/shard_map/all_to_all | solution.py:748
  153.4 2.4 collective-permute-start.23
  155.8 17.6 %shard_map.237 = (f32[2048,128]{1,0:T(8,128)}, bf16[2048,128]{1,0:T(8,128)(2,1)}, bf16[16,64,128]{2,1,0:T(8,128)(2,1)}, f32[8,256]{1,0:T(8,128)}, f32[8,256]{1,0:T(8,128)}) custom-call(s32[5]{0:T(128)} %stack.35.coords, s32[16]{0:T(128)} %convert_reduce_fusion.cuts, f32[8,256]{1,0:T(8,128)} %pad.12.hvec, bf16[16,64,128]{2,1,0:T(8,128)(2,1)} %all_to_all.15.refs_0_, ...), custom_call_target="tpu_custom_call" | custom-call | flops 23000000512 | bytes 1048576 | tf_op jit(solution)/shard_map/pallas_call | solution.py:83
  174.4 4.0 %collective-permute-done.23 = bf16[288,1024]{1,0:T(8,128)(2,1)} collective-permute-done((bf16[288,1024]{1,0:T(8,128)(2,1)}, bf16[288,1024]{1,0:T(8,128)(2,1)}, u32[]{:S(2)}, u32[]{:S(2)}) %collective-permute-start.23) | collective-permute-done | bytes 589856 | tf_op jit(solution)/shard_map/ppermute | solution.py:49
  190.3 2.6 %shard_map.238 = (bf16[4,128,1024]{2,1,0:T(8,128)(2,1)}, f32[8,1024]{1,0:T(8,128)S(1)}, bf16[512,512]{1,0:T(8,128)(2,1)S(1)}, bf16[256,512]{1,0:T(8,128)(2,1)S(1)}) custom-call(s32[5]{0:T(128)S(1)} %copy-done, bf16[768,128]{1,0:T(8,128)(2,1)S(1)} %pad_maximum_fusion.10.refs_0_, bf16[768,128]{1,0:T(8,128)(2,1)S(1)} %collective-permute-done.25.refs_1_, ...), custom_call_target="tpu_custom_call" | custom-call | flops 4600000000 | bytes 1048576 | tf_op jit(solution)/shard_map/pallas_call | solution.py:83
  194.4 3.5 %all-to-all-start.2 = ((bf16[4,128,1024]{2,1,0:T(8,128)(2,1)}), bf16[4,128,1024]{2,1,0:T(8,128)(2,1)S(1)}, u32[]{:S(2)}, u32[]{:S(2)}) async-start(bf16[4,128,1024]{2,1,0:T(8,128)(2,1)} %get-tuple-element.186), calls=%async_computation.2 | async-start | bytes 2097152 | tf_op jit(solution)/shard_map/all_to_all | solution.py:824
  198.0 4.1 %shard_map.239 = (bf16[4,32,3072]{2,1,0:T(8,128)(2,1)}, bf16[4,32,3072]{2,1,0:T(8,128)(2,1)}) custom-call(s32[5]{0:T(128)} %stack.35.coords, bf16[512,512]{1,0:T(8,128)(2,1)} %copy-done.7, bf16[256,512]{1,0:T(8,128)(2,1)} %copy-done.8, bf16[512,1024]{1,0:T(8,128)(2,1)} %get-tuple-element.184.refs_4_.rows_all), custom_call_target="tpu_custom_call" | custom-call | flops 4600000000 | bytes 1048576 | tf_op jit(solution)/shard_map/pallas_call | solution.py:83
  209.8 2.1 fusion.32
  215.8 4.6 %all-to-all-done.2.refs_0_ = bf16[4,128,1024]{2,1,0:T(8,128)(2,1)S(1)} async-done(((bf16[4,128,1024]{2,1,0:T(8,128)(2,1)}), bf16[4,128,1024]{2,1,0:T(8,128)(2,1)S(1)}, u32[]{:S(2)}, u32[]{:S(2)}) %all-to-all-start.2) | async-done | bytes 1048608 | tf_op jit(solution)/shard_map/all_to_all | solution.py:824
  221.2 2.9 %collective-permute-done.31 = bf16[32,3072]{1,0:T(8,128)(2,1)S(1)} collective-permute-done((bf16[32,3072]{1,0:T(8,128)(2,1)S(1)}, bf16[32,3072]{1,0:T(8,128)(2,1)S(1)}, u32[]{:S(2)}, u32[]{:S(2)}) %collective-permute-start.31) | collective-permute-done | bytes 196640 | tf_op jit(solution)/shard_map/ppermute | solution.py:49
  224.2 3.8 %collective-permute-start.39 = (bf16[40,1024]{1,0:T(8,128)(2,1)S(1)}, bf16[40,1024]{1,0:T(8,128)(2,1)S(1)}, u32[]{:S(2)}, u32[]{:S(2)}) collective-permute-start(bf16[40,1024]{1,0:T(8,128)(2,1)S(1)} %get-tuple-element.273), channel_id=1, source_target_pairs={{0,6},{2,4},{4,2},{6,0},{1,7},{3,5},{5,3},{7,1},{8,14},{10,12},{12... | collective-permute-start | bytes 245768 | tf_op jit(solution)/shard_map/ppermute | solution.py:49
  230.7 3.3 %collective-permute-done.38 = bf16[40,1024]{1,0:T(8,128)(2,1)S(1)} collective-permute-done((bf16[40,1024]{1,0:T(8,128)(2,1)S(1)}, bf16[40,1024]{1,0:T(8,128)(2,1)S(1)}, u32[]{:S(2)}, u32[]{:S(2)}) %collective-permute-start.38) | collective-permute-done | bytes 81952 | tf_op jit(solution)/shard_map/ppermute | solution.py:49
  (262 shorter events, 71.5 us)
Async XLA Ops:
  7.2 103.7 %all-gather.2.cloned.1.call-start = ((), (), s32[]{:S(2)}) async-start(), calls=%async_computation.4 | async-start | bytes 4866048 | tf_op jit(solution)/shard_map/all_gather | solution.py:653
  9.6 18.4 %collective-permute-start = (bf16[160,1024]{1,0:T(8,128)(2,1)}, bf16[160,1024]{1,0:T(8,128)(2,1)S(1)}, u32[]{:S(2)}, u32[]{:S(2)}) collective-permute-start(bf16[160,1024]{1,0:T(8,128)(2,1)} %get-tuple-element.113.refs_0_), channel_id=1, source_target_pairs={{0,2},{2,0},{4,6},{6,4},{1,3},{3,1},{5,7},{7,5},{8,10},{10,8},{12,... | collective-permute-start | bytes 983048 | tf_op jit(solution)/shard_map/ppermute | solution.py:49
  12.6 24.5 %collective-permute-start.1 = (bf16[160,1024]{1,0:T(8,128)(2,1)}, bf16[160,1024]{1,0:T(8,128)(2,1)S(1)}, u32[]{:S(2)}, u32[]{:S(2)}) collective-permute-start(bf16[160,1024]{1,0:T(8,128)(2,1)} %get-tuple-element.113.refs_0_), channel_id=1, source_target_pairs={{0,4},{2,6},{4,0},{6,2},{1,5},{3,7},{5,1},{7,3},{8,12},{10,14},{12... | collective-permute-start | bytes 983048 | tf_op jit(solution)/shard_map/ppermute | solution.py:49
  15.2 11.5 %collective-permute-start.3 = (bf16[32,3072]{1,0:T(8,128)(2,1)}, bf16[32,3072]{1,0:T(8,128)(2,1)S(1)}, u32[]{:S(2)}, u32[]{:S(2)}) collective-permute-start(bf16[32,3072]{1,0:T(8,128)(2,1)} %get-tuple-element.117.refs_4_), channel_id=1, source_target_pairs={{0,1},{1,0},{16,17},{17,16},{2,3},{3,2},{18,19},{19,18},{4,5},{5,4... | collective-permute-start | bytes 589832 | tf_op jit(solution)/shard_map/ppermute | solution.py:49
  16.7 10.0 %collective-permute-start.4 = (bf16[32,3072]{1,0:T(8,128)(2,1)}, bf16[32,3072]{1,0:T(8,128)(2,1)S(1)}, u32[]{:S(2)}, u32[]{:S(2)}) collective-permute-start(bf16[32,3072]{1,0:T(8,128)(2,1)} %get-tuple-element.117.refs_4_), channel_id=1, source_target_pairs={{0,16},{1,17},{16,0},{17,1},{2,18},{3,19},{18,2},{19,3},{4,20},{5,... | collective-permute-start | bytes 589832 | tf_op jit(solution)/shard_map/ppermute | solution.py:49
  18.2 8.7 %collective-permute-start.5 = (bf16[32,3072]{1,0:T(8,128)(2,1)}, bf16[32,3072]{1,0:T(8,128)(2,1)S(1)}, u32[]{:S(2)}, u32[]{:S(2)}) collective-permute-start(bf16[32,3072]{1,0:T(8,128)(2,1)} %get-tuple-element.117.refs_4_), channel_id=1, source_target_pairs={{0,17},{1,16},{16,1},{17,0},{2,19},{3,18},{18,3},{19,2},{4,21},{5,... | collective-permute-start | bytes 589832 | tf_op jit(solution)/shard_map/ppermute | solution.py:49
  26.7 10.4 %collective-permute-start.2 = (bf16[160,1024]{1,0:T(8,128)(2,1)}, bf16[160,1024]{1,0:T(8,128)(2,1)S(1)}, u32[]{:S(2)}, u32[]{:S(2)}) collective-permute-start(bf16[160,1024]{1,0:T(8,128)(2,1)} %get-tuple-element.113.refs_0_), channel_id=1, source_target_pairs={{0,6},{2,4},{4,2},{6,0},{1,7},{3,5},{5,3},{7,1},{8,14},{10,12},{12... | collective-permute-start | bytes 983048 | tf_op jit(solution)/shard_map/ppermute | solution.py:49
  27.9 10.6 %collective-permute-start.6 = (bf16[128,3072]{1,0:T(8,128)(2,1)S(1)}, bf16[128,3072]{1,0:T(8,128)(2,1)S(1)}, u32[]{:S(2)}, u32[]{:S(2)}) collective-permute-start(bf16[128,3072]{1,0:T(8,128)(2,1)S(1)} %pad_maximum_fusion.7), channel_id=1, source_target_pairs={{0,8},{8,0},{1,9},{9,1},{2,10},{10,2},{3,11},{11,3},{4,12},{12,4},... | collective-permute-start | bytes 2359304 | tf_op jit(solution)/shard_map/ppermute | solution.py:49
  43.8 7.4 %collective-permute-start.9 = (bf16[768,128]{1,0:T(8,128)(2,1)}, bf16[768,128]{1,0:T(8,128)(2,1)S(1)}, u32[]{:S(2)}, u32[]{:S(2)}) collective-permute-start(bf16[768,128]{1,0:T(8,128)(2,1)} %get-tuple-element.122), channel_id=1, source_target_pairs={{0,17},{1,16},{16,1},{17,0},{2,19},{3,18},{18,3},{19,2},{4,21},{5,... | collective-permute-start | bytes 589832 | tf_op jit(solution)/shard_map/ppermute | solution.py:49
  53.5 31.1 %collective-permute-start.10 = (bf16[256,1024]{1,0:T(8,128)(2,1)S(1)}, bf16[256,1024]{1,0:T(8,128)(2,1)S(1)}, u32[]{:S(2)}, u32[]{:S(2)}) collective-permute-start(bf16[256,1024]{1,0:T(8,128)(2,1)S(1)} %copy-done.22), channel_id=1, source_target_pairs={{0,1},{1,0},{16,17},{17,16},{2,3},{3,2},{18,19},{19,18},{4,5},{5,4... | collective-permute-start | bytes 1572872 | tf_op jit(solution)/shard_map/ppermute | solution.py:49
  55.0 29.6 %collective-permute-start.11 = (bf16[256,1024]{1,0:T(8,128)(2,1)S(1)}, bf16[256,1024]{1,0:T(8,128)(2,1)S(1)}, u32[]{:S(2)}, u32[]{:S(2)}) collective-permute-start(bf16[256,1024]{1,0:T(8,128)(2,1)S(1)} %copy-done.22), channel_id=1, source_target_pairs={{0,16},{1,17},{16,0},{17,1},{2,18},{3,19},{18,2},{19,3},{4,20},{5,... | collective-permute-start | bytes 1572872 | tf_op jit(solution)/shard_map/ppermute | solution.py:49
  56.5 28.1 %collective-permute-start.12 = (bf16[256,1024]{1,0:T(8,128)(2,1)S(1)}, bf16[256,1024]{1,0:T(8,128)(2,1)S(1)}, u32[]{:S(2)}, u32[]{:S(2)}) collective-permute-start(bf16[256,1024]{1,0:T(8,128)(2,1)S(1)} %copy-done.22), channel_id=1, source_target_pairs={{0,17},{1,16},{16,1},{17,0},{2,19},{3,18},{18,3},{19,2},{4,21},{5,... | collective-permute-start | bytes 1572872 | tf_op jit(solution)/shard_map/ppermute | solution.py:49
  70.9 26.8 %all-to-all-start = ((bf16[16,64,128]{2,1,0:T(8,128)(2,1)}), bf16[16,64,128]{2,1,0:T(8,128)(2,1)S(1)}, u32[]{:S(2)}, u32[]{:S(2)}) async-start(bf16[16,64,128]{2,1,0:T(8,128)(2,1)} %get-tuple-element.126), calls=%async_computation | async-start | bytes 524288 | tf_op jit(solution)/shard_map/all_to_all | solution.py:703
  84.4 117.7 %reduce-scatter.2.cloned.1.call-start = ((), (), s32[]{:S(2)}) async-start(), calls=%async_computation.5 | async-start | bytes 4866048 | tf_op jit(solution)/shard_map/reduce_scatter | solution.py:758
  106.2 10.3 %collective-permute-start.15 = (bf16[128,1024]{1,0:T(8,128)(2,1)}, bf16[128,1024]{1,0:T(8,128)(2,1)S(1)}, u32[]{:S(2)}, u32[]{:S(2)}) collective-permute-start(bf16[128,1024]{1,0:T(8,128)(2,1)} %get-tuple-element.133.refs_0_), channel_id=1, source_target_pairs={{0,1},{1,0},{16,17},{17,16},{2,3},{3,2},{18,19},{19,18},{4,5},{5,4... | collective-permute-start | bytes 786440 | tf_op jit(solution)/shard_map/ppermute | solution.py:49
  106.2 10.3 %collective-permute-start.16 = (bf16[128,1024]{1,0:T(8,128)(2,1)}, bf16[128,1024]{1,0:T(8,128)(2,1)S(1)}, u32[]{:S(2)}, u32[]{:S(2)}) collective-permute-start(bf16[128,1024]{1,0:T(8,128)(2,1)} %get-tuple-element.133.refs_0_), channel_id=1, source_target_pairs={{0,16},{1,17},{16,0},{17,1},{2,18},{3,19},{18,2},{19,3},{4,20},{5,... | collective-permute-start | bytes 786440 | tf_op jit(solution)/shard_map/ppermute | solution.py:49
  107.3 14.2 %collective-permute-start.19 = (bf16[128,1024]{1,0:T(8,128)(2,1)}, bf16[128,1024]{1,0:T(8,128)(2,1)S(1)}, u32[]{:S(2)}, u32[]{:S(2)}) collective-permute-start(bf16[128,1024]{1,0:T(8,128)(2,1)} %get-tuple-element.133.refs_0_), channel_id=1, source_target_pairs={{0,17},{1,16},{16,1},{17,0},{2,19},{3,18},{18,3},{19,2},{4,21},{5,... | collective-permute-start | bytes 786440 | tf_op jit(solution)/shard_map/ppermute | solution.py:49
  119.5 14.6 %collective-permute-start.17 = (bf16[128,1024]{1,0:T(8,128)(2,1)S(1)}, bf16[128,1024]{1,0:T(8,128)(2,1)S(1)}, u32[]{:S(2)}, u32[]{:S(2)}) collective-permute-start(bf16[128,1024]{1,0:T(8,128)(2,1)S(1)} %get-tuple-element.140), channel_id=1, source_target_pairs={{0,1},{1,0},{16,17},{17,16},{2,3},{3,2},{18,19},{19,18},{4,5},{5,4... | collective-permute-start | bytes 786440 | tf_op jit(solution)/shard_map/ppermute | solution.py:49
  120.6 13.4 %collective-permute-start.18 = (bf16[128,1024]{1,0:T(8,128)(2,1)S(1)}, bf16[128,1024]{1,0:T(8,128)(2,1)}, u32[]{:S(2)}, u32[]{:S(2)}) collective-permute-start(bf16[128,1024]{1,0:T(8,128)(2,1)S(1)} %get-tuple-element.141), channel_id=1, source_target_pairs={{0,16},{1,17},{16,0},{17,1},{2,18},{3,19},{18,2},{19,3},{4,20},{5,... | collective-permute-start | bytes 786440 | tf_op jit(solution)/shard_map/ppermute | solution.py:49
  124.0 10.1 %collective-permute-start.20 = (bf16[128,1024]{1,0:T(8,128)(2,1)S(1)}, bf16[128,1024]{1,0:T(8,128)(2,1)S(1)}, u32[]{:S(2)}, u32[]{:S(2)}) collective-permute-start(bf16[128,1024]{1,0:T(8,128)(2,1)S(1)} %get-tuple-element.146), channel_id=1, source_target_pairs={{0,17},{1,16},{16,1},{17,0},{2,19},{3,18},{18,3},{19,2},{4,21},{5,... | collective-permute-start | bytes 786440 | tf_op jit(solution)/shard_map/ppermute | solution.py:49
  152.3 22.1 %collective-permute-start.21 = (bf16[288,1024]{1,0:T(8,128)(2,1)}, bf16[288,1024]{1,0:T(8,128)(2,1)S(1)}, u32[]{:S(2)}, u32[]{:S(2)}) collective-permute-start(bf16[288,1024]{1,0:T(8,128)(2,1)} %get-tuple-element.261), channel_id=1, source_target_pairs={{0,1},{1,0},{16,17},{17,16},{2,3},{3,2},{18,19},{19,18},{4,5},{5,4... | collective-permute-start | bytes 1769480 | tf_op jit(solution)/shard_map/ppermute | solution.py:49
  152.3 22.1 %collective-permute-start.22 = (bf16[288,1024]{1,0:T(8,128)(2,1)}, bf16[288,1024]{1,0:T(8,128)(2,1)S(1)}, u32[]{:S(2)}, u32[]{:S(2)}) collective-permute-start(bf16[288,1024]{1,0:T(8,128)(2,1)} %get-tuple-element.262), channel_id=1, source_target_pairs={{0,16},{1,17},{16,0},{17,1},{2,18},{3,19},{18,2},{19,3},{4,20},{5,... | collective-permute-start | bytes 1769480 | tf_op jit(solution)/shard_map/ppermute | solution.py:49
  153.4 25.0 %collective-permute-start.23 = (bf16[288,1024]{1,0:T(8,128)(2,1)}, bf16[288,1024]{1,0:T(8,128)(2,1)}, u32[]{:S(2)}, u32[]{:S(2)}) collective-permute-start(bf16[288,1024]{1,0:T(8,128)(2,1)} %get-tuple-element.260), channel_id=1, source_target_pairs={{0,17},{1,16},{16,1},{17,0},{2,19},{3,18},{18,3},{19,2},{4,21},{5,... | collective-permute-start | bytes 1769480 | tf_op jit(solution)/shard_map/ppermute | solution.py:49
  179.9 9.8 %collective-permute-start.25 = (bf16[768,128]{1,0:T(8,128)(2,1)S(1)}, bf16[768,128]{1,0:T(8,128)(2,1)S(1)}, u32[]{:S(2)}, u32[]{:S(2)}) collective-permute-start(bf16[768,128]{1,0:T(8,128)(2,1)S(1)} %pad_maximum_fusion.11), channel_id=1, source_target_pairs={{0,1},{1,0},{16,17},{17,16},{2,3},{3,2},{18,19},{19,18},{4,5},{5,4... | collective-permute-start | bytes 589832 | tf_op jit(solution)/shard_map/ppermute | solution.py:49
  180.3 9.4 %collective-permute-start.26 = (bf16[768,128]{1,0:T(8,128)(2,1)S(1)}, bf16[768,128]{1,0:T(8,128)(2,1)S(1)}, u32[]{:S(2)}, u32[]{:S(2)}) collective-permute-start(bf16[768,128]{1,0:T(8,128)(2,1)S(1)} %pad_maximum_fusion.12), channel_id=1, source_target_pairs={{0,16},{1,17},{16,0},{17,1},{2,18},{3,19},{18,2},{19,3},{4,20},{5,... | collective-permute-start | bytes 589832 | tf_op jit(solution)/shard_map/ppermute | solution.py:49
  181.5 8.1 %collective-permute-start.27 = (bf16[768,128]{1,0:T(8,128)(2,1)S(1)}, bf16[768,128]{1,0:T(8,128)(2,1)S(1)}, u32[]{:S(2)}, u32[]{:S(2)}) collective-permute-start(bf16[768,128]{1,0:T(8,128)(2,1)S(1)} %pad_maximum_fusion.13), channel_id=1, source_target_pairs={{0,17},{1,16},{16,1},{17,0},{2,19},{3,18},{18,3},{19,2},{4,21},{5,... | collective-permute-start | bytes 589832 | tf_op jit(solution)/shard_map/ppermute | solution.py:49
  194.4 26.1 %all-to-all-start.2 = ((bf16[4,128,1024]{2,1,0:T(8,128)(2,1)}), bf16[4,128,1024]{2,1,0:T(8,128)(2,1)S(1)}, u32[]{:S(2)}, u32[]{:S(2)}) async-start(bf16[4,128,1024]{2,1,0:T(8,128)(2,1)} %get-tuple-element.186), calls=%async_computation.2 | async-start | bytes 2097152 | tf_op jit(solution)/shard_map/all_to_all | solution.py:824
  202.1 9.9 %collective-permute-start.28 = (bf16[4,32,3072]{2,1,0:T(8,128)(2,1)}, bf16[4,32,3072]{2,1,0:T(8,128)(2,1)S(1)}, u32[]{:S(2)}, u32[]{:S(2)}) collective-permute-start(bf16[4,32,3072]{2,1,0:T(8,128)(2,1)} %get-tuple-element.195), channel_id=1, source_target_pairs={{0,8},{8,0},{1,9},{9,1},{2,10},{10,2},{3,11},{11,3},{4,12},{12,4},... | collective-permute-start | bytes 2359304 | tf_op jit(solution)/shard_map/ppermute | solution.py:49
  206.1 9.7 %collective-permute-start.36 = (bf16[4,32,1024]{2,1,0:T(8,128)(2,1)S(1)}, bf16[4,32,1024]{2,1,0:T(8,128)(2,1)S(1)}, u32[]{:S(2)}, u32[]{:S(2)}) collective-permute-start(bf16[4,32,1024]{2,1,0:T(8,128)(2,1)S(1)} %bitcast.107), channel_id=1, source_target_pairs={{0,8},{8,0},{1,9},{9,1},{2,10},{10,2},{3,11},{11,3},{4,12},{12,4},... | collective-permute-start | bytes 786440 | tf_op jit(solution)/shard_map/ppermute | solution.py:49
  212.2 8.3 %collective-permute-start.29 = (bf16[32,3072]{1,0:T(8,128)(2,1)S(1)}, bf16[32,3072]{1,0:T(8,128)(2,1)S(1)}, u32[]{:S(2)}, u32[]{:S(2)}) collective-permute-start(bf16[32,3072]{1,0:T(8,128)(2,1)S(1)} %get-tuple-element.230), channel_id=1, source_target_pairs={{0,1},{1,0},{16,17},{17,16},{2,3},{3,2},{18,19},{19,18},{4,5},{5,4... | collective-permute-start | bytes 589832 | tf_op jit(solution)/shard_map/ppermute | solution.py:49
  213.8 7.4 %collective-permute-start.30 = (bf16[32,3072]{1,0:T(8,128)(2,1)S(1)}, bf16[32,3072]{1,0:T(8,128)(2,1)S(1)}, u32[]{:S(2)}, u32[]{:S(2)}) collective-permute-start(bf16[32,3072]{1,0:T(8,128)(2,1)S(1)} %get-tuple-element.229), channel_id=1, source_target_pairs={{0,16},{1,17},{16,0},{17,1},{2,18},{3,19},{18,2},{19,3},{4,20},{5,... | collective-permute-start | bytes 589832 | tf_op jit(solution)/shard_map/ppermute | solution.py:49
  214.3 9.7 %collective-permute-start.31 = (bf16[32,3072]{1,0:T(8,128)(2,1)S(1)}, bf16[32,3072]{1,0:T(8,128)(2,1)S(1)}, u32[]{:S(2)}, u32[]{:S(2)}) collective-permute-start(bf16[32,3072]{1,0:T(8,128)(2,1)S(1)} %get-tuple-element.228), channel_id=1, source_target_pairs={{0,17},{1,16},{16,1},{17,0},{2,19},{3,18},{18,3},{19,2},{4,21},{5,... | collective-permute-start | bytes 589832 | tf_op jit(solution)/shard_map/ppermute | solution.py:49
  (55 other events, 243.0 us)
Sparse Core Ops, SparseCore 0:
  37.2 59.2 all-gather.1
  149.7 48.4 reduce-scatter.1

commit v3 on v2

--- a/solution.py
+++ b/solution.py
@@ -308,8 +308,8 @@
 
 
 def attend_back_body(tokens, hd, repeat, coords, cuts, hvec, *refs):
-    arrived, queries, keys, keys_t, attended, lse = refs[:6]
-    grad_own, grad_other, grad_q, table_out, far_out = refs[6:11]
+    arrived, queries, keys, keys_t, attended, lse, marks = refs[:7]
+    grad_own, grad_other, grad_q, bucket_out = refs[7:11]
     bias, grad_keys, table_acc, left, right, shifts, grad_queries = refs[11:]
     x_at, c_at, z_at, y_at, r_at = (coords[at] for at in range(5))
     block = 4 * tokens
@@ -405,9 +405,11 @@
         if diff - 1 <= -2:
             far_odd += tile_at(rows, half)
     extra = fold_rows(jnp.where(c_at == 0, far_even, far_odd), jnp.sum)
-    far_out[...] = fold_rows(table_acc[0], jnp.sum)
-    far_out[:, :tokens] += extra
-    table_out[...] = jnp.zeros_like(table_out)
+    far_rows = fold_rows(table_acc[0], jnp.sum)
+    far_rows = far_rows[:, :tokens] + far_rows[:, tokens:] + extra
+    total = jnp.sum(jnp.sum(far_rows, axis=0, keepdims=True), axis=1, keepdims=True)
+    last = 3 * 2 * tokens
+    bucket = total * marks[last : last + 1, :]
     for index, diff in enumerate((-1, 0, 1)):
         even = sum(tile_at(rows, half) for rows, half in spots if rows - 4 - 2 * half == diff)
         odd = sum(tile_at(rows, half) for rows, half in spots if rows - 5 - 2 * half == diff)
@@ -415,7 +417,12 @@
         turned = jnp.dot(flip, tile, precision=HIGHEST, preferred_element_type=F32)
         wide = jnp.concatenate([turned, jnp.zeros_like(turned)], axis=1)
         wide = pltpu.roll(wide, tokens + 1, 1, stride=1, stride_axis=0)
-        table_out[index : index + 1, :] = jnp.sum(wide, axis=0, keepdims=True)
+        diagonals = jnp.broadcast_to(jnp.sum(wide, axis=0, keepdims=True), (8, 2 * tokens))
+        part = marks[index * 2 * tokens : (index + 1) * 2 * tokens, :]
+        bucket = bucket + jnp.dot(
+            diagonals, part, precision=HIGHEST, preferred_element_type=F32
+        )[0:1, :]
+    bucket_out[...] = jnp.broadcast_to(bucket, bucket_out.shape)
 
 
 def project_back_body(hd, coords, *refs):
@@ -770,16 +777,17 @@
         SQUARE,
     )
 
-    grad_own, grad_other, grad_q, table_out, far_out = kernel_call(
+    marks = jnp.concatenate([onehot, far_onehot[None]], axis=0)
+    marks = jnp.pad(marks, ((0, 7), (0, -bucket_count % 128)))
+    grad_own, grad_other, grad_q, bucket_grad = kernel_call(
         functools.partial(attend_back_body, tokens, hd, repeat),
         [
             shape((4 * repeat * block, 2 * hd), F32),
             shape((4 * repeat * block, 2 * hd), BF16),
             shape((16, hd, tokens), BF16),
-            shape((8, 2 * tokens), F32),
-            shape((8, 2 * tokens), F32),
-        ],
-        [coords, cuts, hvec, grad_arrived, queries, keys, keys_t, attended, lse],
+            shape((8, marks.shape[1]), F32),
+        ],
+        [coords, cuts, hvec, grad_arrived, queries, keys, keys_t, attended, lse, marks],
         [
             pltpu.VMEM((places + 2, block, 2 * tokens), F32),
             pltpu.VMEM((length, 2 * hd), F32),
@@ -833,16 +841,14 @@
     near = near.transpose(2, 1, 0, 3).reshape(4 * hd, block)
     out_grads = nn(near, grad_mid_all).astype(BF16)
 
-    table_out, far_out, keep, send, grad_units, out_grads = lax.optimization_barrier(
-        (table_out, far_out, keep, send, grad_units, out_grads)
+    bucket_grad, keep, send, grad_units, out_grads = lax.optimization_barrier(
+        (bucket_grad, keep, send, grad_units, out_grads)
     )
     out_grads = out_grads.reshape(2, 4, hd // 2, width)
     out_grads = (out_grads[0].astype(F32) + swap(out_grads[1], "c", 1).astype(F32)).astype(BF16)
     head_grads = (keep.astype(F32) + swap(send, "c", 1).astype(F32)).astype(BF16)
-    bucket_grad = jnp.dot(table_out[:3].reshape(1, -1), onehot, precision=HIGHEST)[0]
-    bucket_grad = bucket_grad + far_onehot * jnp.sum(far_out)
     head_mark = (jnp.arange(head_count) == head_at).astype(F32)
-    bias_term = bucket_grad[:, None] * head_mark[None, :]
+    bias_term = bucket_grad[0, :bucket_count, None] * head_mark[None, :]
     sums = jnp.concatenate([jnp.sum(gain_first_rows, axis=0), gain_second_term, bias_term.ravel()])
     sums = sums + swap(sums, "c", 1)
     sums = sum_everywhere(sums, SQUARE)

time: 244 us -> 243 us (level)
    unnamed x103 -> x97, local copies, waits for them, and re-layouts: 13.6 us -> 12.1 us
where the time goes in v3:
time: 243 us; the launch traced here: 242 us
  starting transfers between devices  59.4 us (24%)
  Pallas kernels  58 us (24%)
  waiting for transfers between devices  45.8 us (19%)
  local copies, waits for them, and re-layouts  24.2 us (10%)
  other arithmetic  17.7 us (7%)
  between operations  15 us (6%)
  blocking collectives  13 us (5%)
  matrix products  9 us (4%)
    pallas_call x8, Pallas kernels, kernel_call(): pl.pallas_call(body, out_shape=out_shapes, in_specs=in_specs, out_specs=j...  49.5 us
    ppermute x40, starting transfers between devices, swap(): return lax.ppermute(value, axis, [(at, at ^ mask) for at in range(size)])  42.5 us
    ppermute x40, waiting for transfers between devices, swap(): return lax.ppermute(value, axis, [(at, at ^ mask) for at in range(size)])  26 us
    all_to_all x1, waiting for transfers between devices, body(): lax.all_to_all(out_t, ('x', 'y', 'z'), split_axis=0, concat_axis=0, tiled...  13.1 us
    all_to_all x1, starting transfers between devices, body(): lax.all_to_all(out_t, ('x', 'y', 'z'), split_axis=0, concat_axis=0, tiled...  13.1 us
    all_to_all x1, blocking collectives, body(): lax.all_to_all(grad_attended.reshape(16, hd, tokens), ('x', 'y', 'z'), sp...  13 us
    unnamed x97, local copies, waits for them, and re-layouts  12.1 us
    pallas_call x3, Pallas kernels, feed_call(): pl.pallas_call(functools.partial(feed_body, count), grid=(1,), in_specs=[...  7.89 us
  transfers between devices with their start and end apart: 44, of which 13 were waited for; matrix products, arithmetic and copies ran while one was open for 15% of the time, Pallas kernels for 23%

profile of v3, /device:TPU:0, one launch (start us, length us, event | category | flops | bytes accessed | tf_op | source)
XLA Modules:
  0.0 242.0 jit_solution(9059984221396010001)
XLA Ops:
  7.2 2.3 shard_map.229
  9.6 3.0 %collective-permute-start = (bf16[160,1024]{1,0:T(8,128)(2,1)}, bf16[160,1024]{1,0:T(8,128)(2,1)S(1)}, u32[]{:S(2)}, u32[]{:S(2)}) collective-permute-start(bf16[160,1024]{1,0:T(8,128)(2,1)} %get-tuple-element.111.refs_0_), channel_id=1, source_target_pairs={{0,2},{2,0},{4,6},{6,4},{1,3},{3,1},{5,7},{7,5},{8,10},{10,8},{12,... | collective-permute-start | bytes 983048 | tf_op jit(solution)/shard_map/ppermute | solution.py:49
  12.6 2.6 %collective-permute-start.1 = (bf16[160,1024]{1,0:T(8,128)(2,1)}, bf16[160,1024]{1,0:T(8,128)(2,1)S(1)}, u32[]{:S(2)}, u32[]{:S(2)}) collective-permute-start(bf16[160,1024]{1,0:T(8,128)(2,1)} %get-tuple-element.111.refs_0_), channel_id=1, source_target_pairs={{0,4},{2,6},{4,0},{6,2},{1,5},{3,7},{5,1},{7,3},{8,12},{10,14},{12... | collective-permute-start | bytes 983048 | tf_op jit(solution)/shard_map/ppermute | solution.py:49
  20.8 1.9 fusion.24
  28.0 9.0 %collective-permute-done.1.refs_2_ = bf16[160,1024]{1,0:T(8,128)(2,1)S(1)} collective-permute-done((bf16[160,1024]{1,0:T(8,128)(2,1)}, bf16[160,1024]{1,0:T(8,128)(2,1)S(1)}, u32[]{:S(2)}, u32[]{:S(2)}) %collective-permute-start.1) | collective-permute-done | bytes 327712 | tf_op jit(solution)/shard_map/ppermute | solution.py:49
  39.4 4.4 %shard_map.231 = (bf16[768,128]{1,0:T(8,128)(2,1)}, bf16[768,128]{1,0:T(8,128)(2,1)}, bf16[768,128]{1,0:T(8,128)(2,1)}, bf16[768,128]{1,0:T(8,128)(2,1)}, bf16[5...) custom-call(s32[5]{0:T(128)} %stack.35.coords, ...), custom_call_target="tpu_custom_call" | custom-call | flops 4600000000 | bytes 1048576 | tf_op jit(solution)/shard_map/pallas_call | solution.py:83
  43.8 2.5 %collective-permute-start.9 = (bf16[768,128]{1,0:T(8,128)(2,1)}, bf16[768,128]{1,0:T(8,128)(2,1)S(1)}, u32[]{:S(2)}, u32[]{:S(2)}) collective-permute-start(bf16[768,128]{1,0:T(8,128)(2,1)} %get-tuple-element.120), channel_id=1, source_target_pairs={{0,17},{1,16},{16,1},{17,0},{2,19},{3,18},{18,3},{19,2},{4,21},{5,... | collective-permute-start | bytes 589832 | tf_op jit(solution)/shard_map/ppermute | solution.py:49
  48.3 3.2 %collective-permute-done.9.refs_3_ = bf16[768,128]{1,0:T(8,128)(2,1)S(1)} collective-permute-done((bf16[768,128]{1,0:T(8,128)(2,1)}, bf16[768,128]{1,0:T(8,128)(2,1)S(1)}, u32[]{:S(2)}, u32[]{:S(2)}) %collective-permute-start.9) | collective-permute-done | bytes 196640 | tf_op jit(solution)/shard_map/ppermute | solution.py:49
  51.5 2.1 collective-permute-done.8.refs_2_
  58.2 13.0 %shard_map.232 = (bf16[16,64,128]{2,1,0:T(8,128)(2,1)}, f32[8,8,256]{2,1,0:T(8,128)}, f32[8,64,256]{2,1,0:T(8,128)}, bf16[4096,128]{1,0:T(8,128)(2,1)}, bf16[8,1...) custom-call(s32[5]{0:T(128)} %stack.35.coords, s32[16]{0:T(128)} %convert_reduce_fusion.cuts, f32[8,256]{1,0:T(8,128)} %pad.18.hvec, ...), custom_call_target="tpu_custom_call" | custom-call | flops 23000000512 | bytes 1048576 | tf_op jit(solution)/shard_map/pallas_call | solution.py:83
  71.3 13.1 %all-to-all-start = ((bf16[16,64,128]{2,1,0:T(8,128)(2,1)}), bf16[16,64,128]{2,1,0:T(8,128)(2,1)S(1)}, u32[]{:S(2)}, u32[]{:S(2)}) async-start(bf16[16,64,128]{2,1,0:T(8,128)(2,1)} %get-tuple-element.124), calls=%async_computation | async-start | bytes 524288 | tf_op jit(solution)/shard_map/all_to_all | solution.py:710
  84.6 13.1 %all-to-all-done = bf16[16,64,128]{2,1,0:T(8,128)(2,1)S(1)} async-done(((bf16[16,64,128]{2,1,0:T(8,128)(2,1)}), bf16[16,64,128]{2,1,0:T(8,128)(2,1)S(1)}, u32[]{:S(2)}, u32[]{:S(2)}) %all-to-all-start) | async-done | bytes 262176 | tf_op jit(solution)/shard_map/all_to_all | solution.py:710
  99.2 2.0 collective-permute-done.14.refs_4_
  102.3 3.9 %shard_map.233 = (f32[128,1024]{1,0:T(8,128)}, bf16[128,1024]{1,0:T(8,128)(2,1)}, bf16[1024,1024]{1,0:T(8,128)(2,1)}, bf16[4,32,1024]{2,1,0:T(8,128)(2,1)}) custom-call(s32[5]{0:T(128)} %stack.35.coords, bf16[1024,128]{1,0:T(8,128)(2,1)} %bitcast.98, bf16[128,1024]{1,0:T(8,128)(2,1)} %bitcast.86, f32[1,1024]{1,0:T(1,128)} %bitcast.105, ...), custom_call_target="tpu_custom_call" | custom-call | flops 4600000000 | bytes 1048576 | tf_op jit(solution)/shard_map/pallas_call | solution.py:83
  107.3 2.4 collective-permute-start.19
  110.9 2.2 copy-done.1
  114.0 2.5 %shard_map.234 = (bf16[128,1024]{1,0:T(8,128)(2,1)S(1)}, bf16[512,1024]{1,0:T(8,128)(2,1)S(1)}, bf16[512,704]{1,0:T(8,128)(2,1)S(1)}, bf16[512,704]{1,0:T(8,128)(2,1)S(1)}, bf16[512,704]{1,0:T(8,128)(2,1)S(1)}) custom-call(bf16[128,1024]{1,0:T(8,128)(2,1)S(1)} %copy-done.3, bf16[512,1024]{1,0:T(8,128)(2,1)S(1)} %pad_maximum_fusion.2.refs_1_.refs_2_, ...), custom_call_target="tpu_custom_call" | custom-call | flops 2500000000 | bytes 1048576 | tf_op jit(solution)/shard_map/pallas_call | solution.py:557
  116.5 3.0 %shard_map.235 = (bf16[128,1024]{1,0:T(8,128)(2,1)S(1)}, bf16[128,1024]{1,0:T(8,128)(2,1)S(1)}, bf16[512,1024]{1,0:T(8,128)(2,1)S(1)}, bf16[512,704]{1,0:T(8,128...) custom-call(bf16[128,1024]{1,0:T(8,128)(2,1)S(1)} %collective-permut, ...), custom_call_target="tpu_custom_call", output_to_operand_aliasing={{2}: (4, {}), {3}: (5, {}), {4}: (6, {}), {5}: (7, {})} | custom-call | flops 5000000000 | bytes 1048576 | tf_op jit(solution)/shard_map/pallas_call | solution.py:557
  121.6 2.5 %shard_map.236 = (bf16[128,1024]{1,0:T(8,128)(2,1)S(1)}, bf16[512,1024]{1,0:T(8,128)(2,1)S(1)}, bf16[512,704]{1,0:T(8,128)(2,1)S(1)}, bf16[512,704]{1,0:T(8,128)(2,1)S(1)}, bf16[512,704]{1,0:T(8,128)(2,1)S(1)}) custom-call(bf16[128,1024]{1,0:T(8,128)(2,1)S(1)} %collective-permute-done.19.refs, ...), custom_call_target="tpu_custom_call", output_to_operand_aliasing={{1}: (3, {}), {2}: (4, {}), {3}: (5, {}), {4}: (6, {})} | custom-call | flops 2500000000 | bytes 1048576 | tf_op jit(solution)/shard_map/pallas_call | solution.py:557
  128.5 2.2 pad_maximum_fusion
  130.7 3.4 %convolution_convert_fusion.3 = bf16[512,1024]{1,0:T(8,128)(2,1)} fusion(bf16[512,704]{1,0:T(8,128)(2,1)S(1)} %get-tuple-element.148, bf16[704,3072]{1,0:T(8,128)(2,1)} %all-gather.2.cloned.1.call-done.refs_2_.refs_3_), kind=kOutput, calls=%fused_computation.5 | convolution fusion | flops 738721792 | bytes 3211264 | tf_op jit(solution)/shard_map/dot_general | solution.py:40
  136.6 13.0 %all_to_all.15.refs_0_ = bf16[16,64,128]{2,1,0:T(8,128)(2,1)} all-to-all(bf16[16,64,128]{2,1,0:T(8,128)(2,1)S(1)} %bitcast.91), channel_id=1, replica_groups=mesh['x'=2,'c'=2,'z'=4,'y'=2,'r'=1] {'x','y','z'}, dimensions={0} | all-to-all | bytes 524288 | tf_op jit(solution)/shard_map/all_to_all | solution.py:755
  154.0 2.4 collective-permute-start.23
  156.4 18.0 %shard_map.237 = (f32[2048,128]{1,0:T(8,128)}, bf16[2048,128]{1,0:T(8,128)(2,1)}, bf16[16,64,128]{2,1,0:T(8,128)(2,1)}, f32[8,128]{1,0:T(8,128)}) custom-call(s32[5]{0:T(128)} %stack.35.coords, s32[16]{0:T(128)} %convert_reduce_fusion.cuts, f32[8,256]{1,0:T(8,128)} %pad.18.hvec, bf16[16,64,128]{2,1,0:T(8,128)(2,1)} %all_to_all.15.refs_0_, ...), custom_call_target="tpu_custom_call" | custom-call | flops 23000000512 | bytes 1048576 | tf_op jit(solution)/shard_map/pallas_call | solution.py:83
  175.4 3.5 %collective-permute-done.23 = bf16[288,1024]{1,0:T(8,128)(2,1)} collective-permute-done((bf16[288,1024]{1,0:T(8,128)(2,1)}, bf16[288,1024]{1,0:T(8,128)(2,1)}, u32[]{:S(2)}, u32[]{:S(2)}) %collective-permute-start.23) | collective-permute-done | bytes 589856 | tf_op jit(solution)/shard_map/ppermute | solution.py:49
  190.9 2.6 %shard_map.238 = (bf16[4,128,1024]{2,1,0:T(8,128)(2,1)}, f32[8,1024]{1,0:T(8,128)S(1)}, bf16[512,512]{1,0:T(8,128)(2,1)S(1)}, bf16[256,512]{1,0:T(8,128)(2,1)S(1)}) custom-call(s32[5]{0:T(128)S(1)} %copy-done, bf16[768,128]{1,0:T(8,128)(2,1)S(1)} %pad_maximum_fusion.10.refs_0_, bf16[768,128]{1,0:T(8,128)(2,1)S(1)} %collective-permute-done.25.refs_1_, ...), custom_call_target="tpu_custom_call" | custom-call | flops 4600000000 | bytes 1048576 | tf_op jit(solution)/shard_map/pallas_call | solution.py:83
  195.0 3.5 %all-to-all-start.2 = ((bf16[4,128,1024]{2,1,0:T(8,128)(2,1)}), bf16[4,128,1024]{2,1,0:T(8,128)(2,1)S(1)}, u32[]{:S(2)}, u32[]{:S(2)}) async-start(bf16[4,128,1024]{2,1,0:T(8,128)(2,1)} %get-tuple-element.184), calls=%async_computation.2 | async-start | bytes 2097152 | tf_op jit(solution)/shard_map/all_to_all | solution.py:832
  198.6 4.1 %shard_map.239 = (bf16[4,32,3072]{2,1,0:T(8,128)(2,1)}, bf16[4,32,3072]{2,1,0:T(8,128)(2,1)}) custom-call(s32[5]{0:T(128)} %stack.35.coords, bf16[512,512]{1,0:T(8,128)(2,1)} %copy-done.7, bf16[256,512]{1,0:T(8,128)(2,1)} %copy-done.8, bf16[512,1024]{1,0:T(8,128)(2,1)} %get-tuple-element.182.refs_4_.rows_all), custom_call_target="tpu_custom_call" | custom-call | flops 4600000000 | bytes 1048576 | tf_op jit(solution)/shard_map/pallas_call | solution.py:83
  208.9 2.1 fusion.29
  215.0 6.6 %all-to-all-done.2.refs_0_ = bf16[4,128,1024]{2,1,0:T(8,128)(2,1)S(1)} async-done(((bf16[4,128,1024]{2,1,0:T(8,128)(2,1)}), bf16[4,128,1024]{2,1,0:T(8,128)(2,1)S(1)}, u32[]{:S(2)}, u32[]{:S(2)}) %all-to-all-start.2) | async-done | bytes 1048608 | tf_op jit(solution)/shard_map/all_to_all | solution.py:832
  223.3 3.8 %collective-permute-start.39 = (bf16[40,1024]{1,0:T(8,128)(2,1)S(1)}, bf16[40,1024]{1,0:T(8,128)(2,1)S(1)}, u32[]{:S(2)}, u32[]{:S(2)}) collective-permute-start(bf16[40,1024]{1,0:T(8,128)(2,1)S(1)} %get-tuple-element.281), channel_id=1, source_target_pairs={{0,6},{2,4},{4,2},{6,0},{1,7},{3,5},{5,3},{7,1},{8,14},{10,12},{12... | collective-permute-start | bytes 245768 | tf_op jit(solution)/shard_map/ppermute | solution.py:49
  229.7 3.3 %collective-permute-done.38 = bf16[40,1024]{1,0:T(8,128)(2,1)S(1)} collective-permute-done((bf16[40,1024]{1,0:T(8,128)(2,1)S(1)}, bf16[40,1024]{1,0:T(8,128)(2,1)S(1)}, u32[]{:S(2)}, u32[]{:S(2)}) %collective-permute-start.38) | collective-permute-done | bytes 81952 | tf_op jit(solution)/shard_map/ppermute | solution.py:49
  (260 shorter events, 69.6 us)
Async XLA Ops:
  7.2 103.7 %all-gather.2.cloned.1.call-start = ((), (), s32[]{:S(2)}) async-start(), calls=%async_computation.4 | async-start | bytes 4866048 | tf_op jit(solution)/shard_map/all_gather | solution.py:660
  9.6 18.4 %collective-permute-start = (bf16[160,1024]{1,0:T(8,128)(2,1)}, bf16[160,1024]{1,0:T(8,128)(2,1)S(1)}, u32[]{:S(2)}, u32[]{:S(2)}) collective-permute-start(bf16[160,1024]{1,0:T(8,128)(2,1)} %get-tuple-element.111.refs_0_), channel_id=1, source_target_pairs={{0,2},{2,0},{4,6},{6,4},{1,3},{3,1},{5,7},{7,5},{8,10},{10,8},{12,... | collective-permute-start | bytes 983048 | tf_op jit(solution)/shard_map/ppermute | solution.py:49
  12.6 24.5 %collective-permute-start.1 = (bf16[160,1024]{1,0:T(8,128)(2,1)}, bf16[160,1024]{1,0:T(8,128)(2,1)S(1)}, u32[]{:S(2)}, u32[]{:S(2)}) collective-permute-start(bf16[160,1024]{1,0:T(8,128)(2,1)} %get-tuple-element.111.refs_0_), channel_id=1, source_target_pairs={{0,4},{2,6},{4,0},{6,2},{1,5},{3,7},{5,1},{7,3},{8,12},{10,14},{12... | collective-permute-start | bytes 983048 | tf_op jit(solution)/shard_map/ppermute | solution.py:49
  15.2 11.2 %collective-permute-start.3 = (bf16[32,3072]{1,0:T(8,128)(2,1)}, bf16[32,3072]{1,0:T(8,128)(2,1)S(1)}, u32[]{:S(2)}, u32[]{:S(2)}) collective-permute-start(bf16[32,3072]{1,0:T(8,128)(2,1)} %get-tuple-element.115.refs_4_), channel_id=1, source_target_pairs={{0,1},{1,0},{16,17},{17,16},{2,3},{3,2},{18,19},{19,18},{4,5},{5,4... | collective-permute-start | bytes 589832 | tf_op jit(solution)/shard_map/ppermute | solution.py:49
  16.7 9.7 %collective-permute-start.4 = (bf16[32,3072]{1,0:T(8,128)(2,1)}, bf16[32,3072]{1,0:T(8,128)(2,1)S(1)}, u32[]{:S(2)}, u32[]{:S(2)}) collective-permute-start(bf16[32,3072]{1,0:T(8,128)(2,1)} %get-tuple-element.115.refs_4_), channel_id=1, source_target_pairs={{0,16},{1,17},{16,0},{17,1},{2,18},{3,19},{18,2},{19,3},{4,20},{5,... | collective-permute-start | bytes 589832 | tf_op jit(solution)/shard_map/ppermute | solution.py:49
  18.2 8.7 %collective-permute-start.5 = (bf16[32,3072]{1,0:T(8,128)(2,1)}, bf16[32,3072]{1,0:T(8,128)(2,1)S(1)}, u32[]{:S(2)}, u32[]{:S(2)}) collective-permute-start(bf16[32,3072]{1,0:T(8,128)(2,1)} %get-tuple-element.115.refs_4_), channel_id=1, source_target_pairs={{0,17},{1,16},{16,1},{17,0},{2,19},{3,18},{18,3},{19,2},{4,21},{5,... | collective-permute-start | bytes 589832 | tf_op jit(solution)/shard_map/ppermute | solution.py:49
  26.4 10.7 %collective-permute-start.2 = (bf16[160,1024]{1,0:T(8,128)(2,1)}, bf16[160,1024]{1,0:T(8,128)(2,1)S(1)}, u32[]{:S(2)}, u32[]{:S(2)}) collective-permute-start(bf16[160,1024]{1,0:T(8,128)(2,1)} %get-tuple-element.111.refs_0_), channel_id=1, source_target_pairs={{0,6},{2,4},{4,2},{6,0},{1,7},{3,5},{5,3},{7,1},{8,14},{10,12},{12... | collective-permute-start | bytes 983048 | tf_op jit(solution)/shard_map/ppermute | solution.py:49
  27.9 10.6 %collective-permute-start.6 = (bf16[128,3072]{1,0:T(8,128)(2,1)S(1)}, bf16[128,3072]{1,0:T(8,128)(2,1)S(1)}, u32[]{:S(2)}, u32[]{:S(2)}) collective-permute-start(bf16[128,3072]{1,0:T(8,128)(2,1)S(1)} %pad_maximum_fusion.7), channel_id=1, source_target_pairs={{0,8},{8,0},{1,9},{9,1},{2,10},{10,2},{3,11},{11,3},{4,12},{12,4},... | collective-permute-start | bytes 2359304 | tf_op jit(solution)/shard_map/ppermute | solution.py:49
  43.8 7.7 %collective-permute-start.9 = (bf16[768,128]{1,0:T(8,128)(2,1)}, bf16[768,128]{1,0:T(8,128)(2,1)S(1)}, u32[]{:S(2)}, u32[]{:S(2)}) collective-permute-start(bf16[768,128]{1,0:T(8,128)(2,1)} %get-tuple-element.120), channel_id=1, source_target_pairs={{0,17},{1,16},{16,1},{17,0},{2,19},{3,18},{18,3},{19,2},{4,21},{5,... | collective-permute-start | bytes 589832 | tf_op jit(solution)/shard_map/ppermute | solution.py:49
  53.8 30.8 %collective-permute-start.10 = (bf16[256,1024]{1,0:T(8,128)(2,1)S(1)}, bf16[256,1024]{1,0:T(8,128)(2,1)S(1)}, u32[]{:S(2)}, u32[]{:S(2)}) collective-permute-start(bf16[256,1024]{1,0:T(8,128)(2,1)S(1)} %copy-done.22), channel_id=1, source_target_pairs={{0,1},{1,0},{16,17},{17,16},{2,3},{3,2},{18,19},{19,18},{4,5},{5,4... | collective-permute-start | bytes 1572872 | tf_op jit(solution)/shard_map/ppermute | solution.py:49
  55.3 29.3 %collective-permute-start.11 = (bf16[256,1024]{1,0:T(8,128)(2,1)S(1)}, bf16[256,1024]{1,0:T(8,128)(2,1)S(1)}, u32[]{:S(2)}, u32[]{:S(2)}) collective-permute-start(bf16[256,1024]{1,0:T(8,128)(2,1)S(1)} %copy-done.22), channel_id=1, source_target_pairs={{0,16},{1,17},{16,0},{17,1},{2,18},{3,19},{18,2},{19,3},{4,20},{5,... | collective-permute-start | bytes 1572872 | tf_op jit(solution)/shard_map/ppermute | solution.py:49
  56.8 27.9 %collective-permute-start.12 = (bf16[256,1024]{1,0:T(8,128)(2,1)S(1)}, bf16[256,1024]{1,0:T(8,128)(2,1)S(1)}, u32[]{:S(2)}, u32[]{:S(2)}) collective-permute-start(bf16[256,1024]{1,0:T(8,128)(2,1)S(1)} %copy-done.22), channel_id=1, source_target_pairs={{0,17},{1,16},{16,1},{17,0},{2,19},{3,18},{18,3},{19,2},{4,21},{5,... | collective-permute-start | bytes 1572872 | tf_op jit(solution)/shard_map/ppermute | solution.py:49
  71.3 26.5 %all-to-all-start = ((bf16[16,64,128]{2,1,0:T(8,128)(2,1)}), bf16[16,64,128]{2,1,0:T(8,128)(2,1)S(1)}, u32[]{:S(2)}, u32[]{:S(2)}) async-start(bf16[16,64,128]{2,1,0:T(8,128)(2,1)} %get-tuple-element.124), calls=%async_computation | async-start | bytes 524288 | tf_op jit(solution)/shard_map/all_to_all | solution.py:710
  84.4 118.3 %reduce-scatter.2.cloned.1.call-start = ((), (), s32[]{:S(2)}) async-start(), calls=%async_computation.5 | async-start | bytes 4866048 | tf_op jit(solution)/shard_map/reduce_scatter | solution.py:765
  106.2 10.3 %collective-permute-start.15 = (bf16[128,1024]{1,0:T(8,128)(2,1)}, bf16[128,1024]{1,0:T(8,128)(2,1)S(1)}, u32[]{:S(2)}, u32[]{:S(2)}) collective-permute-start(bf16[128,1024]{1,0:T(8,128)(2,1)} %get-tuple-element.131.refs_0_), channel_id=1, source_target_pairs={{0,1},{1,0},{16,17},{17,16},{2,3},{3,2},{18,19},{19,18},{4,5},{5,4... | collective-permute-start | bytes 786440 | tf_op jit(solution)/shard_map/ppermute | solution.py:49
  106.2 10.3 %collective-permute-start.16 = (bf16[128,1024]{1,0:T(8,128)(2,1)}, bf16[128,1024]{1,0:T(8,128)(2,1)S(1)}, u32[]{:S(2)}, u32[]{:S(2)}) collective-permute-start(bf16[128,1024]{1,0:T(8,128)(2,1)} %get-tuple-element.131.refs_0_), channel_id=1, source_target_pairs={{0,16},{1,17},{16,0},{17,1},{2,18},{3,19},{18,2},{19,3},{4,20},{5,... | collective-permute-start | bytes 786440 | tf_op jit(solution)/shard_map/ppermute | solution.py:49
  107.3 14.2 %collective-permute-start.19 = (bf16[128,1024]{1,0:T(8,128)(2,1)}, bf16[128,1024]{1,0:T(8,128)(2,1)S(1)}, u32[]{:S(2)}, u32[]{:S(2)}) collective-permute-start(bf16[128,1024]{1,0:T(8,128)(2,1)} %get-tuple-element.131.refs_0_), channel_id=1, source_target_pairs={{0,17},{1,16},{16,1},{17,0},{2,19},{3,18},{18,3},{19,2},{4,21},{5,... | collective-permute-start | bytes 786440 | tf_op jit(solution)/shard_map/ppermute | solution.py:49
  119.5 14.6 %collective-permute-start.17 = (bf16[128,1024]{1,0:T(8,128)(2,1)S(1)}, bf16[128,1024]{1,0:T(8,128)(2,1)S(1)}, u32[]{:S(2)}, u32[]{:S(2)}) collective-permute-start(bf16[128,1024]{1,0:T(8,128)(2,1)S(1)} %get-tuple-element.138), channel_id=1, source_target_pairs={{0,1},{1,0},{16,17},{17,16},{2,3},{3,2},{18,19},{19,18},{4,5},{5,4... | collective-permute-start | bytes 786440 | tf_op jit(solution)/shard_map/ppermute | solution.py:49
  120.7 13.4 %collective-permute-start.18 = (bf16[128,1024]{1,0:T(8,128)(2,1)S(1)}, bf16[128,1024]{1,0:T(8,128)(2,1)}, u32[]{:S(2)}, u32[]{:S(2)}) collective-permute-start(bf16[128,1024]{1,0:T(8,128)(2,1)S(1)} %get-tuple-element.139), channel_id=1, source_target_pairs={{0,16},{1,17},{16,0},{17,1},{2,18},{3,19},{18,2},{19,3},{4,20},{5,... | collective-permute-start | bytes 786440 | tf_op jit(solution)/shard_map/ppermute | solution.py:49
  124.0 10.1 %collective-permute-start.20 = (bf16[128,1024]{1,0:T(8,128)(2,1)S(1)}, bf16[128,1024]{1,0:T(8,128)(2,1)S(1)}, u32[]{:S(2)}, u32[]{:S(2)}) collective-permute-start(bf16[128,1024]{1,0:T(8,128)(2,1)S(1)} %get-tuple-element.144), channel_id=1, source_target_pairs={{0,17},{1,16},{16,1},{17,0},{2,19},{3,18},{18,3},{19,2},{4,21},{5,... | collective-permute-start | bytes 786440 | tf_op jit(solution)/shard_map/ppermute | solution.py:49
  152.9 22.5 %collective-permute-start.21 = (bf16[288,1024]{1,0:T(8,128)(2,1)}, bf16[288,1024]{1,0:T(8,128)(2,1)S(1)}, u32[]{:S(2)}, u32[]{:S(2)}) collective-permute-start(bf16[288,1024]{1,0:T(8,128)(2,1)} %get-tuple-element.269), channel_id=1, source_target_pairs={{0,1},{1,0},{16,17},{17,16},{2,3},{3,2},{18,19},{19,18},{4,5},{5,4... | collective-permute-start | bytes 1769480 | tf_op jit(solution)/shard_map/ppermute | solution.py:49
  152.9 22.5 %collective-permute-start.22 = (bf16[288,1024]{1,0:T(8,128)(2,1)}, bf16[288,1024]{1,0:T(8,128)(2,1)S(1)}, u32[]{:S(2)}, u32[]{:S(2)}) collective-permute-start(bf16[288,1024]{1,0:T(8,128)(2,1)} %get-tuple-element.270), channel_id=1, source_target_pairs={{0,16},{1,17},{16,0},{17,1},{2,18},{3,19},{18,2},{19,3},{4,20},{5,... | collective-permute-start | bytes 1769480 | tf_op jit(solution)/shard_map/ppermute | solution.py:49
  154.0 25.0 %collective-permute-start.23 = (bf16[288,1024]{1,0:T(8,128)(2,1)}, bf16[288,1024]{1,0:T(8,128)(2,1)}, u32[]{:S(2)}, u32[]{:S(2)}) collective-permute-start(bf16[288,1024]{1,0:T(8,128)(2,1)} %get-tuple-element.268), channel_id=1, source_target_pairs={{0,17},{1,16},{16,1},{17,0},{2,19},{3,18},{18,3},{19,2},{4,21},{5,... | collective-permute-start | bytes 1769480 | tf_op jit(solution)/shard_map/ppermute | solution.py:49
  180.5 9.7 %collective-permute-start.25 = (bf16[768,128]{1,0:T(8,128)(2,1)S(1)}, bf16[768,128]{1,0:T(8,128)(2,1)S(1)}, u32[]{:S(2)}, u32[]{:S(2)}) collective-permute-start(bf16[768,128]{1,0:T(8,128)(2,1)S(1)} %pad_maximum_fusion.11), channel_id=1, source_target_pairs={{0,1},{1,0},{16,17},{17,16},{2,3},{3,2},{18,19},{19,18},{4,5},{5,4... | collective-permute-start | bytes 589832 | tf_op jit(solution)/shard_map/ppermute | solution.py:49
  180.9 9.4 %collective-permute-start.26 = (bf16[768,128]{1,0:T(8,128)(2,1)S(1)}, bf16[768,128]{1,0:T(8,128)(2,1)S(1)}, u32[]{:S(2)}, u32[]{:S(2)}) collective-permute-start(bf16[768,128]{1,0:T(8,128)(2,1)S(1)} %pad_maximum_fusion.12), channel_id=1, source_target_pairs={{0,16},{1,17},{16,0},{17,1},{2,18},{3,19},{18,2},{19,3},{4,20},{5,... | collective-permute-start | bytes 589832 | tf_op jit(solution)/shard_map/ppermute | solution.py:49
  182.1 8.4 %collective-permute-start.27 = (bf16[768,128]{1,0:T(8,128)(2,1)S(1)}, bf16[768,128]{1,0:T(8,128)(2,1)S(1)}, u32[]{:S(2)}, u32[]{:S(2)}) collective-permute-start(bf16[768,128]{1,0:T(8,128)(2,1)S(1)} %pad_maximum_fusion.13), channel_id=1, source_target_pairs={{0,17},{1,16},{16,1},{17,0},{2,19},{3,18},{18,3},{19,2},{4,21},{5,... | collective-permute-start | bytes 589832 | tf_op jit(solution)/shard_map/ppermute | solution.py:49
  195.0 26.5 %all-to-all-start.2 = ((bf16[4,128,1024]{2,1,0:T(8,128)(2,1)}), bf16[4,128,1024]{2,1,0:T(8,128)(2,1)S(1)}, u32[]{:S(2)}, u32[]{:S(2)}) async-start(bf16[4,128,1024]{2,1,0:T(8,128)(2,1)} %get-tuple-element.184), calls=%async_computation.2 | async-start | bytes 2097152 | tf_op jit(solution)/shard_map/all_to_all | solution.py:832
  202.7 8.4 %collective-permute-start.28 = (bf16[4,32,3072]{2,1,0:T(8,128)(2,1)}, bf16[4,32,3072]{2,1,0:T(8,128)(2,1)S(1)}, u32[]{:S(2)}, u32[]{:S(2)}) collective-permute-start(bf16[4,32,3072]{2,1,0:T(8,128)(2,1)} %get-tuple-element.192), channel_id=1, source_target_pairs={{0,8},{8,0},{1,9},{9,1},{2,10},{10,2},{3,11},{11,3},{4,12},{12,4},... | collective-permute-start | bytes 2359304 | tf_op jit(solution)/shard_map/ppermute | solution.py:49
  205.2 9.7 %collective-permute-start.36 = (bf16[4,32,1024]{2,1,0:T(8,128)(2,1)S(1)}, bf16[4,32,1024]{2,1,0:T(8,128)(2,1)S(1)}, u32[]{:S(2)}, u32[]{:S(2)}) collective-permute-start(bf16[4,32,1024]{2,1,0:T(8,128)(2,1)S(1)} %bitcast.99), channel_id=1, source_target_pairs={{0,8},{8,0},{1,9},{9,1},{2,10},{10,2},{3,11},{11,3},{4,12},{12,4},... | collective-permute-start | bytes 786440 | tf_op jit(solution)/shard_map/ppermute | solution.py:49
  211.3 10.2 %collective-permute-start.29 = (bf16[32,3072]{1,0:T(8,128)(2,1)S(1)}, bf16[32,3072]{1,0:T(8,128)(2,1)S(1)}, u32[]{:S(2)}, u32[]{:S(2)}) collective-permute-start(bf16[32,3072]{1,0:T(8,128)(2,1)S(1)} %get-tuple-element.238), channel_id=1, source_target_pairs={{0,1},{1,0},{16,17},{17,16},{2,3},{3,2},{18,19},{19,18},{4,5},{5,4... | collective-permute-start | bytes 589832 | tf_op jit(solution)/shard_map/ppermute | solution.py:49
  212.9 8.6 %collective-permute-start.30 = (bf16[32,3072]{1,0:T(8,128)(2,1)S(1)}, bf16[32,3072]{1,0:T(8,128)(2,1)S(1)}, u32[]{:S(2)}, u32[]{:S(2)}) collective-permute-start(bf16[32,3072]{1,0:T(8,128)(2,1)S(1)} %get-tuple-element.237), channel_id=1, source_target_pairs={{0,16},{1,17},{16,0},{17,1},{2,18},{3,19},{18,2},{19,3},{4,20},{5,... | collective-permute-start | bytes 589832 | tf_op jit(solution)/shard_map/ppermute | solution.py:49
  213.5 9.7 %collective-permute-start.31 = (bf16[32,3072]{1,0:T(8,128)(2,1)S(1)}, bf16[32,3072]{1,0:T(8,128)(2,1)S(1)}, u32[]{:S(2)}, u32[]{:S(2)}) collective-permute-start(bf16[32,3072]{1,0:T(8,128)(2,1)S(1)} %get-tuple-element.236), channel_id=1, source_target_pairs={{0,17},{1,16},{16,1},{17,0},{2,19},{3,18},{18,3},{19,2},{4,21},{5,... | collective-permute-start | bytes 589832 | tf_op jit(solution)/shard_map/ppermute | solution.py:49
  (53 other events, 236.0 us)
Sparse Core Ops, SparseCore 0:
  37.2 59.2 all-gather.1
  149.7 48.4 reduce-scatter.1

commit v4 on v3

--- a/solution.py
+++ b/solution.py
@@ -798,7 +798,7 @@
             pltpu.VMEM((2, hd, 2 * tokens), F32),
         ],
         scalars=2,
-        micros=20,
+        micros=40,
     )
     mixed, grad_own = lax.optimization_barrier((mixed, grad_own))
     grad_pairs = (grad_own + swap(grad_other, "c", 1).astype(F32)).astype(BF16)

time: 243 us -> 243 us (level)
  blocking collectives: 13 us -> 0 us
  waiting for transfers between devices: 45.8 us -> 53.5 us
  starting transfers between devices: 59.4 us -> 62.7 us
    all_to_all x1 -> x0, blocking collectives: 13 us -> none  [body(): lax.all_to_all(grad_attended.reshape(16, hd, tokens), ('x', 'y', 'z'), sp...]
    all_to_all x0 -> x1, waiting for transfers between devices: none -> 7.68 us  [body(): lax.all_to_all(grad_attended.reshape(16, hd, tokens), ('x', 'y', 'z'), sp...]
    all_to_all x0 -> x1, starting transfers between devices: none -> 3.53 us  [body(): lax.all_to_all(grad_attended.reshape(16, hd, tokens), ('x', 'y', 'z'), sp...]
    unnamed x97 -> x99, local copies, waits for them, and re-layouts: 12.1 us -> 12.8 us
  transfers between devices with their start and end apart: 44 -> 45, of which waited for: 13 -> 14; matrix products, arithmetic and copies ran while one was open for 15% -> 15% of each run, Pallas kernels for 23% -> 23%
where the time goes in v4:
time: 243 us; the launch traced here: 241 us
  starting transfers between devices  62.7 us (26%)
  Pallas kernels  58 us (24%)
  waiting for transfers between devices  53.5 us (22%)
  local copies, waits for them, and re-layouts  24.9 us (10%)
  other arithmetic  17.6 us (7%)
  between operations  15 us (6%)
  matrix products  9.68 us (4%)
    pallas_call x8, Pallas kernels, kernel_call(): pl.pallas_call(body, out_shape=out_shapes, in_specs=in_specs, out_specs=j...  49.5 us
    ppermute x40, starting transfers between devices, swap(): return lax.ppermute(value, axis, [(at, at ^ mask) for at in range(size)])  42.5 us
    ppermute x40, waiting for transfers between devices, swap(): return lax.ppermute(value, axis, [(at, at ^ mask) for at in range(size)])  26 us
    all_to_all x1, waiting for transfers between devices, body(): lax.all_to_all(out_t, ('x', 'y', 'z'), split_axis=0, concat_axis=0, tiled...  13.3 us
    all_to_all x1, starting transfers between devices, body(): lax.all_to_all(out_t, ('x', 'y', 'z'), split_axis=0, concat_axis=0, tiled...  13.1 us
    unnamed x99, local copies, waits for them, and re-layouts  12.8 us
    pallas_call x3, Pallas kernels, feed_call(): pl.pallas_call(functools.partial(feed_body, count), grid=(1,), in_specs=[...  7.89 us
    all_to_all x1, waiting for transfers between devices, body(): lax.all_to_all(grad_attended.reshape(16, hd, tokens), ('x', 'y', 'z'), sp...  7.68 us
  transfers between devices with their start and end apart: 45, of which 14 were waited for; matrix products, arithmetic and copies ran while one was open for 15% of the time, Pallas kernels for 23%

profile of v4, /device:TPU:0, one launch (start us, length us, event | category | flops | bytes accessed | tf_op | source)
XLA Modules:
  0.0 241.4 jit_solution(16151653248827743687)
XLA Ops:
  7.2 2.3 shard_map.229
  9.6 3.0 %collective-permute-start = (bf16[160,1024]{1,0:T(8,128)(2,1)}, bf16[160,1024]{1,0:T(8,128)(2,1)S(1)}, u32[]{:S(2)}, u32[]{:S(2)}) collective-permute-start(bf16[160,1024]{1,0:T(8,128)(2,1)} %get-tuple-element.111.refs_0_), channel_id=1, source_target_pairs={{0,2},{2,0},{4,6},{6,4},{1,3},{3,1},{5,7},{7,5},{8,10},{10,8},{12,... | collective-permute-start | bytes 983048 | tf_op jit(solution)/shard_map/ppermute | solution.py:49
  12.6 2.6 %collective-permute-start.1 = (bf16[160,1024]{1,0:T(8,128)(2,1)}, bf16[160,1024]{1,0:T(8,128)(2,1)S(1)}, u32[]{:S(2)}, u32[]{:S(2)}) collective-permute-start(bf16[160,1024]{1,0:T(8,128)(2,1)} %get-tuple-element.111.refs_0_), channel_id=1, source_target_pairs={{0,4},{2,6},{4,0},{6,2},{1,5},{3,7},{5,1},{7,3},{8,12},{10,14},{12... | collective-permute-start | bytes 983048 | tf_op jit(solution)/shard_map/ppermute | solution.py:49
  28.0 9.0 %collective-permute-done.1.refs_2_ = bf16[160,1024]{1,0:T(8,128)(2,1)S(1)} collective-permute-done((bf16[160,1024]{1,0:T(8,128)(2,1)}, bf16[160,1024]{1,0:T(8,128)(2,1)S(1)}, u32[]{:S(2)}, u32[]{:S(2)}) %collective-permute-start.1) | collective-permute-done | bytes 327712 | tf_op jit(solution)/shard_map/ppermute | solution.py:49
  39.4 4.4 %shard_map.231 = (bf16[768,128]{1,0:T(8,128)(2,1)}, bf16[768,128]{1,0:T(8,128)(2,1)}, bf16[768,128]{1,0:T(8,128)(2,1)}, bf16[768,128]{1,0:T(8,128)(2,1)}, bf16[5...) custom-call(s32[5]{0:T(128)} %stack.35.coords, ...), custom_call_target="tpu_custom_call" | custom-call | flops 4600000000 | bytes 1048576 | tf_op jit(solution)/shard_map/pallas_call | solution.py:83
  43.9 2.5 %collective-permute-start.9 = (bf16[768,128]{1,0:T(8,128)(2,1)}, bf16[768,128]{1,0:T(8,128)(2,1)S(1)}, u32[]{:S(2)}, u32[]{:S(2)}) collective-permute-start(bf16[768,128]{1,0:T(8,128)(2,1)} %get-tuple-element.120), channel_id=1, source_target_pairs={{0,17},{1,16},{16,1},{17,0},{2,19},{3,18},{18,3},{19,2},{4,21},{5,... | collective-permute-start | bytes 589832 | tf_op jit(solution)/shard_map/ppermute | solution.py:49
  48.3 3.2 %collective-permute-done.9.refs_3_ = bf16[768,128]{1,0:T(8,128)(2,1)S(1)} collective-permute-done((bf16[768,128]{1,0:T(8,128)(2,1)}, bf16[768,128]{1,0:T(8,128)(2,1)S(1)}, u32[]{:S(2)}, u32[]{:S(2)}) %collective-permute-start.9) | collective-permute-done | bytes 196640 | tf_op jit(solution)/shard_map/ppermute | solution.py:49
  51.5 2.1 collective-permute-done.8.refs_2_
  58.2 13.0 %shard_map.232 = (bf16[16,64,128]{2,1,0:T(8,128)(2,1)}, f32[8,8,256]{2,1,0:T(8,128)}, f32[8,64,256]{2,1,0:T(8,128)}, bf16[4096,128]{1,0:T(8,128)(2,1)}, bf16[8,1...) custom-call(s32[5]{0:T(128)} %stack.35.coords, s32[16]{0:T(128)} %convert_reduce_fusion.cuts, f32[8,256]{1,0:T(8,128)} %pad.18.hvec, ...), custom_call_target="tpu_custom_call" | custom-call | flops 23000000512 | bytes 1048576 | tf_op jit(solution)/shard_map/pallas_call | solution.py:83
  71.3 13.1 %all-to-all-start = ((bf16[16,64,128]{2,1,0:T(8,128)(2,1)}), bf16[16,64,128]{2,1,0:T(8,128)(2,1)S(1)}, u32[]{:S(2)}, u32[]{:S(2)}) async-start(bf16[16,64,128]{2,1,0:T(8,128)(2,1)} %get-tuple-element.124), calls=%async_computation | async-start | bytes 524288 | tf_op jit(solution)/shard_map/all_to_all | solution.py:710
  84.4 13.3 %all-to-all-done = bf16[16,64,128]{2,1,0:T(8,128)(2,1)S(1)} async-done(((bf16[16,64,128]{2,1,0:T(8,128)(2,1)}), bf16[16,64,128]{2,1,0:T(8,128)(2,1)S(1)}, u32[]{:S(2)}, u32[]{:S(2)}) %all-to-all-start) | async-done | bytes 262176 | tf_op jit(solution)/shard_map/all_to_all | solution.py:710
  99.2 2.0 collective-permute-done.14.refs_4_
  102.3 3.9 %shard_map.233 = (f32[128,1024]{1,0:T(8,128)}, bf16[128,1024]{1,0:T(8,128)(2,1)}, bf16[1024,1024]{1,0:T(8,128)(2,1)}, bf16[4,32,1024]{2,1,0:T(8,128)(2,1)}) custom-call(s32[5]{0:T(128)} %stack.35.coords, bf16[1024,128]{1,0:T(8,128)(2,1)} %bitcast.97, bf16[128,1024]{1,0:T(8,128)(2,1)} %bitcast.86, f32[1,1024]{1,0:T(1,128)} %bitcast.104, ...), custom_call_target="tpu_custom_call" | custom-call | flops 4600000000 | bytes 1048576 | tf_op jit(solution)/shard_map/pallas_call | solution.py:83
  107.3 2.4 collective-permute-start.19
  110.9 2.2 copy-done.1
  114.1 2.5 %shard_map.234 = (bf16[128,1024]{1,0:T(8,128)(2,1)S(1)}, bf16[512,1024]{1,0:T(8,128)(2,1)S(1)}, bf16[512,704]{1,0:T(8,128)(2,1)S(1)}, bf16[512,704]{1,0:T(8,128)(2,1)S(1)}, bf16[512,704]{1,0:T(8,128)(2,1)S(1)}) custom-call(bf16[128,1024]{1,0:T(8,128)(2,1)S(1)} %copy-done.3, bf16[512,1024]{1,0:T(8,128)(2,1)S(1)} %pad_maximum_fusion.2.refs_1_.refs_2_, ...), custom_call_target="tpu_custom_call" | custom-call | flops 2500000000 | bytes 1048576 | tf_op jit(solution)/shard_map/pallas_call | solution.py:557
  116.5 3.0 %shard_map.235 = (bf16[128,1024]{1,0:T(8,128)(2,1)S(1)}, bf16[128,1024]{1,0:T(8,128)(2,1)S(1)}, bf16[512,1024]{1,0:T(8,128)(2,1)S(1)}, bf16[512,704]{1,0:T(8,128...) custom-call(bf16[128,1024]{1,0:T(8,128)(2,1)S(1)} %collective-permut, ...), custom_call_target="tpu_custom_call", output_to_operand_aliasing={{2}: (4, {}), {3}: (5, {}), {4}: (6, {}), {5}: (7, {})} | custom-call | flops 5000000000 | bytes 1048576 | tf_op jit(solution)/shard_map/pallas_call | solution.py:557
  121.6 2.5 %shard_map.236 = (bf16[128,1024]{1,0:T(8,128)(2,1)S(1)}, bf16[512,1024]{1,0:T(8,128)(2,1)S(1)}, bf16[512,704]{1,0:T(8,128)(2,1)S(1)}, bf16[512,704]{1,0:T(8,128)(2,1)S(1)}, bf16[512,704]{1,0:T(8,128)(2,1)S(1)}) custom-call(bf16[128,1024]{1,0:T(8,128)(2,1)S(1)} %collective-permute-done.19.refs, ...), custom_call_target="tpu_custom_call", output_to_operand_aliasing={{1}: (3, {}), {2}: (4, {}), {3}: (5, {}), {4}: (6, {})} | custom-call | flops 2500000000 | bytes 1048576 | tf_op jit(solution)/shard_map/pallas_call | solution.py:557
  128.5 2.2 pad_maximum_fusion
  130.7 3.4 %convolution_convert_fusion.3 = bf16[512,1024]{1,0:T(8,128)(2,1)} fusion(bf16[512,704]{1,0:T(8,128)(2,1)S(1)} %get-tuple-element.148, bf16[704,3072]{1,0:T(8,128)(2,1)} %all-gather.2.cloned.1.call-done.refs_2_.refs_3_), kind=kOutput, calls=%fused_computation.5 | convolution fusion | flops 738721792 | bytes 3211264 | tf_op jit(solution)/shard_map/dot_general | solution.py:40
  137.3 3.5 %all-to-all-start.1 = ((bf16[16,64,128]{2,1,0:T(8,128)(2,1)}), bf16[16,64,128]{2,1,0:T(8,128)(2,1)S(1)}, u32[]{:S(2)}, u32[]{:S(2)}) async-start(bf16[16,64,128]{2,1,0:T(8,128)(2,1)} %bitcast.13), calls=%async_computation.1 | async-start | bytes 524288 | tf_op jit(solution)/shard_map/all_to_all | solution.py:755
  142.6 7.7 %all-to-all-done.1.refs_0_ = bf16[16,64,128]{2,1,0:T(8,128)(2,1)S(1)} async-done(((bf16[16,64,128]{2,1,0:T(8,128)(2,1)}), bf16[16,64,128]{2,1,0:T(8,128)(2,1)S(1)}, u32[]{:S(2)}, u32[]{:S(2)}) %all-to-all-start.1) | async-done | bytes 262176 | tf_op jit(solution)/shard_map/all_to_all | solution.py:755
  153.6 2.4 collective-permute-start.23
  156.0 18.0 %shard_map.237 = (f32[2048,128]{1,0:T(8,128)}, bf16[2048,128]{1,0:T(8,128)(2,1)}, bf16[16,64,128]{2,1,0:T(8,128)(2,1)}, f32[8,128]{1,0:T(8,128)}) custom-call(s32[5]{0:T(128)} %stack.35.coords, s32[16]{0:T(128)} %convert_reduce_fusion.cuts, f32[8,256]{1,0:T(8,128)} %pad.18.hvec, bf16[16,64,128]{2,1,0:T(8,128)(2,1)} %copy-done.24, ...), custom_call_target="tpu_custom_call" | custom-call | flops 46000001024 | bytes 1048576 | tf_op jit(solution)/shard_map/pallas_call | solution.py:83
  175.0 3.6 %collective-permute-done.23 = bf16[288,1024]{1,0:T(8,128)(2,1)} collective-permute-done((bf16[288,1024]{1,0:T(8,128)(2,1)}, bf16[288,1024]{1,0:T(8,128)(2,1)}, u32[]{:S(2)}, u32[]{:S(2)}) %collective-permute-start.23) | collective-permute-done | bytes 589856 | tf_op jit(solution)/shard_map/ppermute | solution.py:49
  190.5 2.6 %shard_map.238 = (bf16[4,128,1024]{2,1,0:T(8,128)(2,1)}, f32[8,1024]{1,0:T(8,128)S(1)}, bf16[512,512]{1,0:T(8,128)(2,1)S(1)}, bf16[256,512]{1,0:T(8,128)(2,1)S(1)}) custom-call(s32[5]{0:T(128)S(1)} %copy-done, bf16[768,128]{1,0:T(8,128)(2,1)S(1)} %pad_maximum_fusion.10.refs_0_, bf16[768,128]{1,0:T(8,128)(2,1)S(1)} %collective-permute-done.25.refs_1_, ...), custom_call_target="tpu_custom_call" | custom-call | flops 4600000000 | bytes 1048576 | tf_op jit(solution)/shard_map/pallas_call | solution.py:83
  194.6 3.5 %all-to-all-start.2 = ((bf16[4,128,1024]{2,1,0:T(8,128)(2,1)}), bf16[4,128,1024]{2,1,0:T(8,128)(2,1)S(1)}, u32[]{:S(2)}, u32[]{:S(2)}) async-start(bf16[4,128,1024]{2,1,0:T(8,128)(2,1)} %get-tuple-element.184), calls=%async_computation.2 | async-start | bytes 2097152 | tf_op jit(solution)/shard_map/all_to_all | solution.py:832
  198.1 4.1 %shard_map.239 = (bf16[4,32,3072]{2,1,0:T(8,128)(2,1)}, bf16[4,32,3072]{2,1,0:T(8,128)(2,1)}) custom-call(s32[5]{0:T(128)} %stack.35.coords, bf16[512,512]{1,0:T(8,128)(2,1)} %copy-done.7, bf16[256,512]{1,0:T(8,128)(2,1)} %copy-done.8, bf16[512,1024]{1,0:T(8,128)(2,1)} %get-tuple-element.182.refs_4_.rows_all), custom_call_target="tpu_custom_call" | custom-call | flops 4600000000 | bytes 1048576 | tf_op jit(solution)/shard_map/pallas_call | solution.py:83
  208.5 2.1 fusion.29
  214.7 6.4 %all-to-all-done.2.refs_0_ = bf16[4,128,1024]{2,1,0:T(8,128)(2,1)S(1)} async-done(((bf16[4,128,1024]{2,1,0:T(8,128)(2,1)}), bf16[4,128,1024]{2,1,0:T(8,128)(2,1)S(1)}, u32[]{:S(2)}, u32[]{:S(2)}) %all-to-all-start.2) | async-done | bytes 1048608 | tf_op jit(solution)/shard_map/all_to_all | solution.py:832
  222.9 3.8 %collective-permute-start.39 = (bf16[40,1024]{1,0:T(8,128)(2,1)S(1)}, bf16[40,1024]{1,0:T(8,128)(2,1)S(1)}, u32[]{:S(2)}, u32[]{:S(2)}) collective-permute-start(bf16[40,1024]{1,0:T(8,128)(2,1)S(1)} %get-tuple-element.281), channel_id=1, source_target_pairs={{0,6},{2,4},{4,2},{6,0},{1,7},{3,5},{5,3},{7,1},{8,14},{10,12},{12... | collective-permute-start | bytes 245768 | tf_op jit(solution)/shard_map/ppermute | solution.py:49
  229.3 3.1 %collective-permute-done.38 = bf16[40,1024]{1,0:T(8,128)(2,1)S(1)} collective-permute-done((bf16[40,1024]{1,0:T(8,128)(2,1)S(1)}, bf16[40,1024]{1,0:T(8,128)(2,1)S(1)}, u32[]{:S(2)}, u32[]{:S(2)}) %collective-permute-start.38) | collective-permute-done | bytes 81952 | tf_op jit(solution)/shard_map/ppermute | solution.py:49
  (263 shorter events, 72.8 us)
Async XLA Ops:
  7.2 103.7 %all-gather.2.cloned.1.call-start = ((), (), s32[]{:S(2)}) async-start(), calls=%async_computation.4 | async-start | bytes 4866048 | tf_op jit(solution)/shard_map/all_gather | solution.py:660
  9.6 18.4 %collective-permute-start = (bf16[160,1024]{1,0:T(8,128)(2,1)}, bf16[160,1024]{1,0:T(8,128)(2,1)S(1)}, u32[]{:S(2)}, u32[]{:S(2)}) collective-permute-start(bf16[160,1024]{1,0:T(8,128)(2,1)} %get-tuple-element.111.refs_0_), channel_id=1, source_target_pairs={{0,2},{2,0},{4,6},{6,4},{1,3},{3,1},{5,7},{7,5},{8,10},{10,8},{12,... | collective-permute-start | bytes 983048 | tf_op jit(solution)/shard_map/ppermute | solution.py:49
  12.6 24.5 %collective-permute-start.1 = (bf16[160,1024]{1,0:T(8,128)(2,1)}, bf16[160,1024]{1,0:T(8,128)(2,1)S(1)}, u32[]{:S(2)}, u32[]{:S(2)}) collective-permute-start(bf16[160,1024]{1,0:T(8,128)(2,1)} %get-tuple-element.111.refs_0_), channel_id=1, source_target_pairs={{0,4},{2,6},{4,0},{6,2},{1,5},{3,7},{5,1},{7,3},{8,12},{10,14},{12... | collective-permute-start | bytes 983048 | tf_op jit(solution)/shard_map/ppermute | solution.py:49
  15.2 11.2 %collective-permute-start.3 = (bf16[32,3072]{1,0:T(8,128)(2,1)}, bf16[32,3072]{1,0:T(8,128)(2,1)S(1)}, u32[]{:S(2)}, u32[]{:S(2)}) collective-permute-start(bf16[32,3072]{1,0:T(8,128)(2,1)} %get-tuple-element.115.refs_4_), channel_id=1, source_target_pairs={{0,1},{1,0},{16,17},{17,16},{2,3},{3,2},{18,19},{19,18},{4,5},{5,4... | collective-permute-start | bytes 589832 | tf_op jit(solution)/shard_map/ppermute | solution.py:49
  16.7 9.7 %collective-permute-start.4 = (bf16[32,3072]{1,0:T(8,128)(2,1)}, bf16[32,3072]{1,0:T(8,128)(2,1)S(1)}, u32[]{:S(2)}, u32[]{:S(2)}) collective-permute-start(bf16[32,3072]{1,0:T(8,128)(2,1)} %get-tuple-element.115.refs_4_), channel_id=1, source_target_pairs={{0,16},{1,17},{16,0},{17,1},{2,18},{3,19},{18,2},{19,3},{4,20},{5,... | collective-permute-start | bytes 589832 | tf_op jit(solution)/shard_map/ppermute | solution.py:49
  18.2 8.7 %collective-permute-start.5 = (bf16[32,3072]{1,0:T(8,128)(2,1)}, bf16[32,3072]{1,0:T(8,128)(2,1)S(1)}, u32[]{:S(2)}, u32[]{:S(2)}) collective-permute-start(bf16[32,3072]{1,0:T(8,128)(2,1)} %get-tuple-element.115.refs_4_), channel_id=1, source_target_pairs={{0,17},{1,16},{16,1},{17,0},{2,19},{3,18},{18,3},{19,2},{4,21},{5,... | collective-permute-start | bytes 589832 | tf_op jit(solution)/shard_map/ppermute | solution.py:49
  26.4 10.7 %collective-permute-start.2 = (bf16[160,1024]{1,0:T(8,128)(2,1)}, bf16[160,1024]{1,0:T(8,128)(2,1)S(1)}, u32[]{:S(2)}, u32[]{:S(2)}) collective-permute-start(bf16[160,1024]{1,0:T(8,128)(2,1)} %get-tuple-element.111.refs_0_), channel_id=1, source_target_pairs={{0,6},{2,4},{4,2},{6,0},{1,7},{3,5},{5,3},{7,1},{8,14},{10,12},{12... | collective-permute-start | bytes 983048 | tf_op jit(solution)/shard_map/ppermute | solution.py:49
  27.9 10.6 %collective-permute-start.6 = (bf16[128,3072]{1,0:T(8,128)(2,1)S(1)}, bf16[128,3072]{1,0:T(8,128)(2,1)S(1)}, u32[]{:S(2)}, u32[]{:S(2)}) collective-permute-start(bf16[128,3072]{1,0:T(8,128)(2,1)S(1)} %pad_maximum_fusion.7), channel_id=1, source_target_pairs={{0,8},{8,0},{1,9},{9,1},{2,10},{10,2},{3,11},{11,3},{4,12},{12,4},... | collective-permute-start | bytes 2359304 | tf_op jit(solution)/shard_map/ppermute | solution.py:49
  53.9 30.5 %collective-permute-start.10 = (bf16[256,1024]{1,0:T(8,128)(2,1)S(1)}, bf16[256,1024]{1,0:T(8,128)(2,1)S(1)}, u32[]{:S(2)}, u32[]{:S(2)}) collective-permute-start(bf16[256,1024]{1,0:T(8,128)(2,1)S(1)} %copy-done.22), channel_id=1, source_target_pairs={{0,1},{1,0},{16,17},{17,16},{2,3},{3,2},{18,19},{19,18},{4,5},{5,4... | collective-permute-start | bytes 1572872 | tf_op jit(solution)/shard_map/ppermute | solution.py:49
  55.3 29.1 %collective-permute-start.11 = (bf16[256,1024]{1,0:T(8,128)(2,1)S(1)}, bf16[256,1024]{1,0:T(8,128)(2,1)S(1)}, u32[]{:S(2)}, u32[]{:S(2)}) collective-permute-start(bf16[256,1024]{1,0:T(8,128)(2,1)S(1)} %copy-done.22), channel_id=1, source_target_pairs={{0,16},{1,17},{16,0},{17,1},{2,18},{3,19},{18,2},{19,3},{4,20},{5,... | collective-permute-start | bytes 1572872 | tf_op jit(solution)/shard_map/ppermute | solution.py:49
  56.8 27.6 %collective-permute-start.12 = (bf16[256,1024]{1,0:T(8,128)(2,1)S(1)}, bf16[256,1024]{1,0:T(8,128)(2,1)S(1)}, u32[]{:S(2)}, u32[]{:S(2)}) collective-permute-start(bf16[256,1024]{1,0:T(8,128)(2,1)S(1)} %copy-done.22), channel_id=1, source_target_pairs={{0,17},{1,16},{16,1},{17,0},{2,19},{3,18},{18,3},{19,2},{4,21},{5,... | collective-permute-start | bytes 1572872 | tf_op jit(solution)/shard_map/ppermute | solution.py:49
  71.3 26.5 %all-to-all-start = ((bf16[16,64,128]{2,1,0:T(8,128)(2,1)}), bf16[16,64,128]{2,1,0:T(8,128)(2,1)S(1)}, u32[]{:S(2)}, u32[]{:S(2)}) async-start(bf16[16,64,128]{2,1,0:T(8,128)(2,1)} %get-tuple-element.124), calls=%async_computation | async-start | bytes 524288 | tf_op jit(solution)/shard_map/all_to_all | solution.py:710
  106.2 10.3 %collective-permute-start.15 = (bf16[128,1024]{1,0:T(8,128)(2,1)}, bf16[128,1024]{1,0:T(8,128)(2,1)S(1)}, u32[]{:S(2)}, u32[]{:S(2)}) collective-permute-start(bf16[128,1024]{1,0:T(8,128)(2,1)} %get-tuple-element.131.refs_0_), channel_id=1, source_target_pairs={{0,1},{1,0},{16,17},{17,16},{2,3},{3,2},{18,19},{19,18},{4,5},{5,4... | collective-permute-start | bytes 786440 | tf_op jit(solution)/shard_map/ppermute | solution.py:49
  106.2 10.3 %collective-permute-start.16 = (bf16[128,1024]{1,0:T(8,128)(2,1)}, bf16[128,1024]{1,0:T(8,128)(2,1)S(1)}, u32[]{:S(2)}, u32[]{:S(2)}) collective-permute-start(bf16[128,1024]{1,0:T(8,128)(2,1)} %get-tuple-element.131.refs_0_), channel_id=1, source_target_pairs={{0,16},{1,17},{16,0},{17,1},{2,18},{3,19},{18,2},{19,3},{4,20},{5,... | collective-permute-start | bytes 786440 | tf_op jit(solution)/shard_map/ppermute | solution.py:49
  107.3 14.2 %collective-permute-start.19 = (bf16[128,1024]{1,0:T(8,128)(2,1)}, bf16[128,1024]{1,0:T(8,128)(2,1)S(1)}, u32[]{:S(2)}, u32[]{:S(2)}) collective-permute-start(bf16[128,1024]{1,0:T(8,128)(2,1)} %get-tuple-element.131.refs_0_), channel_id=1, source_target_pairs={{0,17},{1,16},{16,1},{17,0},{2,19},{3,18},{18,3},{19,2},{4,21},{5,... | collective-permute-start | bytes 786440 | tf_op jit(solution)/shard_map/ppermute | solution.py:49
  119.5 14.6 %collective-permute-start.17 = (bf16[128,1024]{1,0:T(8,128)(2,1)S(1)}, bf16[128,1024]{1,0:T(8,128)(2,1)S(1)}, u32[]{:S(2)}, u32[]{:S(2)}) collective-permute-start(bf16[128,1024]{1,0:T(8,128)(2,1)S(1)} %get-tuple-element.138), channel_id=1, source_target_pairs={{0,1},{1,0},{16,17},{17,16},{2,3},{3,2},{18,19},{19,18},{4,5},{5,4... | collective-permute-start | bytes 786440 | tf_op jit(solution)/shard_map/ppermute | solution.py:49
  120.7 13.4 %collective-permute-start.18 = (bf16[128,1024]{1,0:T(8,128)(2,1)S(1)}, bf16[128,1024]{1,0:T(8,128)(2,1)}, u32[]{:S(2)}, u32[]{:S(2)}) collective-permute-start(bf16[128,1024]{1,0:T(8,128)(2,1)S(1)} %get-tuple-element.139), channel_id=1, source_target_pairs={{0,16},{1,17},{16,0},{17,1},{2,18},{3,19},{18,2},{19,3},{4,20},{5,... | collective-permute-start | bytes 786440 | tf_op jit(solution)/shard_map/ppermute | solution.py:49
  124.0 10.1 %collective-permute-start.20 = (bf16[128,1024]{1,0:T(8,128)(2,1)S(1)}, bf16[128,1024]{1,0:T(8,128)(2,1)S(1)}, u32[]{:S(2)}, u32[]{:S(2)}) collective-permute-start(bf16[128,1024]{1,0:T(8,128)(2,1)S(1)} %get-tuple-element.144), channel_id=1, source_target_pairs={{0,17},{1,16},{16,1},{17,0},{2,19},{3,18},{18,3},{19,2},{4,21},{5,... | collective-permute-start | bytes 786440 | tf_op jit(solution)/shard_map/ppermute | solution.py:49
  137.3 13.0 %all-to-all-start.1 = ((bf16[16,64,128]{2,1,0:T(8,128)(2,1)}), bf16[16,64,128]{2,1,0:T(8,128)(2,1)S(1)}, u32[]{:S(2)}, u32[]{:S(2)}) async-start(bf16[16,64,128]{2,1,0:T(8,128)(2,1)} %bitcast.13), calls=%async_computation.1 | async-start | bytes 524288 | tf_op jit(solution)/shard_map/all_to_all | solution.py:755
  140.8 61.4 %reduce-scatter.2.cloned.1.call-start = ((), (), s32[]{:S(2)}) async-start(), calls=%async_computation.5 | async-start | bytes 4866048 | tf_op jit(solution)/shard_map/reduce_scatter | solution.py:765
  152.5 22.5 %collective-permute-start.21 = (bf16[288,1024]{1,0:T(8,128)(2,1)}, bf16[288,1024]{1,0:T(8,128)(2,1)S(1)}, u32[]{:S(2)}, u32[]{:S(2)}) collective-permute-start(bf16[288,1024]{1,0:T(8,128)(2,1)} %get-tuple-element.269), channel_id=1, source_target_pairs={{0,1},{1,0},{16,17},{17,16},{2,3},{3,2},{18,19},{19,18},{4,5},{5,4... | collective-permute-start | bytes 1769480 | tf_op jit(solution)/shard_map/ppermute | solution.py:49
  152.5 22.5 %collective-permute-start.22 = (bf16[288,1024]{1,0:T(8,128)(2,1)}, bf16[288,1024]{1,0:T(8,128)(2,1)S(1)}, u32[]{:S(2)}, u32[]{:S(2)}) collective-permute-start(bf16[288,1024]{1,0:T(8,128)(2,1)} %get-tuple-element.270), channel_id=1, source_target_pairs={{0,16},{1,17},{16,0},{17,1},{2,18},{3,19},{18,2},{19,3},{4,20},{5,... | collective-permute-start | bytes 1769480 | tf_op jit(solution)/shard_map/ppermute | solution.py:49
  153.6 25.0 %collective-permute-start.23 = (bf16[288,1024]{1,0:T(8,128)(2,1)}, bf16[288,1024]{1,0:T(8,128)(2,1)}, u32[]{:S(2)}, u32[]{:S(2)}) collective-permute-start(bf16[288,1024]{1,0:T(8,128)(2,1)} %get-tuple-element.268), channel_id=1, source_target_pairs={{0,17},{1,16},{16,1},{17,0},{2,19},{3,18},{18,3},{19,2},{4,21},{5,... | collective-permute-start | bytes 1769480 | tf_op jit(solution)/shard_map/ppermute | solution.py:49
  180.1 9.7 %collective-permute-start.25 = (bf16[768,128]{1,0:T(8,128)(2,1)S(1)}, bf16[768,128]{1,0:T(8,128)(2,1)S(1)}, u32[]{:S(2)}, u32[]{:S(2)}) collective-permute-start(bf16[768,128]{1,0:T(8,128)(2,1)S(1)} %pad_maximum_fusion.11), channel_id=1, source_target_pairs={{0,1},{1,0},{16,17},{17,16},{2,3},{3,2},{18,19},{19,18},{4,5},{5,4... | collective-permute-start | bytes 589832 | tf_op jit(solution)/shard_map/ppermute | solution.py:49
  180.4 9.4 %collective-permute-start.26 = (bf16[768,128]{1,0:T(8,128)(2,1)S(1)}, bf16[768,128]{1,0:T(8,128)(2,1)S(1)}, u32[]{:S(2)}, u32[]{:S(2)}) collective-permute-start(bf16[768,128]{1,0:T(8,128)(2,1)S(1)} %pad_maximum_fusion.12), channel_id=1, source_target_pairs={{0,16},{1,17},{16,0},{17,1},{2,18},{3,19},{18,2},{19,3},{4,20},{5,... | collective-permute-start | bytes 589832 | tf_op jit(solution)/shard_map/ppermute | solution.py:49
  181.7 8.4 %collective-permute-start.27 = (bf16[768,128]{1,0:T(8,128)(2,1)S(1)}, bf16[768,128]{1,0:T(8,128)(2,1)S(1)}, u32[]{:S(2)}, u32[]{:S(2)}) collective-permute-start(bf16[768,128]{1,0:T(8,128)(2,1)S(1)} %pad_maximum_fusion.13), channel_id=1, source_target_pairs={{0,17},{1,16},{16,1},{17,0},{2,19},{3,18},{18,3},{19,2},{4,21},{5,... | collective-permute-start | bytes 589832 | tf_op jit(solution)/shard_map/ppermute | solution.py:49
  194.6 26.5 %all-to-all-start.2 = ((bf16[4,128,1024]{2,1,0:T(8,128)(2,1)}), bf16[4,128,1024]{2,1,0:T(8,128)(2,1)S(1)}, u32[]{:S(2)}, u32[]{:S(2)}) async-start(bf16[4,128,1024]{2,1,0:T(8,128)(2,1)} %get-tuple-element.184), calls=%async_computation.2 | async-start | bytes 2097152 | tf_op jit(solution)/shard_map/all_to_all | solution.py:832
  202.3 8.5 %collective-permute-start.28 = (bf16[4,32,3072]{2,1,0:T(8,128)(2,1)}, bf16[4,32,3072]{2,1,0:T(8,128)(2,1)S(1)}, u32[]{:S(2)}, u32[]{:S(2)}) collective-permute-start(bf16[4,32,3072]{2,1,0:T(8,128)(2,1)} %get-tuple-element.192), channel_id=1, source_target_pairs={{0,8},{8,0},{1,9},{9,1},{2,10},{10,2},{3,11},{11,3},{4,12},{12,4},... | collective-permute-start | bytes 2359304 | tf_op jit(solution)/shard_map/ppermute | solution.py:49
  204.8 9.8 %collective-permute-start.36 = (bf16[4,32,1024]{2,1,0:T(8,128)(2,1)S(1)}, bf16[4,32,1024]{2,1,0:T(8,128)(2,1)S(1)}, u32[]{:S(2)}, u32[]{:S(2)}) collective-permute-start(bf16[4,32,1024]{2,1,0:T(8,128)(2,1)S(1)} %bitcast.98), channel_id=1, source_target_pairs={{0,8},{8,0},{1,9},{9,1},{2,10},{10,2},{3,11},{11,3},{4,12},{12,4},... | collective-permute-start | bytes 786440 | tf_op jit(solution)/shard_map/ppermute | solution.py:49
  211.0 10.1 %collective-permute-start.29 = (bf16[32,3072]{1,0:T(8,128)(2,1)S(1)}, bf16[32,3072]{1,0:T(8,128)(2,1)S(1)}, u32[]{:S(2)}, u32[]{:S(2)}) collective-permute-start(bf16[32,3072]{1,0:T(8,128)(2,1)S(1)} %get-tuple-element.238), channel_id=1, source_target_pairs={{0,1},{1,0},{16,17},{17,16},{2,3},{3,2},{18,19},{19,18},{4,5},{5,4... | collective-permute-start | bytes 589832 | tf_op jit(solution)/shard_map/ppermute | solution.py:49
  212.5 8.6 %collective-permute-start.30 = (bf16[32,3072]{1,0:T(8,128)(2,1)S(1)}, bf16[32,3072]{1,0:T(8,128)(2,1)S(1)}, u32[]{:S(2)}, u32[]{:S(2)}) collective-permute-start(bf16[32,3072]{1,0:T(8,128)(2,1)S(1)} %get-tuple-element.237), channel_id=1, source_target_pairs={{0,16},{1,17},{16,0},{17,1},{2,18},{3,19},{18,2},{19,3},{4,20},{5,... | collective-permute-start | bytes 589832 | tf_op jit(solution)/shard_map/ppermute | solution.py:49
  213.2 9.6 %collective-permute-start.31 = (bf16[32,3072]{1,0:T(8,128)(2,1)S(1)}, bf16[32,3072]{1,0:T(8,128)(2,1)S(1)}, u32[]{:S(2)}, u32[]{:S(2)}) collective-permute-start(bf16[32,3072]{1,0:T(8,128)(2,1)S(1)} %get-tuple-element.236), channel_id=1, source_target_pairs={{0,17},{1,16},{16,1},{17,0},{2,19},{3,18},{18,3},{19,2},{4,21},{5,... | collective-permute-start | bytes 589832 | tf_op jit(solution)/shard_map/ppermute | solution.py:49
  (55 other events, 256.3 us)
Sparse Core Ops, SparseCore 0:
  37.2 59.2 all-gather.1
  150.4 48.4 reduce-scatter.1
